TPU v7x, 128 devices: a whole 4x4x4 slice. The times are simulated.
128 devices in a mesh: seq: 16 (over y, z), head: 8 (over x, core).
Axes of the slice: x: 4, y: 4, z: 4, core: 2. Of those that a mesh axis runs over, the one named last changes fastest.
Arguments:
- queries: bfloat16 [16384, 8192], P('seq', 'head'), may hold values from -6 to 6
- keys: bfloat16 [16384, 8192], P('seq', 'head'), may hold values from -6 to 6
- values: bfloat16 [16384, 8192], P('seq', 'head'), may hold values from -6 to 6
- out_grad: bfloat16 [16384, 8192], P('seq', 'head'), may hold values from -6 to 6
- level_table: float32 [5, 256], replicated, may hold values from 0.05 to 0.5
- table_index: int32 [16384], P('seq'), may hold values from 0 to 255
- reach: int32 [16], P('seq'), may hold values from 1 to 4, as said below
Outputs:
- query_grad: bfloat16 [16384, 8192], P('seq', 'head')
- key_grad: bfloat16 [16384, 8192], P('seq', 'head')
- value_grad: bfloat16 [16384, 8192], P('seq', 'head')
- table_grad: float32 [5, 256], replicated
Inputs may be any that keep to these rules, and one draw needn't show every extreme that they name: Some group has reach 4 and some has reach 1.
All inputs are finite; a program needn't handle non-finite values.
Results may differ from a plain program's by a relative error of at most 0.0056.
Values sent between devices are 32-bit elements; how exact they have to be, the bound alone decides.
No kernel may reach another device: no remote copies, remote signals or barrier semaphores. Data moves between devices by JAX's collectives and lax.ppermute only.
A program may use at most 128 MiB of HBM per device.

v0:
```python
import jax
import jax.numpy as jnp
from jax import lax
from jax.sharding import PartitionSpec as P

DH = 128


precise = lax.Precision.HIGHEST


def from_partner(x, axis, apart):
    return lax.ppermute(x, axis, [(i, i ^ 1 << apart) for i in range(lax.axis_size(axis))])


def local(queries, keys, values, out_grad, level_table, table_index, reach):
    length = queries.shape[0]
    head_count = queries.shape[1] // DH
    levels = level_table.shape[0] - 1
    scale = 1.0 / DH
    group = lax.axis_index("seq")
    span = lax.axis_size("seq")
    level_ids = jnp.arange(1, levels + 1, dtype=jnp.int32)
    active = (level_ids <= reach[0]).astype(jnp.float32)
    picker = (
        table_index[:, None] == jnp.arange(level_table.shape[1], dtype=jnp.int32)[None, :]
    ).astype(jnp.float32)
    weights = jnp.dot(picker, level_table.T, precision=precise)
    near_weight = weights[:, 0]
    far_weight = weights[:, 1:] * active[None, :]
    query_heads = queries.reshape(length, head_count, DH)
    key_heads = keys.reshape(length, head_count, DH)
    value_heads = values.reshape(length, head_count, DH)
    grad_heads = out_grad.reshape(length, head_count, DH)
    own_state = jnp.einsum(
        "thd,the->hde", key_heads, value_heads, preferred_element_type=jnp.float32
    )
    weighted = (query_heads[:, None, :, :] * far_weight[:, :, None, None]).astype(jnp.bfloat16)
    grad_part = jnp.einsum(
        "tlhd,the->lhde", weighted, grad_heads, preferred_element_type=jnp.float32
    )
    running = own_state
    pending = grad_part
    grad_total = jnp.zeros_like(own_state)
    far_list = []
    for bit_index in range(levels):
        high_bit = jnp.bitwise_and(jnp.right_shift(group, bit_index), 1).astype(jnp.float32)
        partner = from_partner(running, "seq", bit_index)
        incoming = from_partner(pending[bit_index:], "seq", bit_index)
        far_list.append(partner * high_bit)
        running = running + partner
        grad_total = grad_total + incoming[0] * (1.0 - high_bit)
        pending = jnp.concatenate(
            [pending[: bit_index + 1], pending[bit_index + 1 :] + incoming[1:]], 0
        )
    far_states = jnp.stack(far_list, 0)
    state_bf = far_states.astype(jnp.bfloat16)
    reads = jnp.einsum("the,lhde->tlhd", grad_heads, state_bf, preferred_element_type=jnp.float32)
    far_query = scale * jnp.sum(reads * far_weight[:, :, None, None], axis=1)
    far_lambda = scale * jnp.sum(
        reads * query_heads[:, None, :, :].astype(jnp.float32), axis=(2, 3)
    )
    returned_bf = grad_total.astype(jnp.bfloat16)
    far_key = scale * jnp.einsum(
        "the,hde->thd", value_heads, returned_bf, preferred_element_type=jnp.float32
    )
    far_value = scale * jnp.einsum(
        "thd,hde->the", key_heads, returned_bf, preferred_element_type=jnp.float32
    )
    positions = jnp.arange(length, dtype=jnp.int32)
    causal = positions[:, None] >= positions[None, :]
    coef = jnp.where(causal, scale * near_weight[:, None], 0.0)
    contract_rows = (((0,), (0,)), ((), ()))
    contract_cols = (((1,), (1,)), ((), ()))

    def head_step(head_index, carry):
        grad_query, grad_key, grad_value, near_lambda = carry
        start = head_index * DH
        query_one = lax.dynamic_slice_in_dim(queries, start, DH, 1)
        key_one = lax.dynamic_slice_in_dim(keys, start, DH, 1)
        value_one = lax.dynamic_slice_in_dim(values, start, DH, 1)
        grad_one = lax.dynamic_slice_in_dim(out_grad, start, DH, 1)
        scores = lax.dot_general(
            query_one, key_one, contract_cols, preferred_element_type=jnp.float32
        )
        probs = (scores * coef).astype(jnp.bfloat16)
        value_near = lax.dot_general(
            probs, grad_one, contract_rows, preferred_element_type=jnp.float32
        )
        grad_probs = lax.dot_general(
            grad_one, value_one, contract_cols, preferred_element_type=jnp.float32
        )
        grad_scores = (grad_probs * coef).astype(jnp.bfloat16)
        query_near = jnp.dot(grad_scores, key_one, preferred_element_type=jnp.float32)
        key_near = lax.dot_general(
            grad_scores, query_one, contract_rows, preferred_element_type=jnp.float32
        )
        near_lambda = near_lambda + scale * jnp.sum(
            jnp.where(causal, scores * grad_probs, 0.0), axis=1
        )
        grad_query = lax.dynamic_update_slice_in_dim(
            grad_query, lax.dynamic_slice_in_dim(grad_query, start, DH, 1) + query_near, start, 1
        )
        grad_key = lax.dynamic_update_slice_in_dim(
            grad_key, lax.dynamic_slice_in_dim(grad_key, start, DH, 1) + key_near, start, 1
        )
        grad_value = lax.dynamic_update_slice_in_dim(
            grad_value, lax.dynamic_slice_in_dim(grad_value, start, DH, 1) + value_near, start, 1
        )
        return (grad_query, grad_key, grad_value, near_lambda)

    initial = (
        far_query.reshape(length, head_count * DH),
        far_key.reshape(length, head_count * DH),
        far_value.reshape(length, head_count * DH),
        jnp.zeros((length,), jnp.float32),
    )
    grad_query, grad_key, grad_value, near_lambda = lax.fori_loop(0, head_count, head_step, initial)
    lambda_grad = jnp.concatenate([near_lambda[:, None], far_lambda * active[None, :]], 1)
    partial_table = lax.dot_general(lambda_grad, picker, contract_rows, precision=precise)
    table_grad = lax.psum(partial_table, ("seq", "head")) / (length * span)
    return (
        grad_query.astype(jnp.bfloat16),
        grad_key.astype(jnp.bfloat16),
        grad_value.astype(jnp.bfloat16),
        table_grad,
    )


def solution(mesh):
    return jax.shard_map(
        local,
        mesh=mesh,
        in_specs=(
            P("seq", "head"),
            P("seq", "head"),
            P("seq", "head"),
            P("seq", "head"),
            P(),
            P("seq"),
            P("seq"),
        ),
        out_specs=(P("seq", "head"), P("seq", "head"), P("seq", "head"), P()),
        check_vma=False,
    )
```

profile of v0, /device:TPU:0, one launch (start us, length us, event | category | flops | bytes accessed | tf_op | source)
XLA Modules:
  0.0 349.6 jit_solution(16067648765155826152)
XLA Ops:
  1.5 3.5 %copy.56 = bf16[128,8,8,128]{3,2,1,0:T(8,128)(2,1)} copy(bf16[128,8,8,128]{3,1,2,0:T(8,128)(2,1)} %bitcast.68) | data formatting | bytes 4194304
  5.0 3.0 copy.51
  8.8 6.7 %fusion.56 = f32[4,8,128,128]{3,2,0,1:T(8,128)} fusion(bf16[1024,8,128,1]{2,1,0,3:T(8,128)(2,1)} %bitcast.71, f32[1024,8,128]{0,2,1:T(8,128)} %bitcast.69, f32[1024,4]{0,1:T(4,128)S(1)} %slice_multiply_fusion.3), kind=kOutput, calls=%fused_computation.59 | convolution fusion | flops 1082130432 | bytes 8404992 | tf_op jit(solution)/shard_map/tlhd,the->lhde/dot_general | solution.py:39
  15.4 2.0 collective-permute-start.4
  18.7 55.9 %collective-permute-done = f32[8,128,128]{2,1,0:T(8,128)} collective-permute-done((f32[8,128,128]{2,1,0:T(8,128)S(1)}, f32[8,128,128]{2,1,0:T(8,128)}, u32[]{:S(2)}, u32[]{:S(2)}) %collective-permute-start) | collective-permute-done | bytes 524320 | tf_op jit(solution)/shard_map/ppermute | solution.py:13
  75.8 3.8 %collective-permute-start.1 = (f32[8,128,128]{2,1,0:T(8,128)S(1)}, f32[8,128,128]{2,1,0:T(8,128)}, u32[]{:S(2)}, u32[]{:S(2)}) collective-permute-start(f32[8,128,128]{2,1,0:T(8,128)S(1)} %get-tuple-element.288), channel_id=1, source_target_pairs={{0,16},{8,24},{16,0},{24,8},{32,48},{40,56},{48,32},{56,40},{64,80... | collective-permute-start | bytes 1572872 | tf_op jit(solution)/shard_map/ppermute | solution.py:13
  79.6 3.2 slice_add_fusion
  82.8 9.7 %collective-permute-done.1 = f32[8,128,128]{2,1,0:T(8,128)} collective-permute-done((f32[8,128,128]{2,1,0:T(8,128)S(1)}, f32[8,128,128]{2,1,0:T(8,128)}, u32[]{:S(2)}, u32[]{:S(2)}) %collective-permute-start.1) | collective-permute-done | bytes 524320 | tf_op jit(solution)/shard_map/ppermute | solution.py:13
  92.5 1.9 fusion.69
  96.0 8.8 %collective-permute-done.2 = f32[8,128,128]{2,1,0:T(8,128)S(1)} collective-permute-done((f32[8,128,128]{2,1,0:T(8,128)S(1)}, f32[8,128,128]{2,1,0:T(8,128)S(1)}, u32[]{:S(2)}, u32[]{:S(2)}) %collective-permute-start.2) | collective-permute-done | bytes 524320 | tf_op jit(solution)/shard_map/ppermute | solution.py:13
  104.8 4.5 %collective-permute-start.3 = (f32[8,128,128]{2,1,0:T(8,128)S(1)}, f32[8,128,128]{2,1,0:T(8,128)S(1)}, u32[]{:S(2)}, u32[]{:S(2)}) collective-permute-start(f32[8,128,128]{2,1,0:T(8,128)S(1)} %get-tuple-element.292), channel_id=1, source_target_pairs={{0,64},{8,72},{16,80},{24,88},{32,96},{40,104},{48,112},{56,120},{... | collective-permute-start | bytes 1572872 | tf_op jit(solution)/shard_map/ppermute | solution.py:13
  109.3 15.1 %collective-permute-done.5 = f32[3,8,128,128]{3,2,0,1:T(8,128)} collective-permute-done((f32[3,8,128,128]{3,2,0,1:T(8,128)}, f32[3,8,128,128]{3,2,0,1:T(8,128)}, u32[]{:S(2)}, u32[]{:S(2)}) %collective-permute-start.5) | collective-permute-done | bytes 1572896 | tf_op jit(solution)/shard_map/ppermute | solution.py:13
  127.8 6.2 %fusion.40 = (f32[1024,4]{0,1:T(4,128)S(1)}, f32[1024,8,128]{0,2,1:T(8,128)S(1)}) fusion(f32[1024,8,128]{0,2,1:T(8,128)S(1)} %bitcast.70, f32[1024,4]{0,1:T(4,128)S(1)} %slice_multiply_fusion.3, bf16[1024,8,128,1]{2,1,0,3:T(8,128)(2,1)} %bitcast.72, bf16[1,8,128,128]{3,2,1,0:T(8,128)(2,1)S(1)} %fusion.71, ...), kind=kOutput, calls=%fused_computation.39 | convolution fusion | flops 1091039232 | bytes 11567104 | tf_op jit(solution)/shard_map/the,lhde->tlhd/dot_general | solution.py:58
  134.0 15.5 %collective-permute-done.6 = f32[2,8,128,128]{3,2,0,1:T(8,128)S(1)} collective-permute-done((f32[2,8,128,128]{3,2,0,1:T(8,128)S(1)}, f32[2,8,128,128]{3,2,0,1:T(8,128)S(1)}, u32[]{:S(2)}, u32[]{:S(2)}) %collective-permute-start.6) | collective-permute-done | bytes 1048608 | tf_op jit(solution)/shard_map/ppermute | solution.py:13
  150.4 3.2 collective-permute-start.7
  153.6 2.8 broadcast_multiply_fusion
  156.4 5.4 %copy.43 = f32[1024,1024]{1,0:T(8,128)} copy(f32[1024,1024]{0,1:T(8,128)} %bitcast.67) | data formatting | bytes 8388608
  165.0 4.3 %convolution_multiply_fusion = f32[8,128,1024]{2,1,0:T(8,128)} fusion(bf16[1,8,128,128]{3,2,0,1:T(8,128)(2,1)S(1)} %fusion.64, bf16[1024,1024]{1,0:T(8,128)(2,1)} %param.10), kind=kOutput, calls=%fused_computation.44 | convolution fusion | flops 269484032 | bytes 6553600 | tf_op jit(solution)/shard_map/thd,hde->the/dot_general | solution.py:67
  169.3 2.6 convolution_multiply_fusion.1
  172.0 5.4 %copy.45 = f32[1024,1024]{1,0:T(8,128)} copy(f32[1024,1024]{0,1:T(8,128)} %bitcast.66) | data formatting | bytes 8388608
  177.4 5.4 %copy.44 = f32[1024,1024]{1,0:T(8,128)} copy(f32[1024,1024]{0,1:T(8,128)} %bitcast.65) | data formatting | bytes 8388608
  182.7 91.8 %while.20 = (s32[]{:T(128)}, f32[1024,1024]{1,0:T(8,128)}, f32[1024,1024]{1,0:T(8,128)}, f32[1024,1024]{1,0:T(8,128)}, f32[1024]{0:T(1024)S(1)}, /*index=5*/bf16...) while((s32[]{:T(128)}, f32[1024,1024]{1,0:T(8,128)}, ...), condition=%wide.region_3.4_spmd.clone, body=%wide.region_1.3_spmd.clone.sunk | while | flops 1359349760 | bytes 30180548 | solution.py:118
  182.7 1.7 fusion.104
  184.5 2.6 fusion.106
  187.1 2.8 fusion.105
  189.9 1.7 fusion.107
  191.6 2.7 fusion.108
  194.3 1.7 fusion.104
  196.0 2.6 fusion.106
  198.6 2.7 fusion.105
  201.4 1.7 fusion.107
  203.0 2.7 fusion.108
  205.7 1.7 fusion.104
  207.5 2.6 fusion.106
  210.1 2.7 fusion.105
  212.8 1.7 fusion.107
  214.5 2.7 fusion.108
  217.2 1.7 fusion.104
  218.9 2.6 fusion.106
  221.6 2.7 fusion.105
  224.3 1.7 fusion.107
  225.9 2.7 fusion.108
  228.7 1.7 fusion.104
  230.4 2.6 fusion.106
  233.0 2.7 fusion.105
  235.7 1.7 fusion.107
  237.4 2.7 fusion.108
  240.1 1.7 fusion.104
  241.9 2.6 fusion.106
  244.5 2.7 fusion.105
  247.2 1.7 fusion.107
  248.9 2.7 fusion.108
  251.6 1.7 fusion.104
  253.3 2.6 fusion.106
  256.0 2.7 fusion.105
  258.7 1.7 fusion.107
  260.4 2.7 fusion.108
  263.1 1.7 fusion.104
  264.8 2.6 fusion.106
  267.4 2.7 fusion.105
  270.1 1.7 fusion.107
  271.8 2.7 fusion.108
  275.0 65.3 %psum.7 = f32[5,256]{1,0:T(8,128)S(1)} all-reduce(f32[5,256]{1,0:T(8,128)S(1)} %fusion.60), channel_id=1, replica_groups=mesh['seq'=16,'head'=8] {'seq','head'}, use_global_device_ids=true, to_apply=%region_5.6 | all-reduce | flops 1280 | bytes 10240 | tf_op jit(solution)/shard_map/psum | solution.py:121
  340.9 4.1 %convert_element_type.68 = bf16[1024,1024]{1,0:T(8,128)(2,1)} convert(f32[1024,1024]{1,0:T(8,128)} %get-tuple-element.191) | non-fusion elementwise | flops 1048576 | bytes 6291456 | tf_op jit(solution)/shard_map/convert_element_type | solution.py:123
  (55 shorter events, 18.0 us)
Async XLA Ops:
  0.6 7.4 %copy-start = (f32[5,256]{1,0:T(8,128)S(1)}, f32[5,256]{1,0:T(8,128)}, u32[]{:S(2)}) copy-start(f32[5,256]{1,0:T(8,128)} %param.13) | copy-start | bytes 15364
  0.6 4.4 %copy-start.4 = (bf16[1024,1024]{1,0:T(8,128)(2,1)S(1)}, bf16[1024,1024]{1,0:T(8,128)(2,1)}, u32[]{:S(2)}) copy-start(bf16[1024,1024]{1,0:T(8,128)(2,1)} %param.9) | copy-start | bytes 6291460
  1.5 6.6 %copy-start.10 = (s32[1024]{0:T(1024)S(1)}, s32[1024]{0:T(1024)}, u32[]{:S(2)}) copy-start(s32[1024]{0:T(1024)} %param.14) | copy-start | bytes 12292
  8.7 8.7 %copy-start.5 = (bf16[1024,1024]{1,0:T(8,128)(2,1)S(1)}, bf16[1024,1024]{1,0:T(8,128)(2,1)}, u32[]{:S(2)}) copy-start(bf16[1024,1024]{1,0:T(8,128)(2,1)} %param.11) | copy-start | bytes 6291460
  8.7 8.7 %copy-start.7 = (bf16[1024,1024]{1,0:T(8,128)(2,1)S(1)}, bf16[1024,1024]{1,0:T(8,128)(2,1)}, u32[]{:S(2)}) copy-start(bf16[1024,1024]{1,0:T(8,128)(2,1)} %param.10) | copy-start | bytes 6291460
  15.4 64.1 %collective-permute-start.4 = (f32[4,8,128,128]{3,2,0,1:T(8,128)}, f32[4,8,128,128]{3,2,0,1:T(8,128)}, u32[]{:S(2)}, u32[]{:S(2)}) collective-permute-start(f32[4,8,128,128]{3,2,0,1:T(8,128)} %fusion.56), channel_id=1, source_target_pairs={{0,8},{8,0},{16,24},{24,16},{32,40},{40,32},{48,56},{56,48},{64,72... | collective-permute-start | bytes 6291464 | tf_op jit(solution)/shard_map/ppermute | solution.py:13
  18.6 56.0 %collective-permute-start = (f32[8,128,128]{2,1,0:T(8,128)S(1)}, f32[8,128,128]{2,1,0:T(8,128)}, u32[]{:S(2)}, u32[]{:S(2)}) collective-permute-start(f32[8,128,128]{2,1,0:T(8,128)S(1)} %fusion.45), channel_id=1, source_target_pairs={{0,8},{8,0},{16,24},{24,16},{32,40},{40,32},{48,56},{56,48},{64,72... | collective-permute-start | bytes 1572872 | tf_op jit(solution)/shard_map/ppermute | solution.py:13
  75.8 16.7 %collective-permute-start.1 = (f32[8,128,128]{2,1,0:T(8,128)S(1)}, f32[8,128,128]{2,1,0:T(8,128)}, u32[]{:S(2)}, u32[]{:S(2)}) collective-permute-start(f32[8,128,128]{2,1,0:T(8,128)S(1)} %get-tuple-element.288), channel_id=1, source_target_pairs={{0,16},{8,24},{16,0},{24,8},{32,48},{40,56},{48,32},{56,40},{64,80... | collective-permute-start | bytes 1572872 | tf_op jit(solution)/shard_map/ppermute | solution.py:13
  82.8 41.6 %collective-permute-start.5 = (f32[3,8,128,128]{3,2,0,1:T(8,128)}, f32[3,8,128,128]{3,2,0,1:T(8,128)}, u32[]{:S(2)}, u32[]{:S(2)}) collective-permute-start(f32[3,8,128,128]{3,2,0,1:T(8,128)} %slice_add_fusion), channel_id=1, source_target_pairs={{0,16},{8,24},{16,0},{24,8},{32,48},{40,56},{48,32},{56,40},{64,80... | collective-permute-start | bytes 4718600 | tf_op jit(solution)/shard_map/ppermute | solution.py:13
  94.4 10.4 %collective-permute-start.2 = (f32[8,128,128]{2,1,0:T(8,128)S(1)}, f32[8,128,128]{2,1,0:T(8,128)S(1)}, u32[]{:S(2)}, u32[]{:S(2)}) collective-permute-start(f32[8,128,128]{2,1,0:T(8,128)S(1)} %get-tuple-element.290), channel_id=1, source_target_pairs={{0,32},{8,40},{16,48},{24,56},{32,0},{40,8},{48,16},{56,24},{64,96... | collective-permute-start | bytes 1572872 | tf_op jit(solution)/shard_map/ppermute | solution.py:13
  95.9 31.8 %copy-start.8 = (f32[1024,1024]{0,1:T(8,128)S(1)}, f32[1024,1024]{0,1:T(8,128)}, u32[]{:S(2)}) copy-start(f32[1024,1024]{0,1:T(8,128)} %copy.51) | copy-start | bytes 12582916
  96.0 31.9 %copy-start.9 = (bf16[1,8,128,128]{3,2,1,0:T(8,128)(2,1)S(1)}, bf16[1,8,128,128]{3,2,1,0:T(8,128)(2,1)}, u32[]{:S(2)}) copy-start(bf16[1,8,128,128]{3,2,1,0:T(8,128)(2,1)} %get-tuple-element.289) | copy-start | bytes 786436
  104.8 22.9 %collective-permute-start.3 = (f32[8,128,128]{2,1,0:T(8,128)S(1)}, f32[8,128,128]{2,1,0:T(8,128)S(1)}, u32[]{:S(2)}, u32[]{:S(2)}) collective-permute-start(f32[8,128,128]{2,1,0:T(8,128)S(1)} %get-tuple-element.292), channel_id=1, source_target_pairs={{0,64},{8,72},{16,80},{24,88},{32,96},{40,104},{48,112},{56,120},{... | collective-permute-start | bytes 1572872 | tf_op jit(solution)/shard_map/ppermute | solution.py:13
  126.1 23.5 %collective-permute-start.6 = (f32[2,8,128,128]{3,2,0,1:T(8,128)S(1)}, f32[2,8,128,128]{3,2,0,1:T(8,128)S(1)}, u32[]{:S(2)}, u32[]{:S(2)}) collective-permute-start(f32[2,8,128,128]{3,2,0,1:T(8,128)S(1)} %slice_add_fusion.1), channel_id=1, source_target_pairs={{0,32},{8,40},{16,48},{24,56},{32,0},{40,8},{48,16},{56,24},{64,96... | collective-permute-start | bytes 3145736 | tf_op jit(solution)/shard_map/ppermute | solution.py:13
  150.4 13.0 %collective-permute-start.7 = (f32[1,8,128,128]{3,2,0,1:T(8,128)}, f32[1,8,128,128]{3,2,0,1:T(8,128)}, u32[]{:S(2)}, u32[]{:S(2)}) collective-permute-start(f32[1,8,128,128]{3,2,0,1:T(8,128)} %slice_add_fusion.2), channel_id=1, source_target_pairs={{0,64},{8,72},{16,80},{24,88},{32,96},{40,104},{48,112},{56,120},{... | collective-permute-start | bytes 1572872 | tf_op jit(solution)/shard_map/ppermute | solution.py:13
  161.9 7.5 %copy-start.6 = (bf16[1024,1024]{1,0:T(8,128)(2,1)S(1)}, bf16[1024,1024]{1,0:T(8,128)(2,1)}, u32[]{:S(2)}) copy-start(bf16[1024,1024]{1,0:T(8,128)(2,1)} %param.11) | copy-start | bytes 6291460
  340.3 4.7 %copy-start.3 = (f32[1024,1024]{1,0:T(8,128)S(1)}, f32[1024,1024]{1,0:T(8,128)}, u32[]{:S(2)}) copy-start(f32[1024,1024]{1,0:T(8,128)} %get-tuple-element.192) | copy-start | bytes 12582916
  345.0 2.9 copy-start.2
  345.0 4.6 %copy-start.1 = (f32[5,256]{1,0:T(8,128)S(1)}, f32[5,256]{1,0:T(8,128)}, u32[]{:S(2)}) copy-start(f32[5,256]{1,0:T(8,128)} %param.13) | copy-start | bytes 15364
where the time goes:
time: 352 us; the launch traced here: 350 us
  matrix products  114 us (32%)
  waiting for transfers between devices  107 us (30%)
  blocking collectives  65.3 us (19%)
  local copies, waits for them, and re-layouts  24 us (7%)
  other arithmetic  21.6 us (6%)
  starting transfers between devices  16.9 us (5%)
    ppermute x8, waiting for transfers between devices, from_partner(): lax.ppermute(x, axis, [(i, i ^ 1 << apart) for i in range(lax.axis_size(a...  107 us
    psum x1, blocking collectives, local(): table_grad = lax.psum(partial_table, ('seq', 'head')) / (length * span)  65.3 us
    dot_general x8, matrix products, head_step(): jnp.dot(grad_scores, key_one, preferred_element_type=jnp.float32)  21.7 us
    dot_general x8, matrix products, head_step(): lax.dot_general(probs, grad_one, contract_rows, preferred_element_type=jn...  21.6 us
    unnamed x26, local copies, waits for them, and re-layouts  21 us
    dot_general x8, matrix products, head_step(): lax.dot_general(grad_scores, query_one, contract_rows, preferred_element_...  21 us
    ppermute x8, starting transfers between devices, from_partner(): lax.ppermute(x, axis, [(i, i ^ 1 << apart) for i in range(lax.axis_size(a...  16.9 us
    dot_general x8, matrix products, head_step(): lax.dot_general(grad_one, value_one, contract_cols, preferred_element_typ...  13.9 us
  transfers between devices with their start and end apart: 8, of which 6 were waited for; matrix products, arithmetic and copies ran while one was open for 7% of the time, Pallas kernels for 0%

commit v1 on v0

v1 whole, which is shorter than its diff:
```python
import functools

import jax
import jax.numpy as jnp
from jax import lax
from jax.experimental import pallas as pl
from jax.experimental.pallas import tpu as pltpu
from jax.sharding import PartitionSpec as P

DH = 128
CHUNK = 256

precise = lax.Precision.HIGHEST
f32 = jnp.float32
bf16 = jnp.bfloat16


def mm(a, b, ca, cb):
    return lax.dot_general(a, b, (((ca,), (cb,)), ((), ())), preferred_element_type=f32)


def states_kernel(bits, q_ref, k_ref, v_ref, g_ref, w_ref, near_ref, far_ref):
    q = q_ref[...]
    g = g_ref[...].astype(f32)
    own = mm(k_ref[...], v_ref[...], 0, 0)
    w = w_ref[...]
    parts = [(g * w[:, l : l + 1]).astype(bf16) for l in range(1, 5)]
    grads = mm(q, jnp.concatenate(parts, 1), 0, 0)
    for l in range(4):
        x = jnp.where(bits[l] > 0, grads[:, l * DH : (l + 1) * DH], own)
        if l < 2:
            near_ref[l, 0] = x
        else:
            far_ref[0, l - 2, 0] = x


def group_kernel(q_ref, k_ref, v_ref, g_ref, w_ref, qn_ref, kn_ref, vn_ref, lam_ref):
    head = pl.program_id(0)
    scale = 1.0 / DH
    length = q_ref.shape[0]
    count = length // CHUNK
    rows = lax.broadcasted_iota(jnp.int32, (CHUNK, CHUNK), 0)
    cols = lax.broadcasted_iota(jnp.int32, (CHUNK, CHUNK), 1)
    causal = rows >= cols

    @pl.when(head == 0)
    def _():
        lam_ref[...] = jnp.zeros_like(lam_ref)

    state = jnp.zeros((DH, DH), f32)
    gps, scs, qss = [], [], []
    for i in range(count):
        at = pl.ds(i * CHUNK, CHUNK)
        q, k, v, g = q_ref[at, :], k_ref[at, :], v_ref[at, :], g_ref[at, :]
        w0 = w_ref[at, 0:1]
        qf = q.astype(f32)
        qs = (qf * w0).astype(bf16)
        gp = jnp.where(causal, mm(g, v, 1, 1), 0.0).astype(bf16)
        sc = jnp.where(causal, mm(qs, k, 1, 1), 0.0).astype(bf16)
        u = mm(gp, k, 1, 0)
        if i > 0:
            u = u + mm(g, state.astype(bf16), 1, 1)
        lam_ref[at, :] += qf * u
        qn_ref[at, :] = (scale * w0) * u
        if i < count - 1:
            state = state + mm(k, v, 0, 0)
        gps.append(gp)
        scs.append(sc)
        qss.append(qs)
    state = jnp.zeros((DH, DH), f32)
    for i in reversed(range(count)):
        at = pl.ds(i * CHUNK, CHUNK)
        k, v, g = k_ref[at, :], v_ref[at, :], g_ref[at, :]
        kn = mm(gps[i], qss[i], 0, 0)
        vn = mm(scs[i], g, 0, 0)
        if i < count - 1:
            sb = state.astype(bf16)
            kn = kn + mm(v, sb, 1, 1)
            vn = vn + mm(k, sb, 1, 0)
        kn_ref[at, :] = scale * kn
        vn_ref[at, :] = scale * vn
        if i > 0:
            state = state + mm(qss[i], g, 0, 0)


def reads_kernel(bits, q_ref, g_ref, w_ref, qn_ref, lam0_ref, y1_ref, y2_ref, y3_ref, out_ref, lam_ref, acc):
    head = pl.program_id(0)
    scale = 1.0 / DH

    @pl.when(head == 0)
    def _():
        acc[...] = jnp.zeros_like(acc)

    ys = [y1_ref[0], y2_ref[0], y3_ref[0, 0, 0], y3_ref[0, 1, 0]]
    states = [jnp.where(bits[l] > 0, ys[l], 0.0).astype(bf16) for l in range(4)]
    reads = mm(g_ref[...], jnp.concatenate(states, 0), 1, 1)
    q = q_ref[...].astype(f32)
    w = w_ref[...]
    total = None
    for l in range(4):
        read = reads[:, l * DH : (l + 1) * DH]
        acc[l] += q * read
        term = w[:, l + 1 : l + 2] * read
        total = term if total is None else total + term
    out_ref[...] = (qn_ref[...] + scale * total).astype(bf16)

    @pl.when(head == pl.num_programs(0) - 1)
    def _():
        lane = lax.broadcasted_iota(jnp.int32, (1, DH), 1)
        lam = jnp.where(lane == 0, jnp.sum(lam0_ref[...], 1, keepdims=True), 0.0)
        for l in range(4):
            here = (lane == l + 1) & (bits[4] > l)
            lam = jnp.where(here, jnp.sum(acc[l], 1, keepdims=True), lam)
        lam_ref[...] = scale * lam


def returns_kernel(bits, k_ref, v_ref, kn_ref, vn_ref, y1_ref, y2_ref, y3_ref, key_ref, value_ref):
    scale = 1.0 / DH
    ys = [y1_ref[0], y2_ref[0], y3_ref[0, 0, 0], y3_ref[0, 1, 0]]
    total = None
    for l in range(4):
        y = jnp.where(bits[l] > 0, 0.0, ys[l])
        total = y if total is None else total + y
    ret = total.astype(bf16)
    key_ref[...] = (kn_ref[...] + scale * mm(v_ref[...], ret, 1, 1)).astype(bf16)
    value_ref[...] = (vn_ref[...] + scale * mm(k_ref[...], ret, 1, 0)).astype(bf16)


def flip(x, axis, mask):
    return lax.ppermute(x, axis, [(i, i ^ mask) for i in range(lax.axis_size(axis))])


def local(queries, keys, values, out_grad, level_table, table_index, reach):
    length = queries.shape[0]
    heads = queries.shape[1] // DH
    span = lax.axis_size("seq")
    group = lax.axis_index("seq")
    bits = jnp.bitwise_and(jnp.right_shift(group, jnp.arange(4, dtype=jnp.int32)), 1)
    bits = jnp.concatenate([bits, reach.astype(jnp.int32)])
    picker = (
        table_index[:, None] == jnp.arange(level_table.shape[1], dtype=jnp.int32)[None, :]
    ).astype(f32)
    level_ids = jnp.arange(8, dtype=jnp.int32)
    table = jnp.pad(level_table, ((0, 3), (0, 0)))
    table = jnp.where((level_ids <= reach[0])[:, None], table, 0.0)
    weights = jnp.dot(picker, table.T, precision=precise)

    token_spec = pl.BlockSpec((length, DH), lambda h, *_: (0, h))
    fixed = lambda shape: pl.BlockSpec(shape, lambda h, *_: (0,) * len(shape))
    w_spec = fixed((length, 8))
    near_spec = pl.BlockSpec((2, 1, DH, DH), lambda h, *_: (0, h, 0, 0))
    state_spec = pl.BlockSpec((1, DH, DH), lambda h, *_: (h, 0, 0))
    far_spec = pl.BlockSpec((1, 2, 1, DH, DH), lambda h, *_: (h // 2, 0, h % 2, 0, 0))
    params = pltpu.CompilerParams(dimension_semantics=("arbitrary",), vmem_limit_bytes=40 * 2**20)

    near, far = pl.pallas_call(
        states_kernel,
        grid_spec=pltpu.PrefetchScalarGridSpec(
            num_scalar_prefetch=1,
            grid=(heads,),
            in_specs=[token_spec] * 4 + [w_spec],
            out_specs=[near_spec, far_spec],
        ),
        out_shape=[
            jax.ShapeDtypeStruct((2, heads, DH, DH), f32),
            jax.ShapeDtypeStruct((4, 2, heads // 4, DH, DH), f32),
        ],
        compiler_params=params,
        name="states",
    )(bits, queries, keys, values, out_grad, weights)

    rings = [[4 * y + z for z in range(4)] for y in range(span // 4)]
    got = lax.all_to_all(far, "seq", 0, 0, axis_index_groups=rings)
    pair2 = flip(near[1], "seq", 1)
    y1 = flip(near[0], "seq", 1)
    y2 = flip(near[1] + pair2, "seq", 3)
    rows = jnp.sum(got, axis=0)
    other = flip(rows, "seq", 4)
    y3s = other[0]
    y4s = flip(rows[1] + other[1], "seq", 12)
    back = jnp.stack([y3s, y4s], 0)
    y34 = lax.all_to_all(
        jnp.broadcast_to(back[None], (4,) + back.shape), "seq", 0, 0, axis_index_groups=rings
    )

    tokens_f32 = jax.ShapeDtypeStruct((length, heads * DH), f32)
    tokens_bf16 = jax.ShapeDtypeStruct((length, heads * DH), bf16)
    qn, kn, vn, lam0 = pl.pallas_call(
        group_kernel,
        grid=(heads,),
        in_specs=[token_spec] * 4 + [w_spec],
        out_specs=[token_spec] * 3 + [fixed((length, DH))],
        out_shape=[tokens_f32] * 3 + [jax.ShapeDtypeStruct((length, DH), f32)],
        compiler_params=params,
        cost_estimate=pl.CostEstimate(flops=4 * 10**9, bytes_accessed=20 * 2**20, transcendentals=0),
        name="group",
    )(queries, keys, values, out_grad, weights)

    query_grad, lam = pl.pallas_call(
        reads_kernel,
        grid_spec=pltpu.PrefetchScalarGridSpec(
            num_scalar_prefetch=1,
            grid=(heads,),
            in_specs=[token_spec] * 2
            + [w_spec, token_spec, fixed((length, DH)), state_spec, state_spec, far_spec],
            out_specs=[token_spec, fixed((length, DH))],
            scratch_shapes=[pltpu.VMEM((4, length, DH), f32)],
        ),
        out_shape=[tokens_bf16, jax.ShapeDtypeStruct((length, DH), f32)],
        compiler_params=params,
        cost_estimate=pl.CostEstimate(flops=2 * 10**9, bytes_accessed=10 * 2**20, transcendentals=0),
        name="reads",
    )(bits, queries, out_grad, weights, qn, lam0, y1, y2, y34)

    total = lax.dot_general(lam[:, :8], picker, (((0,), (0,)), ((), ())), precision=precise)
    for mask in (1, 2, 6):
        total = total + flip(total, "head", mask)
    for mask in (1, 3, 4, 12):
        total = total + flip(total, "seq", mask)
    table_grad = total[: level_table.shape[0]] / (length * span)

    key_grad, value_grad = pl.pallas_call(
        returns_kernel,
        grid_spec=pltpu.PrefetchScalarGridSpec(
            num_scalar_prefetch=1,
            grid=(heads,),
            in_specs=[token_spec] * 4 + [state_spec, state_spec, far_spec],
            out_specs=[token_spec] * 2,
        ),
        out_shape=[tokens_bf16] * 2,
        compiler_params=params,
        cost_estimate=pl.CostEstimate(flops=10**9, bytes_accessed=16 * 2**20, transcendentals=0),
        name="returns",
    )(bits, keys, values, kn, vn, y1, y2, y34)
    return query_grad, key_grad, value_grad, table_grad


def solution(mesh):
    return jax.shard_map(
        local,
        mesh=mesh,
        in_specs=(
            P("seq", "head"),
            P("seq", "head"),
            P("seq", "head"),
            P("seq", "head"),
            P(),
            P("seq"),
            P("seq"),
        ),
        out_specs=(P("seq", "head"), P("seq", "head"), P("seq", "head"), P()),
        check_vma=False,
    )
```

time: 352 us -> 144 us (0.41)
  matrix products: 114 us -> 2.04 us
  waiting for transfers between devices: 107 us -> 23.2 us
  Pallas kernels: 0 us -> 48.1 us
  blocking collectives: 65.3 us -> 20.3 us
  other arithmetic: 21.6 us -> 2.08 us
  starting transfers between devices: 16.9 us -> 20.7 us
    dot_general x47 -> x2, matrix products: 114 us -> 2.04 us  [the longest x1 1.34 us: local(): weights = jnp.dot(picker, table.T, precision=precise)]
    ppermute x8 -> x12, waiting for transfers between devices: 107 us -> 23.2 us  [flip(): lax.ppermute(x, axis, [(i, i ^ mask) for i in range(lax.axis_size(axis))])]
    psum x1 -> x0, blocking collectives: 65.3 us -> none  [local(): table_grad = lax.psum(partial_table, ('seq', 'head')) / (length * span)]
    pallas_call x0 -> x4, Pallas kernels: none -> 48.1 us  [the longest x1 17.4 us: local(): pl.pallas_call(group_kernel, grid=(heads,), in_specs=[token_spec] * 4 + [...]
    all_to_all x0 -> x1, blocking collectives: none -> 20.3 us  [local(): got = lax.all_to_all(far, 'seq', 0, 0, axis_index_groups=rings)]
    convert_element_type x4 -> x0, other arithmetic: 7.44 us -> none  [the longest x1 4.14 us: local(): grad_query.astype(jnp.bfloat16)]
    another operation x5 -> x1, other arithmetic: 4.73 us -> 0.02 us  [local(): back = jnp.stack([y3s, y4s], 0)]
    add x11 -> x7, other arithmetic: 5.8 us -> 1.28 us  [the longest x1 1.26 us: local(): y2 = flip(near[1] + pair2, 'seq', 3)]
  transfers between devices with their start and end apart: 8 -> 13, of which waited for: 6 -> 8; matrix products, arithmetic and copies ran while one was open for 7% -> 2% of each run, Pallas kernels for 0% -> 18%
where the time goes in v1:
time: 144 us; the launch traced here: 143 us
  Pallas kernels  48.1 us (33%)
  local copies, waits for them, and re-layouts  24.8 us (17%)
  waiting for transfers between devices  23.2 us (16%)
  starting transfers between devices  20.7 us (14%)
  blocking collectives  20.3 us (14%)
  other arithmetic  2.08 us (1%)
  matrix products  2.04 us (1%)
    ppermute x12, waiting for transfers between devices, flip(): lax.ppermute(x, axis, [(i, i ^ mask) for i in range(lax.axis_size(axis))])  23.2 us
    unnamed x46, local copies, waits for them, and re-layouts  22.7 us
    all_to_all x1, blocking collectives, local(): got = lax.all_to_all(far, 'seq', 0, 0, axis_index_groups=rings)  20.3 us
    pallas_call x1, Pallas kernels, local(): pl.pallas_call(group_kernel, grid=(heads,), in_specs=[token_spec] * 4 + [...  17.4 us
    ppermute x12, starting transfers between devices, flip(): lax.ppermute(x, axis, [(i, i ^ mask) for i in range(lax.axis_size(axis))])  17.1 us
    pallas_call x1, Pallas kernels, local(): pl.pallas_call(reads_kernel, grid_spec=pltpu.PrefetchScalarGridSpec(num_s...  11.6 us
    pallas_call x1, Pallas kernels, local(): pl.pallas_call(states_kernel, grid_spec=pltpu.PrefetchScalarGridSpec(num_...  10.6 us
    pallas_call x1, Pallas kernels, local(): pl.pallas_call(returns_kernel, grid_spec=pltpu.PrefetchScalarGridSpec(num...  8.58 us
  transfers between devices with their start and end apart: 13, of which 8 were waited for; matrix products, arithmetic and copies ran while one was open for 2% of the time, Pallas kernels for 18%

profile of v1, /device:TPU:0, one launch (start us, length us, event | category | flops | bytes accessed | tf_op | source)
XLA Modules:
  0.0 142.7 jit_solution(6475972694376027394)
XLA Ops:
  1.3 0.1 pad_add_fusion.bits
  1.4 1.3 fusion.1.w_ref
  2.7 0.0 copy-start
  2.7 1.6 %copy-done = bf16[1024,1024]{1,0:T(8,128)(2,1)S(1)} copy-done((bf16[1024,1024]{1,0:T(8,128)(2,1)S(1)}, bf16[1024,1024]{1,0:T(8,128)(2,1)}, u32[]{:S(2)}) %copy-start) | copy-done | bytes 2097176
  4.3 1.6 %copy-done.2 = bf16[1024,1024]{1,0:T(8,128)(2,1)S(1)} copy-done((bf16[1024,1024]{1,0:T(8,128)(2,1)S(1)}, bf16[1024,1024]{1,0:T(8,128)(2,1)}, u32[]{:S(2)}) %copy-start.2) | copy-done | bytes 2097176
  5.9 1.6 %copy-done.5 = bf16[1024,1024]{1,0:T(8,128)(2,1)S(1)} copy-done((bf16[1024,1024]{1,0:T(8,128)(2,1)S(1)}, bf16[1024,1024]{1,0:T(8,128)(2,1)}, u32[]{:S(2)}) %copy-start.5) | copy-done | bytes 2097176
  7.5 1.6 %copy-done.8 = bf16[1024,1024]{1,0:T(8,128)(2,1)S(1)} copy-done((bf16[1024,1024]{1,0:T(8,128)(2,1)S(1)}, bf16[1024,1024]{1,0:T(8,128)(2,1)}, u32[]{:S(2)}) %copy-start.8) | copy-done | bytes 2097176
  9.1 10.6 %states.1 = (f32[2,8,128,128]{3,2,1,0:T(8,128)S(1)}, f32[4,2,2,128,128]{4,3,2,1,0:T(8,128)S(1)}) custom-call(s32[5]{0:T(128)S(1)} %pad_add_fusion.bits, bf16[1024,1024]{1,0:T(8,128)(2,1)S(1)} %copy-done, bf16[1024,1024]{1,0:T(8,128)(2,1)S(1)} %copy-done.5, bf16[1024,1024]{1,0:T(8,128)(2,1)S(1)} %copy-done.8, bf16[1024,1024]{1,0:T(8,128)(2,1)S(1)} %copy-done.2, ...), custom_call_target="tpu_custom_call" | custom-call | tf_op jit(solution)/shard_map/states/pallas_call | solution.py:156
  19.7 0.0 copy-done.11
  19.7 0.0 copy-start.17
  19.7 20.3 %all_to_all.10 = f32[4,2,2,128,128]{4,3,2,1,0:T(8,128)S(1)} all-to-all(f32[4,2,2,128,128]{4,3,2,1,0:T(8,128)S(1)} %get-tuple-element.17), channel_id=1, replica_groups={{0,8,16,24},{32,40,48,56},{64,72,80,88},{96,104,112,120},{1,9,17,25},{3..., dimensions={0} | all-to-all | bytes 2097152 | tf_op jit(solution)/shard_map/all_to_all | solution.py:173
  40.0 0.1 reduce_sum.9
  40.1 1.7 %collective-permute-start.3 = (f32[2,2,128,128]{3,2,1,0:T(8,128)S(1)}, f32[2,2,128,128]{3,2,1,0:T(8,128)S(1)}, u32[]{:S(2)}, u32[]{:S(2)}) collective-permute-start(f32[2,2,128,128]{3,2,1,0:T(8,128)S(1)} %reduce_sum.9), channel_id=1, source_target_pairs={{0,32},{8,40},{16,48},{24,56},{32,0},{40,8},{48,16},{56,24},{64,96... | collective-permute-start | bytes 786440 | tf_op jit(solution)/shard_map/ppermute | solution.py:130
  41.7 1.1 slice_bitcast_fusion
  42.8 0.0 copy-done.17
  42.8 0.6 collective-permute-start.1
  43.3 3.7 %collective-permute-done.3 = f32[2,2,128,128]{3,2,1,0:T(8,128)S(1)} collective-permute-done((f32[2,2,128,128]{3,2,1,0:T(8,128)S(1)}, f32[2,2,128,128]{3,2,1,0:T(8,128)S(1)}, u32[]{:S(2)}, u32[]{:S(2)}) %collective-permute-start.3) | collective-permute-done | bytes 262176 | tf_op jit(solution)/shard_map/ppermute | solution.py:130
  47.0 3.1 %collective-permute-start.4 = (f32[2,128,128]{2,1,0:T(8,128)S(1)}, f32[2,128,128]{2,1,0:T(8,128)S(1)}, u32[]{:S(2)}, u32[]{:S(2)}) collective-permute-start(f32[2,128,128]{2,1,0:T(8,128)S(1)} %get-tuple-element.27), channel_id=1, source_target_pairs={{0,96},{8,104},{16,112},{24,120},{32,64},{40,72},{48,80},{56,88},{... | collective-permute-start | bytes 393224 | tf_op jit(solution)/shard_map/ppermute | solution.py:130
  50.1 0.6 collective-permute-start
  50.7 2.6 %collective-permute-done.4 = f32[2,128,128]{2,1,0:T(8,128)S(1)} collective-permute-done((f32[2,128,128]{2,1,0:T(8,128)S(1)}, f32[2,128,128]{2,1,0:T(8,128)S(1)}, u32[]{:S(2)}, u32[]{:S(2)}) %collective-permute-start.4) | collective-permute-done | bytes 131104 | tf_op jit(solution)/shard_map/ppermute | solution.py:130
  53.3 1.1 broadcast_in_dim.23
  54.4 3.6 %all-to-all-start.1 = ((f32[4,2,2,128,128]{4,3,2,1,0:T(8,128)}), f32[4,2,2,128,128]{4,3,2,1,0:T(8,128)S(1)}, u32[]{:S(2)}, u32[]{:S(2)}) async-start(f32[4,2,2,128,128]{4,3,2,1,0:T(8,128)} %broadcast_in_dim.23), calls=%async_computation.1 | async-start | bytes 2097152 | tf_op jit(solution)/shard_map/all_to_all | solution.py:182
  58.0 0.0 collective-permute-done.1
  58.0 1.3 fusion.12
  59.3 3.3 %collective-permute-start.2 = (f32[8,128,128]{2,1,0:T(8,128)S(1)}, f32[8,128,128]{2,1,0:T(8,128)S(1)}, u32[]{:S(2)}, u32[]{:S(2)}) collective-permute-start(f32[8,128,128]{2,1,0:T(8,128)S(1)} %fusion.12), channel_id=1, source_target_pairs={{0,24},{8,16},{16,8},{24,0},{32,56},{40,48},{48,40},{56,32},{64,88... | collective-permute-start | bytes 1572872 | tf_op jit(solution)/shard_map/ppermute | solution.py:130
  62.6 0.0 copy-done.1
  62.6 1.6 %copy-done.3 = bf16[1024,1024]{1,0:T(8,128)(2,1)S(1)} copy-done((bf16[1024,1024]{1,0:T(8,128)(2,1)S(1)}, bf16[1024,1024]{1,0:T(8,128)(2,1)}, u32[]{:S(2)}) %copy-start.3) | copy-done | bytes 2097176
  64.2 1.6 %copy-done.6 = bf16[1024,1024]{1,0:T(8,128)(2,1)S(1)} copy-done((bf16[1024,1024]{1,0:T(8,128)(2,1)S(1)}, bf16[1024,1024]{1,0:T(8,128)(2,1)}, u32[]{:S(2)}) %copy-start.6) | copy-done | bytes 2097176
  65.8 1.6 %copy-done.9 = bf16[1024,1024]{1,0:T(8,128)(2,1)S(1)} copy-done((bf16[1024,1024]{1,0:T(8,128)(2,1)S(1)}, bf16[1024,1024]{1,0:T(8,128)(2,1)}, u32[]{:S(2)}) %copy-start.9) | copy-done | bytes 2097176
  67.4 1.0 copy-done.12
  68.4 17.4 %group.1 = (f32[1024,1024]{1,0:T(8,128)S(1)}, f32[1024,1024]{1,0:T(8,128)}, f32[1024,1024]{1,0:T(8,128)}, f32[1024,128]{1,0:T(8,128)S(1)}) custom-call(bf16[1024,1024]{1,0:T(8,128)(2,1)S(1)} %copy-done.1, bf16[1024,1024]{1,0:T(8,128)(2,1)S(1)} %copy-done.6, bf16[1024,1024]{1,0:T(8,128)(2,1)S(1)} %copy-done.9, bf16[1024,1024]{1,0:T(8,128)(2,1)S(1)} %copy-done.3, ...), custom_call_target="tpu_custom_call" | custom-call | flops 4000000000 | bytes 20971520 | tf_op jit(solution)/shard_map/group/pallas_call | solution.py:188
  85.8 2.0 %copy-done.15 = f32[1024,1024]{1,0:T(8,128)} copy-done((f32[1024,1024]{1,0:T(8,128)}, f32[1024,1024]{1,0:T(8,128)S(1)}, u32[]{:S(2)}) %copy-start.15) | copy-done | bytes 4194328
  87.8 0.8 copy-done.20
  88.6 0.0 collective-permute-done.y1_ref
  88.6 0.0 collective-permute-done.2.y2_ref
  88.6 0.8 copy-done.18
  89.4 0.0 all-to-all-done.1.y3_ref
  89.4 1.6 %copy-done.4 = bf16[1024,1024]{1,0:T(8,128)(2,1)S(1)} copy-done((bf16[1024,1024]{1,0:T(8,128)(2,1)S(1)}, bf16[1024,1024]{1,0:T(8,128)(2,1)}, u32[]{:S(2)}) %copy-start.4) | copy-done | bytes 2097176
  91.0 1.0 copy-done.13
  92.1 2.2 %copy-done.16 = f32[1024,1024]{1,0:T(8,128)S(1)} copy-done((f32[1024,1024]{1,0:T(8,128)S(1)}, f32[1024,1024]{1,0:T(8,128)}, u32[]{:S(2)}) %copy-start.16) | copy-done | bytes 4194328
  94.3 1.0 copy-done.19
  95.3 1.0 copy-done.21
  96.4 11.6 %reads.1 = (bf16[1024,1024]{1,0:T(8,128)(2,1)}, f32[1024,128]{1,0:T(8,128)S(1)}) custom-call(s32[5]{0:T(128)S(1)} %pad_add_fusion.bits, bf16[1024,1024]{1,0:T(8,128)(2,1)S(1)} %copy-done.1, bf16[1024,1024]{1,0:T(8,128)(2,1)S(1)} %copy-done.4, f32[1024,8]{1,0:T(8,128)S(1)} %copy-done.13, f32[1024,1024]{1,0:T(8,128)S(1)} %copy-done.16, ...), custom_call_target="tpu_custom_call" | custom-call | flops 2000000000 | bytes 10485760 | tf_op jit(solution)/shard_map/reads/pallas_call | solution.py:199
  107.9 0.0 copy-done.22
  107.9 0.7 fusion
  108.6 0.0 collective-permute-start.5
  108.6 1.2 collective-permute-done.5
  109.8 1.5 %collective-permute-start.6 = (f32[8,256]{1,0:T(8,128)S(1)}, f32[8,256]{1,0:T(8,128)S(1)}, u32[]{:S(2)}, u32[]{:S(2)}) collective-permute-start(f32[8,256]{1,0:T(8,128)S(1)} %add.35), channel_id=1, source_target_pairs={{0,2},{1,3},{2,0},{3,1},{4,6},{5,7},{6,4},{7,5},{8,10},{9,11},{10,... | collective-permute-start | bytes 24584 | tf_op jit(solution)/shard_map/ppermute | solution.py:130
  111.3 2.2 %collective-permute-done.6 = f32[8,256]{1,0:T(8,128)S(1)} collective-permute-done((f32[8,256]{1,0:T(8,128)S(1)}, f32[8,256]{1,0:T(8,128)S(1)}, u32[]{:S(2)}, u32[]{:S(2)}) %collective-permute-start.6) | collective-permute-done | bytes 8224 | tf_op jit(solution)/shard_map/ppermute | solution.py:130
  113.5 2.8 %collective-permute-start.7 = (f32[8,256]{1,0:T(8,128)S(1)}, f32[8,256]{1,0:T(8,128)S(1)}, u32[]{:S(2)}, u32[]{:S(2)}) collective-permute-start(f32[8,256]{1,0:T(8,128)S(1)} %add.36), channel_id=1, source_target_pairs={{0,6},{1,7},{2,4},{3,5},{4,2},{5,3},{6,0},{7,1},{8,14},{9,15},{10,... | collective-permute-start | bytes 24584 | tf_op jit(solution)/shard_map/ppermute | solution.py:130
  116.2 2.1 %collective-permute-done.7 = f32[8,256]{1,0:T(8,128)S(1)} collective-permute-done((f32[8,256]{1,0:T(8,128)S(1)}, f32[8,256]{1,0:T(8,128)S(1)}, u32[]{:S(2)}, u32[]{:S(2)}) %collective-permute-start.7) | collective-permute-done | bytes 8224 | tf_op jit(solution)/shard_map/ppermute | solution.py:130
  118.3 0.2 collective-permute-start.8
  118.6 3.4 %collective-permute-done.8 = f32[8,256]{1,0:T(8,128)S(1)} collective-permute-done((f32[8,256]{1,0:T(8,128)S(1)}, f32[8,256]{1,0:T(8,128)S(1)}, u32[]{:S(2)}, u32[]{:S(2)}) %collective-permute-start.8) | collective-permute-done | bytes 8224 | tf_op jit(solution)/shard_map/ppermute | solution.py:130
  122.0 0.0 collective-permute-start.9
  122.0 4.8 %collective-permute-done.9 = f32[8,256]{1,0:T(8,128)S(1)} collective-permute-done((f32[8,256]{1,0:T(8,128)S(1)}, f32[8,256]{1,0:T(8,128)S(1)}, u32[]{:S(2)}, u32[]{:S(2)}) %collective-permute-start.9) | collective-permute-done | bytes 8224 | tf_op jit(solution)/shard_map/ppermute | solution.py:130
  126.8 0.4 collective-permute-start.10
  127.2 3.3 %collective-permute-done.10 = f32[8,256]{1,0:T(8,128)S(1)} collective-permute-done((f32[8,256]{1,0:T(8,128)S(1)}, f32[8,256]{1,0:T(8,128)S(1)}, u32[]{:S(2)}, u32[]{:S(2)}) %collective-permute-start.10) | collective-permute-done | bytes 8224 | tf_op jit(solution)/shard_map/ppermute | solution.py:130
  130.5 3.0 %collective-permute-start.11 = (f32[8,256]{1,0:T(8,128)S(1)}, f32[8,256]{1,0:T(8,128)S(1)}, u32[]{:S(2)}, u32[]{:S(2)}) collective-permute-start(f32[8,256]{1,0:T(8,128)S(1)} %add.40), channel_id=1, source_target_pairs={{0,96},{8,104},{16,112},{24,120},{32,64},{40,72},{48,80},{56,88},{... | collective-permute-start | bytes 24584 | tf_op jit(solution)/shard_map/ppermute | solution.py:130
  133.5 0.0 copy-done.7
  133.5 0.0 copy-done.10
  133.5 0.0 copy-done.14
  133.5 8.6 %returns.1 = (bf16[1024,1024]{1,0:T(8,128)(2,1)}, bf16[1024,1024]{1,0:T(8,128)(2,1)}) custom-call(s32[5]{0:T(128)S(1)} %pad_add_fusion.bits, bf16[1024,1024]{1,0:T(8,128)(2,1)S(1)} %copy-done.7, bf16[1024,1024]{1,0:T(8,128)(2,1)S(1)} %copy-done.10, f32[1024,1024]{1,0:T(8,128)S(1)} %copy-done.14, f32[1024,1024]{1,0:T(8,128)} %get-tuple-element.20.vn_ref, ...), custom_call_target="tpu_custom_call" | custom-call | flops 1000000000 | bytes 16777216 | tf_op jit(solution)/shard_map/returns/pallas_call | solution.py:222
  142.1 0.0 collective-permute-done.11
  142.1 0.6 fusion.6
  (31 shorter events, 0.1 us)
Async XLA Ops:
  2.7 1.6 %copy-start = (bf16[1024,1024]{1,0:T(8,128)(2,1)S(1)}, bf16[1024,1024]{1,0:T(8,128)(2,1)}, u32[]{:S(2)}) copy-start(bf16[1024,1024]{1,0:T(8,128)(2,1)} %q_ref.5) | copy-start | bytes 6291460
  4.3 1.6 %copy-start.2 = (bf16[1024,1024]{1,0:T(8,128)(2,1)S(1)}, bf16[1024,1024]{1,0:T(8,128)(2,1)}, u32[]{:S(2)}) copy-start(bf16[1024,1024]{1,0:T(8,128)(2,1)} %g_ref.5) | copy-start | bytes 6291460
  5.9 1.6 %copy-start.5 = (bf16[1024,1024]{1,0:T(8,128)(2,1)S(1)}, bf16[1024,1024]{1,0:T(8,128)(2,1)}, u32[]{:S(2)}) copy-start(bf16[1024,1024]{1,0:T(8,128)(2,1)} %k_ref.5) | copy-start | bytes 6291460
  7.5 1.6 %copy-start.8 = (bf16[1024,1024]{1,0:T(8,128)(2,1)S(1)}, bf16[1024,1024]{1,0:T(8,128)(2,1)}, u32[]{:S(2)}) copy-start(bf16[1024,1024]{1,0:T(8,128)(2,1)} %v_ref.5) | copy-start | bytes 6291460
  9.1 10.6 %copy-start.11 = (f32[1024,8]{1,0:T(8,128)}, f32[1024,8]{1,0:T(8,128)S(1)}, u32[]{:S(2)}) copy-start(f32[1024,8]{1,0:T(8,128)S(1)} %fusion.1.w_ref) | copy-start | bytes 98308
  19.7 23.1 %copy-start.17 = (f32[2,8,128,128]{3,2,1,0:T(8,128)}, f32[2,8,128,128]{3,2,1,0:T(8,128)S(1)}, u32[]{:S(2)}) copy-start(f32[2,8,128,128]{3,2,1,0:T(8,128)S(1)} %get-tuple-element.16) | copy-start | bytes 3145732
  40.1 6.9 %collective-permute-start.3 = (f32[2,2,128,128]{3,2,1,0:T(8,128)S(1)}, f32[2,2,128,128]{3,2,1,0:T(8,128)S(1)}, u32[]{:S(2)}, u32[]{:S(2)}) collective-permute-start(f32[2,2,128,128]{3,2,1,0:T(8,128)S(1)} %reduce_sum.9), channel_id=1, source_target_pairs={{0,32},{8,40},{16,48},{24,56},{32,0},{40,8},{48,16},{56,24},{64,96... | collective-permute-start | bytes 786440 | tf_op jit(solution)/shard_map/ppermute | solution.py:130
  42.8 15.3 %collective-permute-start.1 = (f32[8,128,128]{2,1,0:T(8,128)}, f32[8,128,128]{2,1,0:T(8,128)}, u32[]{:S(2)}, u32[]{:S(2)}) collective-permute-start(f32[8,128,128]{2,1,0:T(8,128)} %get-tuple-element.24), channel_id=1, source_target_pairs={{0,8},{8,0},{16,24},{24,16},{32,40},{40,32},{48,56},{56,48},{64,72... | collective-permute-start | bytes 1572872 | tf_op jit(solution)/shard_map/ppermute | solution.py:130
  47.0 6.3 %collective-permute-start.4 = (f32[2,128,128]{2,1,0:T(8,128)S(1)}, f32[2,128,128]{2,1,0:T(8,128)S(1)}, u32[]{:S(2)}, u32[]{:S(2)}) collective-permute-start(f32[2,128,128]{2,1,0:T(8,128)S(1)} %get-tuple-element.27), channel_id=1, source_target_pairs={{0,96},{8,104},{16,112},{24,120},{32,64},{40,72},{48,80},{56,88},{... | collective-permute-start | bytes 393224 | tf_op jit(solution)/shard_map/ppermute | solution.py:130
  50.1 38.5 %collective-permute-start = (f32[8,128,128]{2,1,0:T(8,128)}, f32[8,128,128]{2,1,0:T(8,128)}, u32[]{:S(2)}, u32[]{:S(2)}) collective-permute-start(f32[8,128,128]{2,1,0:T(8,128)} %get-tuple-element.25), channel_id=1, source_target_pairs={{0,8},{8,0},{16,24},{24,16},{32,40},{40,32},{48,56},{56,48},{64,72... | collective-permute-start | bytes 1572872 | tf_op jit(solution)/shard_map/ppermute | solution.py:130
  54.4 8.2 %copy-start.1 = (bf16[1024,1024]{1,0:T(8,128)(2,1)S(1)}, bf16[1024,1024]{1,0:T(8,128)(2,1)}, u32[]{:S(2)}) copy-start(bf16[1024,1024]{1,0:T(8,128)(2,1)} %q_ref.5) | copy-start | bytes 6291460
  54.4 35.1 %all-to-all-start.1 = ((f32[4,2,2,128,128]{4,3,2,1,0:T(8,128)}), f32[4,2,2,128,128]{4,3,2,1,0:T(8,128)S(1)}, u32[]{:S(2)}, u32[]{:S(2)}) async-start(f32[4,2,2,128,128]{4,3,2,1,0:T(8,128)} %broadcast_in_dim.23), calls=%async_computation.1 | async-start | bytes 2097152 | tf_op jit(solution)/shard_map/all_to_all | solution.py:182
  59.3 29.3 %collective-permute-start.2 = (f32[8,128,128]{2,1,0:T(8,128)S(1)}, f32[8,128,128]{2,1,0:T(8,128)S(1)}, u32[]{:S(2)}, u32[]{:S(2)}) collective-permute-start(f32[8,128,128]{2,1,0:T(8,128)S(1)} %fusion.12), channel_id=1, source_target_pairs={{0,24},{8,16},{16,8},{24,0},{32,56},{40,48},{48,40},{56,32},{64,88... | collective-permute-start | bytes 1572872 | tf_op jit(solution)/shard_map/ppermute | solution.py:130
  62.6 1.6 %copy-start.3 = (bf16[1024,1024]{1,0:T(8,128)(2,1)S(1)}, bf16[1024,1024]{1,0:T(8,128)(2,1)}, u32[]{:S(2)}) copy-start(bf16[1024,1024]{1,0:T(8,128)(2,1)} %g_ref.5) | copy-start | bytes 6291460
  64.2 1.6 %copy-start.6 = (bf16[1024,1024]{1,0:T(8,128)(2,1)S(1)}, bf16[1024,1024]{1,0:T(8,128)(2,1)}, u32[]{:S(2)}) copy-start(bf16[1024,1024]{1,0:T(8,128)(2,1)} %k_ref.5) | copy-start | bytes 6291460
  65.8 1.6 %copy-start.9 = (bf16[1024,1024]{1,0:T(8,128)(2,1)S(1)}, bf16[1024,1024]{1,0:T(8,128)(2,1)}, u32[]{:S(2)}) copy-start(bf16[1024,1024]{1,0:T(8,128)(2,1)} %v_ref.5) | copy-start | bytes 6291460
  67.4 1.0 copy-start.12
  85.8 2.0 %copy-start.15 = (f32[1024,1024]{1,0:T(8,128)}, f32[1024,1024]{1,0:T(8,128)S(1)}, u32[]{:S(2)}) copy-start(f32[1024,1024]{1,0:T(8,128)S(1)} %get-tuple-element.14.qn_ref) | copy-start | bytes 12582916
  87.8 0.8 copy-start.20
  88.6 0.8 copy-start.18
  89.4 1.6 %copy-start.4 = (bf16[1024,1024]{1,0:T(8,128)(2,1)S(1)}, bf16[1024,1024]{1,0:T(8,128)(2,1)}, u32[]{:S(2)}) copy-start(bf16[1024,1024]{1,0:T(8,128)(2,1)} %g_ref.5) | copy-start | bytes 6291460
  91.0 1.0 copy-start.13
  92.1 2.2 %copy-start.16 = (f32[1024,1024]{1,0:T(8,128)S(1)}, f32[1024,1024]{1,0:T(8,128)}, u32[]{:S(2)}) copy-start(f32[1024,1024]{1,0:T(8,128)} %copy-done.15) | copy-start | bytes 12582916
  94.3 1.0 copy-start.19
  95.3 1.0 copy-start.21
  96.3 11.6 %copy-start.22 = (s32[1024]{0:T(1024)S(1)}, s32[1024]{0:T(1024)}, u32[]{:S(2)}) copy-start(s32[1024]{0:T(1024)} %param.12) | copy-start | bytes 12292
  96.3 37.2 %copy-start.7 = (bf16[1024,1024]{1,0:T(8,128)(2,1)S(1)}, bf16[1024,1024]{1,0:T(8,128)(2,1)}, u32[]{:S(2)}) copy-start(bf16[1024,1024]{1,0:T(8,128)(2,1)} %k_ref.5) | copy-start | bytes 6291460
  96.3 37.2 %copy-start.10 = (bf16[1024,1024]{1,0:T(8,128)(2,1)S(1)}, bf16[1024,1024]{1,0:T(8,128)(2,1)}, u32[]{:S(2)}) copy-start(bf16[1024,1024]{1,0:T(8,128)(2,1)} %v_ref.5) | copy-start | bytes 6291460
  96.3 37.2 %copy-start.14 = (f32[1024,1024]{1,0:T(8,128)S(1)}, f32[1024,1024]{1,0:T(8,128)}, u32[]{:S(2)}) copy-start(f32[1024,1024]{1,0:T(8,128)} %get-tuple-element.19.kn_ref) | copy-start | bytes 12582916
  108.6 1.2 collective-permute-start.5
  109.8 3.7 %collective-permute-start.6 = (f32[8,256]{1,0:T(8,128)S(1)}, f32[8,256]{1,0:T(8,128)S(1)}, u32[]{:S(2)}, u32[]{:S(2)}) collective-permute-start(f32[8,256]{1,0:T(8,128)S(1)} %add.35), channel_id=1, source_target_pairs={{0,2},{1,3},{2,0},{3,1},{4,6},{5,7},{6,4},{7,5},{8,10},{9,11},{10,... | collective-permute-start | bytes 24584 | tf_op jit(solution)/shard_map/ppermute | solution.py:130
  113.5 4.9 %collective-permute-start.7 = (f32[8,256]{1,0:T(8,128)S(1)}, f32[8,256]{1,0:T(8,128)S(1)}, u32[]{:S(2)}, u32[]{:S(2)}) collective-permute-start(f32[8,256]{1,0:T(8,128)S(1)} %add.36), channel_id=1, source_target_pairs={{0,6},{1,7},{2,4},{3,5},{4,2},{5,3},{6,0},{7,1},{8,14},{9,15},{10,... | collective-permute-start | bytes 24584 | tf_op jit(solution)/shard_map/ppermute | solution.py:130
  118.3 3.7 %collective-permute-start.8 = (f32[8,256]{1,0:T(8,128)S(1)}, f32[8,256]{1,0:T(8,128)S(1)}, u32[]{:S(2)}, u32[]{:S(2)}) collective-permute-start(f32[8,256]{1,0:T(8,128)S(1)} %add.37), channel_id=1, source_target_pairs={{0,8},{8,0},{16,24},{24,16},{32,40},{40,32},{48,56},{56,48},{64,72... | collective-permute-start | bytes 24584 | tf_op jit(solution)/shard_map/ppermute | solution.py:130
  122.0 4.9 %collective-permute-start.9 = (f32[8,256]{1,0:T(8,128)S(1)}, f32[8,256]{1,0:T(8,128)S(1)}, u32[]{:S(2)}, u32[]{:S(2)}) collective-permute-start(f32[8,256]{1,0:T(8,128)S(1)} %add.38), channel_id=1, source_target_pairs={{0,24},{8,16},{16,8},{24,0},{32,56},{40,48},{48,40},{56,32},{64,88... | collective-permute-start | bytes 24584 | tf_op jit(solution)/shard_map/ppermute | solution.py:130
  126.8 3.7 %collective-permute-start.10 = (f32[8,256]{1,0:T(8,128)S(1)}, f32[8,256]{1,0:T(8,128)S(1)}, u32[]{:S(2)}, u32[]{:S(2)}) collective-permute-start(f32[8,256]{1,0:T(8,128)S(1)} %add.39), channel_id=1, source_target_pairs={{0,32},{8,40},{16,48},{24,56},{32,0},{40,8},{48,16},{56,24},{64,96... | collective-permute-start | bytes 24584 | tf_op jit(solution)/shard_map/ppermute | solution.py:130
  130.5 11.6 %collective-permute-start.11 = (f32[8,256]{1,0:T(8,128)S(1)}, f32[8,256]{1,0:T(8,128)S(1)}, u32[]{:S(2)}, u32[]{:S(2)}) collective-permute-start(f32[8,256]{1,0:T(8,128)S(1)} %add.40), channel_id=1, source_target_pairs={{0,96},{8,104},{16,112},{24,120},{32,64},{40,72},{48,80},{56,88},{... | collective-permute-start | bytes 24584 | tf_op jit(solution)/shard_map/ppermute | solution.py:130

commit v2 on v1

v2 whole, which is shorter than its diff:
```python
import functools

import jax
import jax.numpy as jnp
from jax import lax
from jax.experimental import pallas as pl
from jax.experimental.pallas import tpu as pltpu
from jax.sharding import PartitionSpec as P

DH = 128
CHUNK = 256

precise = lax.Precision.HIGHEST
f32 = jnp.float32
bf16 = jnp.bfloat16


def mm(a, b, ca, cb):
    return lax.dot_general(a, b, (((ca,), (cb,)), ((), ())), preferred_element_type=f32)


def states_kernel(bits, q_hbm, k_hbm, v_hbm, g_hbm, w_ref, near1_ref, near2_ref, *rest):
    far_refs, buf, sem = rest[:4], rest[4], rest[5]
    sources = (q_hbm, k_hbm, v_hbm, g_hbm)
    wide = buf.shape[-1]
    each = wide // DH

    def copy(j, a):
        cols = pl.ds(pl.multiple_of((bits[5] ^ j) * wide, wide), wide)
        return pltpu.make_async_copy(sources[a].at[:, cols], buf.at[j, a], sem.at[j, a])

    for j in range(4):
        for a in range(4):
            copy(j, a).start()
    w = w_ref[...]
    for j in range(4):
        for a in range(4):
            copy(j, a).wait()
        for i in range(each):
            c = slice(i * DH, (i + 1) * DH)
            head = (bits[5] ^ j) * each + i
            own = mm(buf[j, 2, :, c].T, buf[j, 1, :, c], 1, 0)
            gt = buf[j, 3, :, c].T.astype(f32)
            parts = [(gt * w[l : l + 1, :]).astype(bf16) for l in range(1, 5)]
            grads = mm(jnp.concatenate(parts, 0), buf[j, 0, :, c], 1, 0)
            xs = [
                jnp.where(bits[l] > 0, grads[l * DH : (l + 1) * DH], own) for l in range(4)
            ]
            near1_ref[head] = xs[0]
            near2_ref[head] = xs[1]
            far_refs[j][0, i] = xs[2]
            far_refs[j][1, i] = xs[3]


def group_kernel(q_ref, k_ref, v_ref, g_ref, w_ref, qn_ref, kn_ref, vn_ref, lam_ref):
    head = pl.program_id(0)
    scale = 1.0 / DH
    length = q_ref.shape[0]
    count = length // CHUNK
    rows = lax.broadcasted_iota(jnp.int32, (CHUNK, CHUNK), 0)
    cols = lax.broadcasted_iota(jnp.int32, (CHUNK, CHUNK), 1)
    causal = rows >= cols

    @pl.when(head == 0)
    def _():
        lam_ref[...] = jnp.zeros_like(lam_ref)

    state = jnp.zeros((DH, DH), f32)
    gps, scs, qss = [], [], []
    for i in range(count):
        at = pl.ds(i * CHUNK, CHUNK)
        q, k, v, g = q_ref[at, :], k_ref[at, :], v_ref[at, :], g_ref[at, :]
        w0 = w_ref[at, 0:1]
        qf = q.astype(f32)
        qs = (qf * w0).astype(bf16)
        gp = jnp.where(causal, mm(g, v, 1, 1), 0.0).astype(bf16)
        sc = jnp.where(causal, mm(qs, k, 1, 1), 0.0).astype(bf16)
        u = mm(gp, k, 1, 0)
        if i > 0:
            u = u + mm(g, state.astype(bf16), 1, 1)
        lam_ref[at, :] += qf * u
        qn_ref[at, :] = (scale * w0) * u
        if i < count - 1:
            state = state + mm(k, v, 0, 0)
        gps.append(gp)
        scs.append(sc)
        qss.append(qs)
    state = jnp.zeros((DH, DH), f32)
    for i in reversed(range(count)):
        at = pl.ds(i * CHUNK, CHUNK)
        k, v, g = k_ref[at, :], v_ref[at, :], g_ref[at, :]
        kn = mm(gps[i], qss[i], 0, 0)
        vn = mm(scs[i], g, 0, 0)
        if i < count - 1:
            sb = state.astype(bf16)
            kn = kn + mm(v, sb, 1, 1)
            vn = vn + mm(k, sb, 1, 0)
        kn_ref[at, :] = scale * kn
        vn_ref[at, :] = scale * vn
        if i > 0:
            state = state + mm(qss[i], g, 0, 0)


def gather_states(bits, keep, st, y1_ref, y2a_ref, y2b_ref, y3_refs, y4_refs, put):
    heads = y1_ref.shape[0]
    each = heads // 4
    for j in range(4):
        for i in range(each):
            head = (bits[5] ^ j) * each + i
            ys = (
                y1_ref[head],
                y2a_ref[head] + y2b_ref[head],
                y3_refs[j][i],
                y4_refs[j][i],
            )
            put(st, head, [jnp.where(bits[l] == keep, ys[l], 0.0) for l in range(4)])


def reads_kernel(bits, q_ref, g_ref, w_ref, qn_ref, lam0_ref, y1_ref, y2a_ref, y2b_ref, *rest):
    y3_refs, y4_refs, (out_ref, lam_ref, st) = rest[:4], rest[4:8], rest[8:]
    scale = 1.0 / DH
    heads = y1_ref.shape[0]

    def put(st, head, parts):
        st[head] = jnp.concatenate(parts, 1).astype(bf16)

    @pl.when(pl.program_id(0) == 0)
    def _():
        gather_states(bits, 1, st, y1_ref, y2a_ref, y2b_ref, y3_refs, y4_refs, put)

    tile = q_ref.shape[0]
    w = w_ref[...]
    wide = [jnp.broadcast_to(w[:, l : l + 1], (tile, DH)) for l in range(1, 5)]
    acc = [None] * 4
    for h in range(heads):
        c = slice(h * DH, (h + 1) * DH)
        reads = mm(g_ref[:, c], st[h], 1, 0)
        q = q_ref[:, c].astype(f32)
        total = None
        for l in range(4):
            read = reads[:, l * DH : (l + 1) * DH]
            product = q * read
            acc[l] = product if acc[l] is None else acc[l] + product
            term = wide[l] * read
            total = term if total is None else total + term
        out_ref[:, c] = (qn_ref[:, c] + scale * total).astype(bf16)
    lane = lax.broadcasted_iota(jnp.int32, (1, DH), 1)
    lam = jnp.where(lane == 0, jnp.sum(lam0_ref[...], 1, keepdims=True), 0.0)
    for l in range(4):
        here = (lane == l + 1) & (bits[4] > l)
        lam = jnp.where(here, jnp.sum(acc[l], 1, keepdims=True), lam)
    lam_ref[...] = scale * lam


def returns_kernel(bits, k_ref, v_ref, kn_ref, vn_ref, y1_ref, y2a_ref, y2b_ref, *rest):
    y3_refs, y4_refs, (key_ref, value_ref, st) = rest[:4], rest[4:8], rest[8:]
    scale = 1.0 / DH
    heads = y1_ref.shape[0]

    def put(st, head, parts):
        st[head] = (parts[0] + parts[1] + parts[2] + parts[3]).astype(bf16)

    @pl.when(pl.program_id(0) == 0)
    def _():
        gather_states(bits, 0, st, y1_ref, y2a_ref, y2b_ref, y3_refs, y4_refs, put)

    for h in range(heads):
        c = slice(h * DH, (h + 1) * DH)
        key_ref[:, c] = (kn_ref[:, c] + scale * mm(v_ref[:, c], st[h], 1, 0)).astype(bf16)
        value_ref[:, c] = (vn_ref[:, c] + scale * mm(k_ref[:, c], st[h], 1, 1)).astype(bf16)


def flip(x, axis, mask):
    return lax.ppermute(x, axis, [(i, i ^ mask) for i in range(lax.axis_size(axis))])


def local(queries, keys, values, out_grad, level_table, table_index, reach):
    length = queries.shape[0]
    heads = queries.shape[1] // DH
    span = lax.axis_size("seq")
    group = lax.axis_index("seq")
    bits = jnp.bitwise_and(jnp.right_shift(group, jnp.arange(4, dtype=jnp.int32)), 1)
    place = jnp.bitwise_and(group, 3)
    bits = jnp.concatenate([bits, reach.astype(jnp.int32), place[None].astype(jnp.int32)])
    picker = (
        table_index[:, None] == jnp.arange(level_table.shape[1], dtype=jnp.int32)[None, :]
    ).astype(f32)
    level_ids = jnp.arange(8, dtype=jnp.int32)
    table = jnp.pad(level_table, ((0, 3), (0, 0)))
    table = jnp.where((level_ids <= reach[0])[:, None], table, 0.0)
    weights = jnp.dot(picker, table.T, precision=precise)
    each = heads // 4

    whole = pl.BlockSpec(memory_space=pltpu.VMEM)
    near, near2, *far = pl.pallas_call(
        states_kernel,
        in_specs=[pl.BlockSpec(memory_space=pltpu.SMEM)]
        + [pl.BlockSpec(memory_space=pl.ANY)] * 4
        + [whole],
        out_specs=[whole] * 6,
        out_shape=[jax.ShapeDtypeStruct((heads, DH, DH), f32)] * 2
        + [jax.ShapeDtypeStruct((2, each, DH, DH), f32)] * 4,
        scratch_shapes=[
            pltpu.VMEM((4, 4, length, each * DH), bf16),
            pltpu.SemaphoreType.DMA((4, 4)),
        ],
        compiler_params=pltpu.CompilerParams(vmem_limit_bytes=60 * 2**20),
        name="states",
    )(bits, queries, keys, values, out_grad, weights.T)

    rows = (far[0] + flip(far[2], "seq", 2)) + (flip(far[1], "seq", 1) + flip(far[3], "seq", 3))
    rows, near, near2 = lax.optimization_barrier((rows, near, near2))
    other = flip(rows, "seq", 4)
    y1 = flip(near, "seq", 1)
    y2a = flip(near2, "seq", 3)
    y2b = flip(near2, "seq", 2)
    y3 = other[0]
    y4 = flip(rows[1] + other[1], "seq", 12)
    y3s = [y3] + [flip(y3, "seq", m) for m in (1, 2, 3)]
    y4s = [y4] + [flip(y4, "seq", m) for m in (1, 2, 3)]
    arrived = (y1, y2a, y2b, *y3s, *y4s)

    token_spec = pl.BlockSpec((length, DH), lambda h, *_: (0, h))
    fixed = lambda shape: pl.BlockSpec(shape, lambda h, *_: (0,) * len(shape))
    tile = 256
    tile_spec = pl.BlockSpec((tile, heads * DH), lambda i, *_: (i, 0))
    lam_spec = pl.BlockSpec((tile, DH), lambda i, *_: (i, 0))
    arrived_specs = [fixed(y.shape) for y in arrived]
    params = pltpu.CompilerParams(
        dimension_semantics=("arbitrary",), vmem_limit_bytes=60 * 2**20
    )
    tokens_f32 = jax.ShapeDtypeStruct((length, heads * DH), f32)
    tokens_bf16 = jax.ShapeDtypeStruct((length, heads * DH), bf16)
    qn, kn, vn, lam0 = pl.pallas_call(
        group_kernel,
        grid=(heads,),
        in_specs=[token_spec] * 4 + [fixed((length, 8))],
        out_specs=[token_spec] * 3 + [fixed((length, DH))],
        out_shape=[tokens_f32] * 3 + [jax.ShapeDtypeStruct((length, DH), f32)],
        compiler_params=params,
        cost_estimate=pl.CostEstimate(flops=4 * 10**9, bytes_accessed=20 * 2**20, transcendentals=0),
        name="group",
    )(queries, keys, values, out_grad, weights)

    query_grad, lam = pl.pallas_call(
        reads_kernel,
        grid_spec=pltpu.PrefetchScalarGridSpec(
            num_scalar_prefetch=1,
            grid=(length // tile,),
            in_specs=[tile_spec] * 2
            + [pl.BlockSpec((tile, 8), lambda i, *_: (i, 0)), tile_spec, lam_spec]
            + arrived_specs,
            out_specs=[tile_spec, lam_spec],
            scratch_shapes=[pltpu.VMEM((heads, DH, 4 * DH), bf16)],
        ),
        out_shape=[tokens_bf16, jax.ShapeDtypeStruct((length, DH), f32)],
        compiler_params=params,
        cost_estimate=pl.CostEstimate(flops=2 * 10**9, bytes_accessed=10 * 2**20, transcendentals=0),
        name="reads",
    )(bits, queries, out_grad, weights, qn, lam0, *arrived)

    total = lax.dot_general(lam[:, :8], picker, (((0,), (0,)), ((), ())), precision=precise)
    total = total + flip(total, "head", 1)
    for axis, unit in (("head", 2), ("seq", 1), ("seq", 4)):
        one, two, three = [flip(total, axis, m * unit) for m in (1, 2, 3)]
        total = (total + two) + (one + three)
    table_grad = total[: level_table.shape[0]] / (length * span)

    key_grad, value_grad = pl.pallas_call(
        returns_kernel,
        grid_spec=pltpu.PrefetchScalarGridSpec(
            num_scalar_prefetch=1,
            grid=(length // tile,),
            in_specs=[tile_spec] * 4 + arrived_specs,
            out_specs=[tile_spec] * 2,
            scratch_shapes=[pltpu.VMEM((heads, DH, DH), bf16)],
        ),
        out_shape=[tokens_bf16] * 2,
        compiler_params=params,
        cost_estimate=pl.CostEstimate(flops=10**9, bytes_accessed=16 * 2**20, transcendentals=0),
        name="returns",
    )(bits, keys, values, kn, vn, *arrived)
    return query_grad, key_grad, value_grad, table_grad


def solution(mesh):
    return jax.shard_map(
        local,
        mesh=mesh,
        in_specs=(
            P("seq", "head"),
            P("seq", "head"),
            P("seq", "head"),
            P("seq", "head"),
            P(),
            P("seq"),
            P("seq"),
        ),
        out_specs=(P("seq", "head"), P("seq", "head"), P("seq", "head"), P()),
        check_vma=False,
    )
```

time: 144 us -> 130 us (0.903)
  local copies, waits for them, and re-layouts: 24.8 us -> 2.08 us
  starting transfers between devices: 20.7 us -> 41.4 us
  blocking collectives: 20.3 us -> 0 us
  waiting for transfers between devices: 23.2 us -> 36 us
  Pallas kernels: 48.1 us -> 42 us
  matrix products: 2.04 us -> 3.69 us
    ppermute x12 -> x24, starting transfers between devices: 17.1 us -> 41.4 us  [flip(): lax.ppermute(x, axis, [(i, i ^ mask) for i in range(lax.axis_size(axis))])]
    unnamed x46 -> x26, local copies, waits for them, and re-layouts: 22.7 us -> 1.08 us
    all_to_all x1 -> x0, blocking collectives: 20.3 us -> none  [local(): got = lax.all_to_all(far, 'seq', 0, 0, axis_index_groups=rings)]
    ppermute x12 -> x24, waiting for transfers between devices: 23.2 us -> 36 us  [flip(): lax.ppermute(x, axis, [(i, i ^ mask) for i in range(lax.axis_size(axis))])]
    all_to_all x1 -> x0, starting transfers between devices: 3.65 us -> none  [local(): lax.all_to_all(jnp.broadcast_to(back[None], (4,) + back.shape), 'seq', 0,...]
    pallas_call x1, Pallas kernels: 10.6 us -> 7.17 us  [local(): pl.pallas_call(states_kernel, in_specs=[pl.BlockSpec(memory_space=pltpu.S...]
    pallas_call x1, Pallas kernels: 11.6 us -> 9.64 us  [local(): pl.pallas_call(reads_kernel, grid_spec=pltpu.PrefetchScalarGridSpec(num_s...]
  transfers between devices with their start and end apart: 13 -> 24, of which waited for: 8 -> 10; matrix products, arithmetic and copies ran while one was open for 2% -> 1% of each run, Pallas kernels for 18% -> 20%
where the time goes in v2:
time: 130 us; the launch traced here: 129 us
  Pallas kernels  42 us (32%)
  starting transfers between devices  41.4 us (32%)
  waiting for transfers between devices  36 us (28%)
  matrix products  3.69 us (3%)
  other arithmetic  2.26 us (2%)
  local copies, waits for them, and re-layouts  2.08 us (2%)
  between operations  1.5 us (1%)
    ppermute x24, starting transfers between devices, flip(): lax.ppermute(x, axis, [(i, i ^ mask) for i in range(lax.axis_size(axis))])  41.4 us
    ppermute x24, waiting for transfers between devices, flip(): lax.ppermute(x, axis, [(i, i ^ mask) for i in range(lax.axis_size(axis))])  36 us
    pallas_call x1, Pallas kernels, local(): pl.pallas_call(group_kernel, grid=(heads,), in_specs=[token_spec] * 4 + [...  16.1 us
    pallas_call x1, Pallas kernels, local(): pl.pallas_call(reads_kernel, grid_spec=pltpu.PrefetchScalarGridSpec(num_s...  9.64 us
    pallas_call x1, Pallas kernels, local(): pl.pallas_call(returns_kernel, grid_spec=pltpu.PrefetchScalarGridSpec(num...  9.14 us
    pallas_call x1, Pallas kernels, local(): pl.pallas_call(states_kernel, in_specs=[pl.BlockSpec(memory_space=pltpu.S...  7.17 us
  transfers between devices with their start and end apart: 24, of which 10 were waited for; matrix products, arithmetic and copies ran while one was open for 1% of the time, Pallas kernels for 20%

profile of v2, /device:TPU:0, one launch (start us, length us, event | category | flops | bytes accessed | tf_op | source)
XLA Modules:
  0.0 128.9 jit_solution(1944824402634898025)
XLA Ops:
  1.3 0.6 pad_add_fusion.bits
  1.9 1.9 %fusion.1 = f32[1024,8]{0,1:T(8,128)} fusion(s32[1024]{0:T(1024)} %param.12, f32[5,256]{1,0:T(8,128)} %param.11, pred[8]{0:T(512)(128)(4,1)S(1)} %iota_compare_fusion.3), kind=kOutput, calls=%fused_computation.2 | convolution fusion | flops 25430016 | bytes 41992 | tf_op jit(solution)/shard_map/dot_general | solution.py:191
  3.8 7.2 %states.1 = (f32[8,128,128]{2,1,0:T(8,128)}, f32[8,128,128]{2,1,0:T(8,128)}, f32[2,2,128,128]{3,2,1,0:T(8,128)}, f32[2,2,128,128]{3,2,1,0:T(8,128)}, f32[2,2,128...) custom-call(s32[6]{0:T(128)} %pad_add_fusion.bits, bf16[1024,1024]{1,0:T(8,128)(2,1)} %q_ref.3, bf16[1024,1024]{1,0:T(8,128)(2,1)} %k_ref.3, ...), custom_call_target="tpu_custom_call" | custom-call | tf_op jit(solution)/shard_map/states/pallas_call | solution.py:195
  11.0 4.1 %collective-permute-start = (f32[2,2,128,128]{3,2,1,0:T(8,128)}, f32[2,2,128,128]{3,2,1,0:T(8,128)S(1)}, u32[]{:S(2)}, u32[]{:S(2)}) collective-permute-start(f32[2,2,128,128]{3,2,1,0:T(8,128)} %get-tuple-element.24), channel_id=1, source_target_pairs={{0,16},{8,24},{16,0},{24,8},{32,48},{40,56},{48,32},{56,40},{64,80... | collective-permute-start | bytes 786440 | tf_op jit(solution)/shard_map/ppermute | solution.py:174
  15.1 1.0 collective-permute-start.1
  16.1 0.0 collective-permute-start.2
  16.1 6.3 %collective-permute-done = f32[2,2,128,128]{3,2,1,0:T(8,128)S(1)} collective-permute-done((f32[2,2,128,128]{3,2,1,0:T(8,128)}, f32[2,2,128,128]{3,2,1,0:T(8,128)S(1)}, u32[]{:S(2)}, u32[]{:S(2)}) %collective-permute-start) | collective-permute-done | bytes 262176 | tf_op jit(solution)/shard_map/ppermute | solution.py:174
  22.4 5.5 %collective-permute-done.1 = f32[2,2,128,128]{3,2,1,0:T(8,128)S(1)} collective-permute-done((f32[2,2,128,128]{3,2,1,0:T(8,128)}, f32[2,2,128,128]{3,2,1,0:T(8,128)S(1)}, u32[]{:S(2)}, u32[]{:S(2)}) %collective-permute-start.1) | collective-permute-done | bytes 262176 | tf_op jit(solution)/shard_map/ppermute | solution.py:174
  28.0 0.0 collective-permute-done.2
  28.0 1.0 add_add_fusion
  29.0 1.7 %collective-permute-start.6 = (f32[2,2,128,128]{3,2,1,0:T(8,128)S(1)}, f32[2,2,128,128]{3,2,1,0:T(8,128)S(1)}, u32[]{:S(2)}, u32[]{:S(2)}) collective-permute-start(f32[2,2,128,128]{3,2,1,0:T(8,128)S(1)} %add_add_fusion), channel_id=1, source_target_pairs={{0,32},{8,40},{16,48},{24,56},{32,0},{40,8},{48,16},{56,24},{64,96... | collective-permute-start | bytes 786440 | tf_op jit(solution)/shard_map/ppermute | solution.py:174
  30.7 1.0 collective-permute-start.3
  31.7 4.8 %collective-permute-done.6 = f32[2,2,128,128]{3,2,1,0:T(8,128)S(1)} collective-permute-done((f32[2,2,128,128]{3,2,1,0:T(8,128)S(1)}, f32[2,2,128,128]{3,2,1,0:T(8,128)S(1)}, u32[]{:S(2)}, u32[]{:S(2)}) %collective-permute-start.6) | collective-permute-done | bytes 262176 | tf_op jit(solution)/shard_map/ppermute | solution.py:174
  36.5 0.0 copy-start.3
  36.5 3.1 %collective-permute-start.10 = (f32[2,128,128]{2,1,0:T(8,128)S(1)}, f32[2,128,128]{2,1,0:T(8,128)S(1)}, u32[]{:S(2)}, u32[]{:S(2)}) collective-permute-start(f32[2,128,128]{2,1,0:T(8,128)S(1)} %get-tuple-element.38), channel_id=1, source_target_pairs={{0,96},{8,104},{16,112},{24,120},{32,64},{40,72},{48,80},{56,88},{... | collective-permute-start | bytes 393224 | tf_op jit(solution)/shard_map/ppermute | solution.py:174
  39.6 3.4 %collective-permute-start.9 = (f32[2,128,128]{2,1,0:T(8,128)S(1)}, f32[2,128,128]{2,1,0:T(8,128)S(1)}, u32[]{:S(2)}, u32[]{:S(2)}) collective-permute-start(f32[2,128,128]{2,1,0:T(8,128)S(1)} %get-tuple-element.39.rest_0_), channel_id=1, source_target_pairs={{0,24},{8,16},{16,8},{24,0},{32,56},{40,48},{48,40},{56,32},{64,88... | collective-permute-start | bytes 393224 | tf_op jit(solution)/shard_map/ppermute | solution.py:174
  43.1 0.0 collective-permute-start.5
  43.1 2.5 %collective-permute-start.4 = (f32[8,128,128]{2,1,0:T(8,128)}, f32[8,128,128]{2,1,0:T(8,128)S(1)}, u32[]{:S(2)}, u32[]{:S(2)}) collective-permute-start(f32[8,128,128]{2,1,0:T(8,128)} %get-tuple-element.30), channel_id=1, source_target_pairs={{0,24},{8,16},{16,8},{24,0},{32,56},{40,48},{48,40},{56,32},{64,88... | collective-permute-start | bytes 1572872 | tf_op jit(solution)/shard_map/ppermute | solution.py:174
  45.5 0.0 collective-permute-done.10.rest_4_
  45.6 1.1 collective-permute-start.8
  46.7 12.9 %collective-permute-done.9.rest_3_ = f32[2,128,128]{2,1,0:T(8,128)S(1)} collective-permute-done((f32[2,128,128]{2,1,0:T(8,128)S(1)}, f32[2,128,128]{2,1,0:T(8,128)S(1)}, u32[]{:S(2)}, u32[]{:S(2)}) %collective-permute-start.9) | collective-permute-done | bytes 131104 | tf_op jit(solution)/shard_map/ppermute | solution.py:174
  59.6 1.0 collective-permute-start.7
  60.6 1.0 copy.12.w_ref
  61.6 0.0 collective-permute-done.8.rest_2_
  61.6 3.1 %collective-permute-start.13 = (f32[2,128,128]{2,1,0:T(8,128)S(1)}, f32[2,128,128]{2,1,0:T(8,128)S(1)}, u32[]{:S(2)}, u32[]{:S(2)}) collective-permute-start(f32[2,128,128]{2,1,0:T(8,128)S(1)} %collective-permute-done.10.rest_4_), channel_id=1, source_target_pairs={{0,24},{8,16},{16,8},{24,0},{32,56},{40,48},{48,40},{56,32},{64,88... | collective-permute-start | bytes 393224 | tf_op jit(solution)/shard_map/ppermute | solution.py:174
  64.7 0.0 collective-permute-done.7.rest_1_
  64.7 3.4 %collective-permute-start.12 = (f32[2,128,128]{2,1,0:T(8,128)S(1)}, f32[2,128,128]{2,1,0:T(8,128)S(1)}, u32[]{:S(2)}, u32[]{:S(2)}) collective-permute-start(f32[2,128,128]{2,1,0:T(8,128)S(1)} %collective-permute-done.10.rest_4_), channel_id=1, source_target_pairs={{0,16},{8,24},{16,0},{24,8},{32,48},{40,56},{48,32},{56,40},{64,80... | collective-permute-start | bytes 393224 | tf_op jit(solution)/shard_map/ppermute | solution.py:174
  68.1 0.0 collective-permute-done.3.y1_ref
  68.1 1.9 %collective-permute-start.11 = (f32[2,128,128]{2,1,0:T(8,128)S(1)}, f32[2,128,128]{2,1,0:T(8,128)S(1)}, u32[]{:S(2)}, u32[]{:S(2)}) collective-permute-start(f32[2,128,128]{2,1,0:T(8,128)S(1)} %collective-permute-done.10.rest_4_), channel_id=1, source_target_pairs={{0,8},{8,0},{16,24},{24,16},{32,40},{40,32},{48,56},{56,48},{64,72... | collective-permute-start | bytes 393224 | tf_op jit(solution)/shard_map/ppermute | solution.py:174
  70.0 16.1 %group.1 = (f32[1024,1024]{1,0:T(8,128)}, f32[1024,1024]{1,0:T(8,128)}, f32[1024,1024]{1,0:T(8,128)}, f32[1024,128]{1,0:T(8,128)}) custom-call(bf16[1024,1024]{1,0:T(8,128)(2,1)} %q_ref.3, bf16[1024,1024]{1,0:T(8,128)(2,1)} %k_ref.3, bf16[1024,1024]{1,0:T(8,128)(2,1)} %v_ref.3, bf16[1024,1024]{1,0:T(8,128)(2,1)} %g_ref.3, f32[1024,8]{1,0:T(8,128)} %copy.12.w_ref), custom_call_target="tpu_custom_call" | custom-call | flops 4000000000 | bytes 20971520 | tf_op jit(solution)/shard_map/group/pallas_call | solution.py:234
  86.2 0.0 collective-permute-done.5.y2b_ref
  86.2 0.0 collective-permute-done.4.y2a_ref
  86.2 0.0 collective-permute-done.13.rest_7_
  86.2 0.0 collective-permute-done.12.rest_6_
  86.2 0.0 collective-permute-done.11.rest_5_
  86.3 0.7 copy-done.1
  86.9 0.2 copy-done.2
  87.1 0.1 copy-done.8
  87.2 0.1 copy-done.9
  87.2 0.1 copy-done.10
  87.3 9.6 %reads.1 = (bf16[1024,1024]{1,0:T(8,128)(2,1)}, f32[1024,128]{1,0:T(8,128)}) custom-call(s32[6]{0:T(128)} %pad_add_fusion.bits, bf16[1024,1024]{1,0:T(8,128)(2,1)} %q_ref.3, bf16[1024,1024]{1,0:T(8,128)(2,1)} %g_ref.3, f32[1024,8]{1,0:T(8,128)} %copy.12.w_ref, f32[1024,1024]{1,0:T(8,128)} %get-tuple-element.21.qn_ref, ...), custom_call_target="tpu_custom_call" | custom-call | flops 2000000000 | bytes 10485760 | tf_op jit(solution)/shard_map/reads/pallas_call | solution.py:245
  96.9 1.7 %fusion = f32[8,256]{1,0:T(8,128)S(1)} fusion(f32[1024,128]{1,0:T(8,128)} %get-tuple-element.37, s32[1024]{0:T(1024)S(1)} %copy-done.12), kind=kOutput, calls=%fused_computation.1 | convolution fusion | flops 25427968 | bytes 536576 | tf_op jit(solution)/shard_map/dot_general | solution.py:262
  98.7 0.0 collective-permute-start.14
  98.7 1.2 collective-permute-done.14
  99.9 2.8 %collective-permute-start.17 = (f32[8,256]{1,0:T(8,128)S(1)}, f32[8,256]{1,0:T(8,128)S(1)}, u32[]{:S(2)}, u32[]{:S(2)}) collective-permute-start(f32[8,256]{1,0:T(8,128)S(1)} %add.52), channel_id=1, source_target_pairs={{0,6},{1,7},{2,4},{3,5},{4,2},{5,3},{6,0},{7,1},{8,14},{9,15},{10,... | collective-permute-start | bytes 24584 | tf_op jit(solution)/shard_map/ppermute | solution.py:174
  102.6 0.3 collective-permute-start.16
  102.9 1.7 %collective-permute-start.15 = (f32[8,256]{1,0:T(8,128)S(1)}, f32[8,256]{1,0:T(8,128)S(1)}, u32[]{:S(2)}, u32[]{:S(2)}) collective-permute-start(f32[8,256]{1,0:T(8,128)S(1)} %add.52), channel_id=1, source_target_pairs={{0,4},{1,5},{2,6},{3,7},{4,0},{5,1},{6,2},{7,3},{8,12},{9,13},{10,... | collective-permute-start | bytes 24584 | tf_op jit(solution)/shard_map/ppermute | solution.py:174
  104.6 0.2 collective-permute-done.17
  104.7 1.5 %collective-permute-done.16 = f32[8,256]{1,0:T(8,128)S(1)} collective-permute-done((f32[8,256]{1,0:T(8,128)S(1)}, f32[8,256]{1,0:T(8,128)S(1)}, u32[]{:S(2)}, u32[]{:S(2)}) %collective-permute-start.16) | collective-permute-done | bytes 8224 | tf_op jit(solution)/shard_map/ppermute | solution.py:174
  106.3 1.8 %collective-permute-done.15 = f32[8,256]{1,0:T(8,128)S(1)} collective-permute-done((f32[8,256]{1,0:T(8,128)S(1)}, f32[8,256]{1,0:T(8,128)S(1)}, u32[]{:S(2)}, u32[]{:S(2)}) %collective-permute-start.15) | collective-permute-done | bytes 8224 | tf_op jit(solution)/shard_map/ppermute | solution.py:174
  108.0 0.0 collective-permute-start.20
  108.1 0.6 collective-permute-start.19
  108.7 4.1 %collective-permute-start.18 = (f32[8,256]{1,0:T(8,128)S(1)}, f32[8,256]{1,0:T(8,128)S(1)}, u32[]{:S(2)}, u32[]{:S(2)}) collective-permute-start(f32[8,256]{1,0:T(8,128)S(1)} %add_add_fusion.2), channel_id=1, source_target_pairs={{0,16},{8,24},{16,0},{24,8},{32,48},{40,56},{48,32},{56,40},{64,80... | collective-permute-start | bytes 24584 | tf_op jit(solution)/shard_map/ppermute | solution.py:174
  112.7 0.2 collective-permute-done.20
  112.9 0.0 collective-permute-done.19
  112.9 1.5 %collective-permute-done.18 = f32[8,256]{1,0:T(8,128)S(1)} collective-permute-done((f32[8,256]{1,0:T(8,128)S(1)}, f32[8,256]{1,0:T(8,128)S(1)}, u32[]{:S(2)}, u32[]{:S(2)}) %collective-permute-start.18) | collective-permute-done | bytes 8224 | tf_op jit(solution)/shard_map/ppermute | solution.py:174
  114.5 1.5 %collective-permute-start.23 = (f32[8,256]{1,0:T(8,128)S(1)}, f32[8,256]{1,0:T(8,128)S(1)}, u32[]{:S(2)}, u32[]{:S(2)}) collective-permute-start(f32[8,256]{1,0:T(8,128)S(1)} %add_add_fusion.1), channel_id=1, source_target_pairs={{0,96},{8,104},{16,112},{24,120},{32,64},{40,72},{48,80},{56,88},{... | collective-permute-start | bytes 24584 | tf_op jit(solution)/shard_map/ppermute | solution.py:174
  115.9 0.0 collective-permute-start.22
  115.9 3.2 %collective-permute-start.21 = (f32[8,256]{1,0:T(8,128)S(1)}, f32[8,256]{1,0:T(8,128)S(1)}, u32[]{:S(2)}, u32[]{:S(2)}) collective-permute-start(f32[8,256]{1,0:T(8,128)S(1)} %add_add_fusion.1), channel_id=1, source_target_pairs={{0,64},{8,72},{16,80},{24,88},{32,96},{40,104},{48,112},{56,120},{... | collective-permute-start | bytes 24584 | tf_op jit(solution)/shard_map/ppermute | solution.py:174
  119.2 9.1 %returns.1 = (bf16[1024,1024]{1,0:T(8,128)(2,1)}, bf16[1024,1024]{1,0:T(8,128)(2,1)}) custom-call(s32[6]{0:T(128)} %pad_add_fusion.bits, bf16[1024,1024]{1,0:T(8,128)(2,1)} %k_ref.3, bf16[1024,1024]{1,0:T(8,128)(2,1)} %v_ref.3, f32[1024,1024]{1,0:T(8,128)} %get-tuple-element.33.kn_ref, f32[1024,1024]{1,0:T(8,128)} %get-tuple-element.34.vn_ref, ...), custom_call_target="tpu_custom_call" | custom-call | flops 1000000000 | bytes 16777216 | tf_op jit(solution)/shard_map/returns/pallas_call | solution.py:269
  128.3 0.0 collective-permute-done.23
  128.3 0.0 collective-permute-done.22
  128.3 0.0 collective-permute-done.21
  128.3 0.6 fusion.7
  (26 shorter events, 0.1 us)
Async XLA Ops:
  3.8 56.8 %copy-start.11 = (f32[1024,8]{0,1:T(8,128)S(1)}, f32[1024,8]{0,1:T(8,128)}, u32[]{:S(2)}) copy-start(f32[1024,8]{0,1:T(8,128)} %fusion.1) | copy-start | bytes 98308
  11.0 11.4 %collective-permute-start = (f32[2,2,128,128]{3,2,1,0:T(8,128)}, f32[2,2,128,128]{3,2,1,0:T(8,128)S(1)}, u32[]{:S(2)}, u32[]{:S(2)}) collective-permute-start(f32[2,2,128,128]{3,2,1,0:T(8,128)} %get-tuple-element.24), channel_id=1, source_target_pairs={{0,16},{8,24},{16,0},{24,8},{32,48},{40,56},{48,32},{56,40},{64,80... | collective-permute-start | bytes 786440 | tf_op jit(solution)/shard_map/ppermute | solution.py:174
  15.1 12.9 %collective-permute-start.1 = (f32[2,2,128,128]{3,2,1,0:T(8,128)}, f32[2,2,128,128]{3,2,1,0:T(8,128)S(1)}, u32[]{:S(2)}, u32[]{:S(2)}) collective-permute-start(f32[2,2,128,128]{3,2,1,0:T(8,128)} %get-tuple-element.25), channel_id=1, source_target_pairs={{0,8},{8,0},{16,24},{24,16},{32,40},{40,32},{48,56},{56,48},{64,72... | collective-permute-start | bytes 786440 | tf_op jit(solution)/shard_map/ppermute | solution.py:174
  16.1 11.9 %collective-permute-start.2 = (f32[2,2,128,128]{3,2,1,0:T(8,128)}, f32[2,2,128,128]{3,2,1,0:T(8,128)S(1)}, u32[]{:S(2)}, u32[]{:S(2)}) collective-permute-start(f32[2,2,128,128]{3,2,1,0:T(8,128)} %get-tuple-element.26), channel_id=1, source_target_pairs={{0,24},{8,16},{16,8},{24,0},{32,56},{40,48},{48,40},{56,32},{64,88... | collective-permute-start | bytes 786440 | tf_op jit(solution)/shard_map/ppermute | solution.py:174
  29.0 7.5 %collective-permute-start.6 = (f32[2,2,128,128]{3,2,1,0:T(8,128)S(1)}, f32[2,2,128,128]{3,2,1,0:T(8,128)S(1)}, u32[]{:S(2)}, u32[]{:S(2)}) collective-permute-start(f32[2,2,128,128]{3,2,1,0:T(8,128)S(1)} %add_add_fusion), channel_id=1, source_target_pairs={{0,32},{8,40},{16,48},{24,56},{32,0},{40,8},{48,16},{56,24},{64,96... | collective-permute-start | bytes 786440 | tf_op jit(solution)/shard_map/ppermute | solution.py:174
  30.7 37.5 %collective-permute-start.3 = (f32[8,128,128]{2,1,0:T(8,128)}, f32[8,128,128]{2,1,0:T(8,128)S(1)}, u32[]{:S(2)}, u32[]{:S(2)}) collective-permute-start(f32[8,128,128]{2,1,0:T(8,128)} %get-tuple-element.29), channel_id=1, source_target_pairs={{0,8},{8,0},{16,24},{24,16},{32,40},{40,32},{48,56},{56,48},{64,72... | collective-permute-start | bytes 1572872 | tf_op jit(solution)/shard_map/ppermute | solution.py:174
  36.5 49.6 %copy-start.3 = (f32[2,128,128]{2,1,0:T(8,128)}, f32[2,128,128]{2,1,0:T(8,128)S(1)}, u32[]{:S(2)}) copy-start(f32[2,128,128]{2,1,0:T(8,128)S(1)} %get-tuple-element.39.rest_0_) | copy-start | bytes 393220
  36.5 9.0 %collective-permute-start.10 = (f32[2,128,128]{2,1,0:T(8,128)S(1)}, f32[2,128,128]{2,1,0:T(8,128)S(1)}, u32[]{:S(2)}, u32[]{:S(2)}) collective-permute-start(f32[2,128,128]{2,1,0:T(8,128)S(1)} %get-tuple-element.38), channel_id=1, source_target_pairs={{0,96},{8,104},{16,112},{24,120},{32,64},{40,72},{48,80},{56,88},{... | collective-permute-start | bytes 393224 | tf_op jit(solution)/shard_map/ppermute | solution.py:174
  39.6 20.0 %collective-permute-start.9 = (f32[2,128,128]{2,1,0:T(8,128)S(1)}, f32[2,128,128]{2,1,0:T(8,128)S(1)}, u32[]{:S(2)}, u32[]{:S(2)}) collective-permute-start(f32[2,128,128]{2,1,0:T(8,128)S(1)} %get-tuple-element.39.rest_0_), channel_id=1, source_target_pairs={{0,24},{8,16},{16,8},{24,0},{32,56},{40,48},{48,40},{56,32},{64,88... | collective-permute-start | bytes 393224 | tf_op jit(solution)/shard_map/ppermute | solution.py:174
  43.1 43.1 %collective-permute-start.5 = (f32[8,128,128]{2,1,0:T(8,128)}, f32[8,128,128]{2,1,0:T(8,128)S(1)}, u32[]{:S(2)}, u32[]{:S(2)}) collective-permute-start(f32[8,128,128]{2,1,0:T(8,128)} %get-tuple-element.30), channel_id=1, source_target_pairs={{0,16},{8,24},{16,0},{24,8},{32,48},{40,56},{48,32},{56,40},{64,80... | collective-permute-start | bytes 1572872 | tf_op jit(solution)/shard_map/ppermute | solution.py:174
  43.1 43.1 %collective-permute-start.4 = (f32[8,128,128]{2,1,0:T(8,128)}, f32[8,128,128]{2,1,0:T(8,128)S(1)}, u32[]{:S(2)}, u32[]{:S(2)}) collective-permute-start(f32[8,128,128]{2,1,0:T(8,128)} %get-tuple-element.30), channel_id=1, source_target_pairs={{0,24},{8,16},{16,8},{24,0},{32,56},{40,48},{48,40},{56,32},{64,88... | collective-permute-start | bytes 1572872 | tf_op jit(solution)/shard_map/ppermute | solution.py:174
  45.5 40.6 %copy-start.4 = (f32[2,128,128]{2,1,0:T(8,128)}, f32[2,128,128]{2,1,0:T(8,128)S(1)}, u32[]{:S(2)}) copy-start(f32[2,128,128]{2,1,0:T(8,128)S(1)} %collective-permute-done.10.rest_4_) | copy-start | bytes 393220
  45.6 16.1 %collective-permute-start.8 = (f32[2,128,128]{2,1,0:T(8,128)S(1)}, f32[2,128,128]{2,1,0:T(8,128)S(1)}, u32[]{:S(2)}, u32[]{:S(2)}) collective-permute-start(f32[2,128,128]{2,1,0:T(8,128)S(1)} %get-tuple-element.39.rest_0_), channel_id=1, source_target_pairs={{0,16},{8,24},{16,0},{24,8},{32,48},{40,56},{48,32},{56,40},{64,80... | collective-permute-start | bytes 393224 | tf_op jit(solution)/shard_map/ppermute | solution.py:174
  59.6 26.5 %copy-start.5 = (f32[2,128,128]{2,1,0:T(8,128)}, f32[2,128,128]{2,1,0:T(8,128)S(1)}, u32[]{:S(2)}) copy-start(f32[2,128,128]{2,1,0:T(8,128)S(1)} %collective-permute-done.9.rest_3_) | copy-start | bytes 393220
  59.6 5.1 %collective-permute-start.7 = (f32[2,128,128]{2,1,0:T(8,128)S(1)}, f32[2,128,128]{2,1,0:T(8,128)S(1)}, u32[]{:S(2)}, u32[]{:S(2)}) collective-permute-start(f32[2,128,128]{2,1,0:T(8,128)S(1)} %get-tuple-element.39.rest_0_), channel_id=1, source_target_pairs={{0,8},{8,0},{16,24},{24,16},{32,40},{40,32},{48,56},{56,48},{64,72... | collective-permute-start | bytes 393224 | tf_op jit(solution)/shard_map/ppermute | solution.py:174
  61.6 24.5 %copy-start.6 = (f32[2,128,128]{2,1,0:T(8,128)}, f32[2,128,128]{2,1,0:T(8,128)S(1)}, u32[]{:S(2)}) copy-start(f32[2,128,128]{2,1,0:T(8,128)S(1)} %collective-permute-done.8.rest_2_) | copy-start | bytes 393220
  61.6 24.6 %collective-permute-start.13 = (f32[2,128,128]{2,1,0:T(8,128)S(1)}, f32[2,128,128]{2,1,0:T(8,128)S(1)}, u32[]{:S(2)}, u32[]{:S(2)}) collective-permute-start(f32[2,128,128]{2,1,0:T(8,128)S(1)} %collective-permute-done.10.rest_4_), channel_id=1, source_target_pairs={{0,24},{8,16},{16,8},{24,0},{32,56},{40,48},{48,40},{56,32},{64,88... | collective-permute-start | bytes 393224 | tf_op jit(solution)/shard_map/ppermute | solution.py:174
  64.7 21.4 %copy-start.7 = (f32[2,128,128]{2,1,0:T(8,128)}, f32[2,128,128]{2,1,0:T(8,128)S(1)}, u32[]{:S(2)}) copy-start(f32[2,128,128]{2,1,0:T(8,128)S(1)} %collective-permute-done.7.rest_1_) | copy-start | bytes 393220
  64.7 21.5 %collective-permute-start.12 = (f32[2,128,128]{2,1,0:T(8,128)S(1)}, f32[2,128,128]{2,1,0:T(8,128)S(1)}, u32[]{:S(2)}, u32[]{:S(2)}) collective-permute-start(f32[2,128,128]{2,1,0:T(8,128)S(1)} %collective-permute-done.10.rest_4_), channel_id=1, source_target_pairs={{0,16},{8,24},{16,0},{24,8},{32,48},{40,56},{48,32},{56,40},{64,80... | collective-permute-start | bytes 393224 | tf_op jit(solution)/shard_map/ppermute | solution.py:174
  68.1 18.0 %copy-start = (f32[8,128,128]{2,1,0:T(8,128)}, f32[8,128,128]{2,1,0:T(8,128)S(1)}, u32[]{:S(2)}) copy-start(f32[8,128,128]{2,1,0:T(8,128)S(1)} %collective-permute-done.3.y1_ref) | copy-start | bytes 1572868
  68.1 18.1 %collective-permute-start.11 = (f32[2,128,128]{2,1,0:T(8,128)S(1)}, f32[2,128,128]{2,1,0:T(8,128)S(1)}, u32[]{:S(2)}, u32[]{:S(2)}) collective-permute-start(f32[2,128,128]{2,1,0:T(8,128)S(1)} %collective-permute-done.10.rest_4_), channel_id=1, source_target_pairs={{0,8},{8,0},{16,24},{24,16},{32,40},{40,32},{48,56},{56,48},{64,72... | collective-permute-start | bytes 393224 | tf_op jit(solution)/shard_map/ppermute | solution.py:174
  86.2 0.8 copy-start.1
  86.2 0.9 copy-start.2
  86.2 1.0 copy-start.8
  86.2 1.0 copy-start.9
  86.2 1.0 copy-start.10
  87.3 9.6 %copy-start.12 = (s32[1024]{0:T(1024)S(1)}, s32[1024]{0:T(1024)}, u32[]{:S(2)}) copy-start(s32[1024]{0:T(1024)} %param.12) | copy-start | bytes 12292
  98.7 1.2 collective-permute-start.14
  99.9 4.9 %collective-permute-start.17 = (f32[8,256]{1,0:T(8,128)S(1)}, f32[8,256]{1,0:T(8,128)S(1)}, u32[]{:S(2)}, u32[]{:S(2)}) collective-permute-start(f32[8,256]{1,0:T(8,128)S(1)} %add.52), channel_id=1, source_target_pairs={{0,6},{1,7},{2,4},{3,5},{4,2},{5,3},{6,0},{7,1},{8,14},{9,15},{10,... | collective-permute-start | bytes 24584 | tf_op jit(solution)/shard_map/ppermute | solution.py:174
  102.6 3.7 %collective-permute-start.16 = (f32[8,256]{1,0:T(8,128)S(1)}, f32[8,256]{1,0:T(8,128)S(1)}, u32[]{:S(2)}, u32[]{:S(2)}) collective-permute-start(f32[8,256]{1,0:T(8,128)S(1)} %add.52), channel_id=1, source_target_pairs={{0,2},{1,3},{2,0},{3,1},{4,6},{5,7},{6,4},{7,5},{8,10},{9,11},{10,... | collective-permute-start | bytes 24584 | tf_op jit(solution)/shard_map/ppermute | solution.py:174
  102.9 5.2 %collective-permute-start.15 = (f32[8,256]{1,0:T(8,128)S(1)}, f32[8,256]{1,0:T(8,128)S(1)}, u32[]{:S(2)}, u32[]{:S(2)}) collective-permute-start(f32[8,256]{1,0:T(8,128)S(1)} %add.52), channel_id=1, source_target_pairs={{0,4},{1,5},{2,6},{3,7},{4,0},{5,1},{6,2},{7,3},{8,12},{9,13},{10,... | collective-permute-start | bytes 24584 | tf_op jit(solution)/shard_map/ppermute | solution.py:174
  108.0 4.9 %collective-permute-start.20 = (f32[8,256]{1,0:T(8,128)S(1)}, f32[8,256]{1,0:T(8,128)S(1)}, u32[]{:S(2)}, u32[]{:S(2)}) collective-permute-start(f32[8,256]{1,0:T(8,128)S(1)} %add_add_fusion.2), channel_id=1, source_target_pairs={{0,24},{8,16},{16,8},{24,0},{32,56},{40,48},{48,40},{56,32},{64,88... | collective-permute-start | bytes 24584 | tf_op jit(solution)/shard_map/ppermute | solution.py:174
  108.1 4.9 %collective-permute-start.19 = (f32[8,256]{1,0:T(8,128)S(1)}, f32[8,256]{1,0:T(8,128)S(1)}, u32[]{:S(2)}, u32[]{:S(2)}) collective-permute-start(f32[8,256]{1,0:T(8,128)S(1)} %add_add_fusion.2), channel_id=1, source_target_pairs={{0,8},{8,0},{16,24},{24,16},{32,40},{40,32},{48,56},{56,48},{64,72... | collective-permute-start | bytes 24584 | tf_op jit(solution)/shard_map/ppermute | solution.py:174
  108.7 5.8 %collective-permute-start.18 = (f32[8,256]{1,0:T(8,128)S(1)}, f32[8,256]{1,0:T(8,128)S(1)}, u32[]{:S(2)}, u32[]{:S(2)}) collective-permute-start(f32[8,256]{1,0:T(8,128)S(1)} %add_add_fusion.2), channel_id=1, source_target_pairs={{0,16},{8,24},{16,0},{24,8},{32,48},{40,56},{48,32},{56,40},{64,80... | collective-permute-start | bytes 24584 | tf_op jit(solution)/shard_map/ppermute | solution.py:174
  114.5 13.8 %collective-permute-start.23 = (f32[8,256]{1,0:T(8,128)S(1)}, f32[8,256]{1,0:T(8,128)S(1)}, u32[]{:S(2)}, u32[]{:S(2)}) collective-permute-start(f32[8,256]{1,0:T(8,128)S(1)} %add_add_fusion.1), channel_id=1, source_target_pairs={{0,96},{8,104},{16,112},{24,120},{32,64},{40,72},{48,80},{56,88},{... | collective-permute-start | bytes 24584 | tf_op jit(solution)/shard_map/ppermute | solution.py:174
  115.9 12.4 %collective-permute-start.22 = (f32[8,256]{1,0:T(8,128)S(1)}, f32[8,256]{1,0:T(8,128)S(1)}, u32[]{:S(2)}, u32[]{:S(2)}) collective-permute-start(f32[8,256]{1,0:T(8,128)S(1)} %add_add_fusion.1), channel_id=1, source_target_pairs={{0,32},{8,40},{16,48},{24,56},{32,0},{40,8},{48,16},{56,24},{64,96... | collective-permute-start | bytes 24584 | tf_op jit(solution)/shard_map/ppermute | solution.py:174
  115.9 12.4 %collective-permute-start.21 = (f32[8,256]{1,0:T(8,128)S(1)}, f32[8,256]{1,0:T(8,128)S(1)}, u32[]{:S(2)}, u32[]{:S(2)}) collective-permute-start(f32[8,256]{1,0:T(8,128)S(1)} %add_add_fusion.1), channel_id=1, source_target_pairs={{0,64},{8,72},{16,80},{24,88},{32,96},{40,104},{48,112},{56,120},{... | collective-permute-start | bytes 24584 | tf_op jit(solution)/shard_map/ppermute | solution.py:174

commit v3 on v2

v3 whole, which is shorter than its diff:
```python
import jax
import jax.numpy as jnp
from jax import lax
from jax.experimental import pallas as pl
from jax.experimental.pallas import tpu as pltpu
from jax.sharding import PartitionSpec as P

DH = 128
CHUNK = 256
SCALE = 1.0 / DH
MIB = 2**20

f32 = jnp.float32
bf16 = jnp.bfloat16


def mm(a, b, ca, cb):
    return lax.dot_general(a, b, (((ca,), (cb,)), ((), ())), preferred_element_type=f32)


def place():
    group = lax.axis_index("seq")
    bits = [jnp.bitwise_and(jnp.right_shift(group, l), 1) for l in range(4)]
    return bits, jnp.bitwise_and(group, 3)


def thirds(x):
    one = x.astype(bf16)
    rest = x - one.astype(f32)
    two = rest.astype(bf16)
    return one, two, (rest - two.astype(f32)).astype(bf16)


def one_hot(index_row, size):
    ids = lax.broadcasted_iota(jnp.int32, (size, index_row.shape[1]), 0)
    return jnp.where(ids == index_row, 1.0, 0.0).astype(bf16)


def states_kernel(reach, index_ref, table_ref, q_hbm, k_hbm, v_hbm, g_hbm, w_ref, near1_ref, near2_ref, *rest):
    far_refs, buf, table, sem = rest[:4], rest[4], rest[5], rest[6]
    sources = (q_hbm, k_hbm, v_hbm, g_hbm)
    wide = buf.shape[-1]
    each = wide // DH
    bits, spot = place()

    def copy(j, a):
        cols = pl.ds(pl.multiple_of((spot ^ j) * wide, wide), wide)
        return pltpu.make_async_copy(sources[a].at[:, cols], buf.at[j, a], sem.at[j, a])

    for j in range(4):
        for a in range(4):
            copy(j, a).start()
    table[...] = jnp.zeros_like(table)
    table[0 : table_ref.shape[0], :] = table_ref[...]
    level = lax.broadcasted_iota(jnp.int32, table.shape, 0)
    picked = one_hot(index_ref[...], table.shape[1])
    pieces = thirds(jnp.where(level <= reach[0], table[...], 0.0))
    w = mm(pieces[0], picked, 1, 0) + mm(pieces[1], picked, 1, 0) + mm(pieces[2], picked, 1, 0)
    w_ref[...] = w
    for j in range(4):
        for a in range(4):
            copy(j, a).wait()
        for i in range(each):
            c = slice(i * DH, (i + 1) * DH)
            head = (spot ^ j) * each + i
            own = mm(buf[j, 2, :, c].T, buf[j, 1, :, c], 1, 0)
            gt = buf[j, 3, :, c].T.astype(f32)
            parts = [(gt * w[l : l + 1, :]).astype(bf16) for l in range(1, 5)]
            grads = mm(jnp.concatenate(parts, 0), buf[j, 0, :, c], 1, 0)
            xs = [jnp.where(bits[l] > 0, grads[l * DH : (l + 1) * DH], own) for l in range(4)]
            near1_ref[head] = xs[0]
            near2_ref[head] = xs[1]
            far_refs[j][0, i] = xs[2]
            far_refs[j][1, i] = xs[3]


def causal_mask(flip_sides):
    rows = lax.broadcasted_iota(jnp.int32, (CHUNK, CHUNK), 0)
    cols = lax.broadcasted_iota(jnp.int32, (CHUNK, CHUNK), 1)
    return rows <= cols if flip_sides else rows >= cols


def query_kernel(order, q_ref, k_ref, v_ref, g_ref, w_ref, out_ref, lam_ref):
    @pl.when(pl.program_id(0) == 0)
    def _():
        lam_ref[...] = jnp.zeros_like(lam_ref)

    causal = causal_mask(False)
    state = jnp.zeros((DH, DH), f32)
    count = q_ref.shape[0] // CHUNK
    for i in range(count):
        at = pl.ds(i * CHUNK, CHUNK)
        k, v, g = k_ref[at, :], v_ref[at, :], g_ref[at, :]
        near = jnp.where(causal, mm(g, v, 1, 1), 0.0).astype(bf16)
        u = mm(near, k, 1, 0)
        if i > 0:
            u = u + mm(g, state.astype(bf16), 1, 0)
        lam_ref[at, :] += q_ref[at, :].astype(f32) * u
        out_ref[at, :] = (SCALE * w_ref[at, 0:1]) * u
        if i < count - 1:
            state = state + mm(v, k, 0, 0)


def key_value_kernel(order, q_ref, k_ref, v_ref, g_ref, w_ref, key_ref, value_ref):
    causal = causal_mask(True)
    state = jnp.zeros((DH, DH), f32)
    count = q_ref.shape[0] // CHUNK
    for i in reversed(range(count)):
        at = pl.ds(i * CHUNK, CHUNK)
        k, v, g = k_ref[at, :], v_ref[at, :], g_ref[at, :]
        q = (q_ref[at, :].astype(f32) * w_ref[at, 0:1]).astype(bf16)
        near_key = jnp.where(causal, mm(v, g, 1, 1), 0.0).astype(bf16)
        near_value = jnp.where(causal, mm(k, q, 1, 1), 0.0).astype(bf16)
        key = mm(near_key, q, 1, 0)
        value = mm(near_value, g, 1, 0)
        if i < count - 1:
            held = state.astype(bf16)
            key = key + mm(v, held, 1, 0)
            value = value + mm(k, held, 1, 1)
        key_ref[at, :] = SCALE * key
        value_ref[at, :] = SCALE * value
        if i > 0:
            state = state + mm(g, q, 0, 0)


def level_states(keep, y1_ref, y2a_ref, y2b_ref, y3_refs, y4_refs, bits, head, j, i):
    ys = (y1_ref[head], y2a_ref[head] + y2b_ref[head], y3_refs[j][i], y4_refs[j][i])
    return [jnp.where(bits[l] == keep, ys[l], 0.0) for l in range(4)]


def reads_kernel(reach, q_ref, g_ref, w_ref, qn_ref, lam0_ref, index_ref, y1_ref, y2a_ref, y2b_ref, *rest):
    y3_refs, y4_refs, (out_hbm, table_ref, st, out_buf, sem) = rest[:4], rest[4:8], rest[8:]
    length = q_ref.shape[0]
    heads = y1_ref.shape[0]
    each = heads // 4
    tile = CHUNK
    bits, spot = place()
    for j in range(4):
        for i in range(each):
            head = (spot ^ j) * each + i
            parts = level_states(1, y1_ref, y2a_ref, y2b_ref, y3_refs, y4_refs, bits, head, j, i)
            st[head] = jnp.concatenate(parts, 1).astype(bf16)
    lane = lax.broadcasted_iota(jnp.int32, (1, DH), 1)
    table = None
    copies = []
    for t in range(length // tile):
        at = pl.ds(t * tile, tile)
        w = w_ref[at, :]
        wide = [jnp.broadcast_to(w[:, l : l + 1], (tile, DH)) for l in range(1, 5)]
        acc = [None] * 4
        for h in range(heads):
            c = slice(h * DH, (h + 1) * DH)
            reads = mm(g_ref[at, c], st[h], 1, 0)
            q = q_ref[at, c].astype(f32)
            total = None
            for l in range(4):
                read = reads[:, l * DH : (l + 1) * DH]
                product = q * read
                acc[l] = product if acc[l] is None else acc[l] + product
                term = wide[l] * read
                total = term if total is None else total + term
            out_buf[at, c] = (qn_ref[at, c] + SCALE * total).astype(bf16)
        copies.append(pltpu.make_async_copy(out_buf.at[at, :], out_hbm.at[at, :], sem.at[t]))
        copies[-1].start()
        lam = jnp.where(lane == 0, jnp.sum(lam0_ref[at, :], 1, keepdims=True), 0.0)
        for l in range(4):
            here = (lane == l + 1) & (reach[0] > l)
            lam = jnp.where(here, jnp.sum(acc[l], 1, keepdims=True), lam)
        lam = (SCALE * lam).T[:8]
        picked = one_hot(index_ref[:, at], table_ref.shape[1])
        for piece in thirds(lam):
            part = mm(piece, picked, 1, 1)
            table = part if table is None else table + part
    table_ref[...] = table
    for copy in copies:
        copy.wait()


def returns_kernel(start, order, k_ref, v_ref, kn_ref, vn_ref, y1_ref, y2a_ref, y2b_ref, *rest):
    y3_refs, y4_refs, rest = rest[:4], rest[4:8], rest[8:]
    key_hbm, value_hbm, key_buf, value_buf, st, sem = rest[-6:]
    heads = y1_ref.shape[0]
    each = heads // 4
    count = key_buf.shape[1] // DH
    near_start = start % (kn_ref.shape[1] // DH)
    bits, spot = place()
    for j in range(4):
        for i in range(each):
            head = (spot ^ j) * each + i

            @pl.when((head >= start) & (head < start + count))
            def _():
                parts = level_states(0, y1_ref, y2a_ref, y2b_ref, y3_refs, y4_refs, bits, head, j, i)
                st[head] = (parts[0] + parts[1] + parts[2] + parts[3]).astype(bf16)

    for i in range(count):
        head = start + i
        c = slice(head * DH, (head + 1) * DH)
        n = slice((near_start + i) * DH, (near_start + i + 1) * DH)
        o = slice(i * DH, (i + 1) * DH)
        key_buf[:, o] = (kn_ref[:, n] + SCALE * mm(v_ref[:, c], st[head], 1, 0)).astype(bf16)
        value_buf[:, o] = (vn_ref[:, n] + SCALE * mm(k_ref[:, c], st[head], 1, 1)).astype(bf16)
    cols = pl.ds(start * DH, count * DH)
    key_copy = pltpu.make_async_copy(key_buf, key_hbm.at[:, cols], sem.at[0])
    value_copy = pltpu.make_async_copy(value_buf, value_hbm.at[:, cols], sem.at[1])
    key_copy.start()
    value_copy.start()
    key_copy.wait()
    value_copy.wait()


def flip(x, axis, mask):
    return lax.ppermute(x, axis, [(i, i ^ mask) for i in range(lax.axis_size(axis))])


def tie(x, *deps):
    return lax.optimization_barrier((x, *deps))[0]


def local(queries, keys, values, out_grad, level_table, table_index, reach):
    length = queries.shape[0]
    heads = queries.shape[1] // DH
    each = heads // 4
    span = lax.axis_size("seq")
    names = level_table.shape[1]
    index_row = table_index.reshape(1, length)
    sds = jax.ShapeDtypeStruct
    whole = pl.BlockSpec(memory_space=pltpu.VMEM)
    scalar = pl.BlockSpec(memory_space=pltpu.SMEM)
    anywhere = pl.BlockSpec(memory_space=pl.ANY)
    limit = lambda mib: pltpu.CompilerParams(vmem_limit_bytes=mib * MIB)
    cost = lambda us: pl.CostEstimate(flops=int(us * 10**9), bytes_accessed=MIB, transcendentals=0)

    w_rows, near, near2, *far = pl.pallas_call(
        states_kernel,
        in_specs=[scalar, whole, whole] + [anywhere] * 4,
        out_specs=[whole] * 7,
        out_shape=[sds((8, length), f32)]
        + [sds((heads, DH, DH), f32)] * 2
        + [sds((2, each, DH, DH), f32)] * 4,
        scratch_shapes=[
            pltpu.VMEM((4, 4, length, each * DH), bf16),
            pltpu.VMEM((8, names), f32),
            pltpu.SemaphoreType.DMA((4, 4)),
        ],
        compiler_params=limit(60),
        name="states",
    )(reach, index_row, level_table, queries, keys, values, out_grad)
    w_cols = w_rows.T

    token_spec = lambda start: pl.BlockSpec((length, DH), lambda h: (0, h + start))
    fixed = lambda shape: pl.BlockSpec(shape, lambda h: (0,) * len(shape))

    def near_part(kernel, order, start, count, out_shape, out_specs, name):
        return pl.pallas_call(
            kernel,
            grid=(count,),
            in_specs=[scalar] + [token_spec(start)] * 4 + [fixed((length, 8))],
            out_specs=out_specs,
            out_shape=out_shape,
            compiler_params=pltpu.CompilerParams(
                dimension_semantics=("arbitrary",), vmem_limit_bytes=20 * MIB
            ),
            cost_estimate=cost(5),
            name=name,
        )(order, queries, keys, values, out_grad, w_cols)

    def key_value_part(order, start, count, name):
        shape = sds((length, count * DH), f32)
        return near_part(
            key_value_kernel, order, start, count, [shape] * 2, [token_spec(0)] * 2, name
        )

    got = [flip(far[m], "seq", m) for m in (1, 3, 2)]
    qn, lam0 = near_part(
        query_kernel,
        tie(reach, *far),
        0,
        heads,
        [sds((length, heads * DH), f32), sds((length, DH), f32)],
        [token_spec(0), fixed((length, DH))],
        "query",
    )
    got = lax.optimization_barrier((*got, qn))[:3]
    rows = (far[0] + got[2]) + (got[0] + got[1])
    other = flip(rows, "seq", 4)
    near, near2 = lax.optimization_barrier((near, near2, rows))[:2]
    y1 = flip(near, "seq", 1)
    y2a = flip(near2, "seq", 3)
    y2b = flip(near2, "seq", 2)
    half = heads // 2
    kn_a, vn_a = key_value_part(tie(reach, rows), 0, half, "key_value_a")
    other = tie(other, kn_a)
    y3 = other[0]
    far4 = rows[1] + other[1]
    y4 = flip(far4, "seq", 12)
    y3s = [y3] + [flip(y3, "seq", m) for m in (1, 2, 3)]
    kn_b, vn_b = key_value_part(tie(reach, far4), half, half, "key_value_b")
    y4 = tie(y4, kn_b)
    y4s = [y4] + [flip(y4, "seq", m) for m in (1, 2, 3)]
    arrived = (y1, y2a, y2b, *y3s, *y4s)

    query_grad, total = pl.pallas_call(
        reads_kernel,
        in_specs=[scalar] + [whole] * 17,
        out_specs=[anywhere, whole],
        out_shape=[sds((length, heads * DH), bf16), sds((8, names), f32)],
        scratch_shapes=[
            pltpu.VMEM((heads, DH, 4 * DH), bf16),
            pltpu.VMEM((length, heads * DH), bf16),
            pltpu.SemaphoreType.DMA((length // CHUNK,)),
        ],
        compiler_params=limit(30),
        cost_estimate=cost(6),
        name="reads",
    )(reach, queries, out_grad, w_cols, qn, lam0, index_row, *arrived)

    def returns(order, start, count, held):
        kn, vn = (kn_a, vn_a) if start < half else (kn_b, vn_b)
        shape = sds((length, heads * DH), bf16)

        def kernel(*refs):
            returns_kernel(start, *refs)

        return pl.pallas_call(
            kernel,
            in_specs=[scalar] + [whole] * 15 + [anywhere] * len(held),
            out_specs=[anywhere] * 2,
            out_shape=[shape] * 2,
            scratch_shapes=[
                pltpu.VMEM((length, count * DH), bf16),
                pltpu.VMEM((length, count * DH), bf16),
                pltpu.VMEM((heads, DH, DH), bf16),
                pltpu.SemaphoreType.DMA((2,)),
            ],
            input_output_aliases={16: 0, 17: 1} if held else {},
            compiler_params=limit(20),
            cost_estimate=cost(1),
            name="returns",
        )(order, keys, values, kn, vn, *arrived, *held)

    got = [flip(total, "head", 1)]
    held = returns(tie(reach, total), 0, each, ())
    total = total + tie(got[0], *held)
    for stage, (axis, unit) in enumerate((("head", 2), ("seq", 1), ("seq", 4))):
        got = [flip(total, axis, m * unit) for m in (1, 2, 3)]
        held = returns(tie(reach, total), (stage + 1) * each, each, tuple(held))
        one, two, three = lax.optimization_barrier((*got, *held))[:3]
        total = (total + two) + (one + three)
    table_grad = total[: level_table.shape[0]] / (length * span)
    return query_grad, held[0], held[1], table_grad


def solution(mesh):
    return jax.shard_map(
        local,
        mesh=mesh,
        in_specs=(
            P("seq", "head"),
            P("seq", "head"),
            P("seq", "head"),
            P("seq", "head"),
            P(),
            P("seq"),
            P("seq"),
        ),
        out_specs=(P("seq", "head"), P("seq", "head"), P("seq", "head"), P()),
        check_vma=False,
    )
```

time: 130 us -> 111 us (0.85)
  waiting for transfers between devices: 36 us -> 24.9 us
  starting transfers between devices: 41.4 us -> 35.6 us
  matrix products: 3.69 us -> 0 us
  local copies, waits for them, and re-layouts: 2.08 us -> 5.76 us
  other arithmetic: 2.26 us -> 0.7 us
    ppermute x24, waiting for transfers between devices: 36 us -> 24.9 us  [flip(): lax.ppermute(x, axis, [(i, i ^ mask) for i in range(lax.axis_size(axis))])]
    ppermute x24, starting transfers between devices: 41.4 us -> 35.6 us  [flip(): lax.ppermute(x, axis, [(i, i ^ mask) for i in range(lax.axis_size(axis))])]
    unnamed x26 -> x22, local copies, waits for them, and re-layouts: 1.08 us -> 4.81 us
    dot_general x2 -> x0, matrix products: 3.69 us -> none  [the longest x1 1.94 us: local(): weights = jnp.dot(picker, table.T, precision=precise)]
    pallas_call x4 -> x9, Pallas kernels: 42 us -> 41.9 us  [the longest x3 21.5 us: near_part(): pl.pallas_call(kernel, grid=(count,), in_specs=[scalar] + [token_spec(sta...]
  transfers between devices with their start and end apart: 24 -> 24, of which waited for: 10 -> 7; matrix products, arithmetic and copies ran while one was open for 1% -> 1% of each run, Pallas kernels for 20% -> 25%
where the time goes in v3:
time: 111 us; the launch traced here: 110 us
  Pallas kernels  41.9 us (38%)
  starting transfers between devices  35.6 us (32%)
  waiting for transfers between devices  24.9 us (22%)
  local copies, waits for them, and re-layouts  5.76 us (5%)
  between operations  1.58 us (1%)
    ppermute x24, starting transfers between devices, flip(): lax.ppermute(x, axis, [(i, i ^ mask) for i in range(lax.axis_size(axis))])  35.6 us
    ppermute x24, waiting for transfers between devices, flip(): lax.ppermute(x, axis, [(i, i ^ mask) for i in range(lax.axis_size(axis))])  24.9 us
    pallas_call x3, Pallas kernels, near_part(): pl.pallas_call(kernel, grid=(count,), in_specs=[scalar] + [token_spec(sta...  21.5 us
    pallas_call x1, Pallas kernels, local(): pl.pallas_call(states_kernel, in_specs=[scalar, whole, whole] + [anywhere...  7.27 us
    pallas_call x1, Pallas kernels, local(): pl.pallas_call(reads_kernel, in_specs=[scalar] + [whole] * 17, out_specs=...  6.9 us
    pallas_call x4, Pallas kernels, returns(): pl.pallas_call(kernel, in_specs=[scalar] + [whole] * 15 + [anywhere] * le...  6.2 us
    unnamed x22, local copies, waits for them, and re-layouts  4.81 us
  transfers between devices with their start and end apart: 24, of which 7 were waited for; matrix products, arithmetic and copies ran while one was open for 1% of the time, Pallas kernels for 25%

profile of v3, /device:TPU:0, one launch (start us, length us, event | category | flops | bytes accessed | tf_op | source)
XLA Modules:
  0.0 110.4 jit_solution(16209901566205105674)
XLA Ops:
  1.3 7.3 %states.1 = (f32[8,1024]{1,0:T(8,128)}, f32[8,128,128]{2,1,0:T(8,128)}, f32[8,128,128]{2,1,0:T(8,128)}, f32[2,2,128,128]{3,2,1,0:T(8,128)}, f32[2,2,128,128]{3,2...) custom-call(s32[1]{0:T(128)S(6)} %copy.24.reach.order.refs_0_, s32[1,1024]{1,0:T(1,128)} %bitcast.10, ...), custom_call_target="tpu_custom_call" | custom-call | tf_op jit(solution)/shard_map/states/pallas_call | solution.py:234
  8.6 2.1 %collective-permute-start = (f32[2,2,128,128]{3,2,1,0:T(8,128)}, f32[2,2,128,128]{3,2,1,0:T(8,128)S(1)}, u32[]{:S(2)}, u32[]{:S(2)}) collective-permute-start(f32[2,2,128,128]{3,2,1,0:T(8,128)} %get-tuple-element.53), channel_id=1, source_target_pairs={{0,8},{8,0},{16,24},{24,16},{32,40},{40,32},{48,56},{56,48},{64,72... | collective-permute-start | bytes 786440 | tf_op jit(solution)/shard_map/ppermute | solution.py:213
  10.7 3.6 %collective-permute-start.2 = (f32[2,2,128,128]{3,2,1,0:T(8,128)}, f32[2,2,128,128]{3,2,1,0:T(8,128)S(1)}, u32[]{:S(2)}, u32[]{:S(2)}) collective-permute-start(f32[2,2,128,128]{3,2,1,0:T(8,128)} %get-tuple-element.54), channel_id=1, source_target_pairs={{0,16},{8,24},{16,0},{24,8},{32,48},{40,56},{48,32},{56,40},{64,80... | collective-permute-start | bytes 786440 | tf_op jit(solution)/shard_map/ppermute | solution.py:213
  14.3 0.0 collective-permute-start.1
  14.3 1.0 copy.17
  15.2 0.0 copy-start.1
  15.3 1.6 %copy-done.1 = bf16[1024,1024]{1,0:T(8,128)(2,1)S(1)} copy-done((bf16[1024,1024]{1,0:T(8,128)(2,1)S(1)}, bf16[1024,1024]{1,0:T(8,128)(2,1)}, u32[]{:S(2)}) %copy-start.1) | copy-done | bytes 2097176
  16.8 1.6 %copy-done.3 = bf16[1024,1024]{1,0:T(8,128)(2,1)S(1)} copy-done((bf16[1024,1024]{1,0:T(8,128)(2,1)S(1)}, bf16[1024,1024]{1,0:T(8,128)(2,1)}, u32[]{:S(2)}) %copy-start.3) | copy-done | bytes 2097176
  18.4 1.6 %copy-done.5 = bf16[1024,1024]{1,0:T(8,128)(2,1)S(1)} copy-done((bf16[1024,1024]{1,0:T(8,128)(2,1)S(1)}, bf16[1024,1024]{1,0:T(8,128)(2,1)}, u32[]{:S(2)}) %copy-start.5) | copy-done | bytes 2097176
  20.0 9.0 %query.1 = (f32[1024,1024]{1,0:T(8,128)S(1)}, f32[1024,128]{1,0:T(8,128)S(1)}) custom-call(s32[1]{0:T(128)S(6)} %copy.24.reach.order.refs_0_, bf16[1024,1024]{1,0:T(8,128)(2,1)S(1)} %copy-done.3, bf16[1024,1024]{1,0:T(8,128)(2,1)S(1)} %copy-done, bf16[1024,1024]{1,0:T(8,128)(2,1)S(1)} %copy-done.1, bf16[1024,1024]{1,0:T(8,128)(2,1)S(1)} %copy-done.5, ...), custom_call_target="tpu_custom_call" | custom-call | flops 5000000000 | bytes 1048576 | tf_op jit(solution)/shard_map/query/pallas_call | solution.py:255
  29.1 0.0 collective-permute-done
  29.1 0.0 collective-permute-done.2
  29.1 0.0 collective-permute-done.1
  29.1 0.1 add_add_fusion
  29.2 0.0 copy-start.10
  29.2 0.0 copy-start.9
  29.2 1.6 %collective-permute-start.6 = (f32[2,2,128,128]{3,2,1,0:T(8,128)S(1)}, f32[2,2,128,128]{3,2,1,0:T(8,128)S(1)}, u32[]{:S(2)}, u32[]{:S(2)}) collective-permute-start(f32[2,2,128,128]{3,2,1,0:T(8,128)S(1)} %add_add_fusion), channel_id=1, source_target_pairs={{0,32},{8,40},{16,48},{24,56},{32,0},{40,8},{48,16},{56,24},{64,96... | collective-permute-start | bytes 786440 | tf_op jit(solution)/shard_map/ppermute | solution.py:213
  30.8 6.3 %key_value_a.1 = (f32[1024,512]{1,0:T(8,128)S(1)}, f32[1024,512]{1,0:T(8,128)S(1)}) custom-call(s32[1]{0:T(128)S(6)} %copy.24.reach.order.refs_0_, bf16[1024,1024]{1,0:T(8,128)(2,1)S(1)} %copy-done.3, bf16[1024,1024]{1,0:T(8,128)(2,1)S(1)} %copy-done, bf16[1024,1024]{1,0:T(8,128)(2,1)S(1)} %copy-done.1, bf16[1024,1024]{1,0:T(8,128)(2,1)S(1)} %copy-done.5, ...), custom_call_target="tpu_custom_call" | custom-call | flops 5000000000 | bytes 1048576 | tf_op jit(solution)/shard_map/key_value_a/pallas_call | solution.py:255
  37.1 0.0 collective-permute-done.6
  37.1 2.7 %collective-permute-start.10 = (f32[2,128,128]{2,1,0:T(8,128)S(1)}, f32[2,128,128]{2,1,0:T(8,128)S(1)}, u32[]{:S(2)}, u32[]{:S(2)}) collective-permute-start(f32[2,128,128]{2,1,0:T(8,128)S(1)} %get-tuple-element.98), channel_id=1, source_target_pairs={{0,96},{8,104},{16,112},{24,120},{32,64},{40,72},{48,80},{56,88},{... | collective-permute-start | bytes 393224 | tf_op jit(solution)/shard_map/ppermute | solution.py:213
  39.9 3.0 %collective-permute-start.9 = (f32[2,128,128]{2,1,0:T(8,128)S(1)}, f32[2,128,128]{2,1,0:T(8,128)S(1)}, u32[]{:S(2)}, u32[]{:S(2)}) collective-permute-start(f32[2,128,128]{2,1,0:T(8,128)S(1)} %get-tuple-element.99.rest_0_.refs_8_), channel_id=1, source_target_pairs={{0,24},{8,16},{16,8},{24,0},{32,56},{40,48},{48,40},{56,32},{64,88... | collective-permute-start | bytes 393224 | tf_op jit(solution)/shard_map/ppermute | solution.py:213
  42.8 0.1 collective-permute-start.3
  42.9 1.7 %collective-permute-start.5 = (f32[8,128,128]{2,1,0:T(8,128)S(1)}, f32[8,128,128]{2,1,0:T(8,128)S(1)}, u32[]{:S(2)}, u32[]{:S(2)}) collective-permute-start(f32[8,128,128]{2,1,0:T(8,128)S(1)} %copy-done.9), channel_id=1, source_target_pairs={{0,16},{8,24},{16,0},{24,8},{32,48},{40,56},{48,32},{56,40},{64,80... | collective-permute-start | bytes 1572872 | tf_op jit(solution)/shard_map/ppermute | solution.py:213
  44.7 3.0 %collective-permute-start.4 = (f32[8,128,128]{2,1,0:T(8,128)S(1)}, f32[8,128,128]{2,1,0:T(8,128)S(1)}, u32[]{:S(2)}, u32[]{:S(2)}) collective-permute-start(f32[8,128,128]{2,1,0:T(8,128)S(1)} %copy-done.9), channel_id=1, source_target_pairs={{0,24},{8,16},{16,8},{24,0},{32,56},{40,48},{48,40},{56,32},{64,88... | collective-permute-start | bytes 1572872 | tf_op jit(solution)/shard_map/ppermute | solution.py:213
  47.6 0.0 collective-permute-done.10.rest_4_.refs_12_
  47.6 0.0 collective-permute-start.8
  47.6 0.0 collective-permute-done.9.rest_3_.refs_11_
  47.6 1.1 %collective-permute-start.7 = (f32[2,128,128]{2,1,0:T(8,128)S(1)}, f32[2,128,128]{2,1,0:T(8,128)S(1)}, u32[]{:S(2)}, u32[]{:S(2)}) collective-permute-start(f32[2,128,128]{2,1,0:T(8,128)S(1)} %get-tuple-element.99.rest_0_.refs_8_), channel_id=1, source_target_pairs={{0,8},{8,0},{16,24},{24,16},{32,40},{40,32},{48,56},{56,48},{64,72... | collective-permute-start | bytes 393224 | tf_op jit(solution)/shard_map/ppermute | solution.py:213
  48.8 6.3 %key_value_b.1 = (f32[1024,512]{1,0:T(8,128)S(1)}, f32[1024,512]{1,0:T(8,128)S(1)}) custom-call(s32[1]{0:T(128)S(6)} %copy.24.reach.order.refs_0_, bf16[1024,1024]{1,0:T(8,128)(2,1)S(1)} %copy-done.3, bf16[1024,1024]{1,0:T(8,128)(2,1)S(1)} %copy-done, bf16[1024,1024]{1,0:T(8,128)(2,1)S(1)} %copy-done.1, bf16[1024,1024]{1,0:T(8,128)(2,1)S(1)} %copy-done.5, ...), custom_call_target="tpu_custom_call" | custom-call | flops 5000000000 | bytes 1048576 | tf_op jit(solution)/shard_map/key_value_b/pallas_call | solution.py:255
  55.0 15.0 %collective-permute-done.8.rest_2_.refs_10_ = f32[2,128,128]{2,1,0:T(8,128)S(1)} collective-permute-done((f32[2,128,128]{2,1,0:T(8,128)S(1)}, f32[2,128,128]{2,1,0:T(8,128)S(1)}, u32[]{:S(2)}, u32[]{:S(2)}) %collective-permute-start.8) | collective-permute-done | bytes 131104 | tf_op jit(solution)/shard_map/ppermute | solution.py:213
  70.0 2.9 %collective-permute-start.13 = (f32[2,128,128]{2,1,0:T(8,128)S(1)}, f32[2,128,128]{2,1,0:T(8,128)S(1)}, u32[]{:S(2)}, u32[]{:S(2)}) collective-permute-start(f32[2,128,128]{2,1,0:T(8,128)S(1)} %collective-permute-done.10.rest_4_.refs_12_), channel_id=1, source_target_pairs={{0,24},{8,16},{16,8},{24,0},{32,56},{40,48},{48,40},{56,32},{64,88... | collective-permute-start | bytes 393224 | tf_op jit(solution)/shard_map/ppermute | solution.py:213
  72.9 0.0 collective-permute-done.7.rest_1_.refs_9_
  73.0 0.0 collective-permute-start.12
  73.0 0.0 collective-permute-done.3.y1_ref.refs_5_
  73.0 1.1 %collective-permute-start.11 = (f32[2,128,128]{2,1,0:T(8,128)S(1)}, f32[2,128,128]{2,1,0:T(8,128)S(1)}, u32[]{:S(2)}, u32[]{:S(2)}) collective-permute-start(f32[2,128,128]{2,1,0:T(8,128)S(1)} %collective-permute-done.10.rest_4_.refs_12_), channel_id=1, source_target_pairs={{0,8},{8,0},{16,24},{24,16},{32,40},{40,32},{48,56},{56,48},{64,72... | collective-permute-start | bytes 393224 | tf_op jit(solution)/shard_map/ppermute | solution.py:213
  74.1 0.0 collective-permute-done.5.y2b_ref.refs_7_
  74.1 0.0 collective-permute-done.4.y2a_ref.refs_6_
  74.1 2.8 %collective-permute-done.13.rest_7_.refs_15_ = f32[2,128,128]{2,1,0:T(8,128)S(1)} collective-permute-done((f32[2,128,128]{2,1,0:T(8,128)S(1)}, f32[2,128,128]{2,1,0:T(8,128)S(1)}, u32[]{:S(2)}, u32[]{:S(2)}) %collective-permute-start.13) | collective-permute-done | bytes 131104 | tf_op jit(solution)/shard_map/ppermute | solution.py:213
  76.9 2.6 %collective-permute-done.12.rest_6_.refs_14_ = f32[2,128,128]{2,1,0:T(8,128)S(1)} collective-permute-done((f32[2,128,128]{2,1,0:T(8,128)S(1)}, f32[2,128,128]{2,1,0:T(8,128)S(1)}, u32[]{:S(2)}, u32[]{:S(2)}) %collective-permute-start.12) | collective-permute-done | bytes 131104 | tf_op jit(solution)/shard_map/ppermute | solution.py:213
  79.4 0.0 collective-permute-done.11.rest_5_.refs_13_
  79.4 0.0 copy-start.2
  79.5 6.9 %reads.1 = (bf16[1024,1024]{1,0:T(8,128)(2,1)}, f32[8,256]{1,0:T(8,128)S(1)}) custom-call(s32[1]{0:T(128)S(6)} %copy.24.reach.order.refs_0_, bf16[1024,1024]{1,0:T(8,128)(2,1)S(1)} %copy-done.4, bf16[1024,1024]{1,0:T(8,128)(2,1)S(1)} %copy-done.6, f32[1024,8]{1,0:T(8,128)S(1)} %bitcast.9, f32[1024,1024]{1,0:T(8,128)S(1)} %get-tuple-element.57.qn_ref, ...), custom_call_target="tpu_custom_call" | custom-call | flops 6000000000 | bytes 1048576 | tf_op jit(solution)/shard_map/reads/pallas_call | solution.py:303
  86.4 0.1 collective-permute-start.14
  86.5 1.6 %returns.4 = (bf16[1024,1024]{1,0:T(8,128)(2,1)}, bf16[1024,1024]{1,0:T(8,128)(2,1)}) custom-call(s32[1]{0:T(128)S(6)} %copy.24.reach.order.refs_0_, bf16[1024,1024]{1,0:T(8,128)(2,1)S(1)} %copy-done, bf16[1024,1024]{1,0:T(8,128)(2,1)S(1)} %copy-done.2, f32[1024,512]{1,0:T(8,128)S(1)} %get-tuple-element.67.refs_3_, ...), custom_call_target="tpu_custom_call" | custom-call | flops 1000000000 | bytes 1048576 | tf_op jit(solution)/shard_map/returns/pallas_call | solution.py:325
  88.1 0.0 collective-permute-done.14
  88.1 2.8 %collective-permute-start.17 = (f32[8,256]{1,0:T(8,128)S(1)}, f32[8,256]{1,0:T(8,128)S(1)}, u32[]{:S(2)}, u32[]{:S(2)}) collective-permute-start(f32[8,256]{1,0:T(8,128)S(1)} %add.50), channel_id=1, source_target_pairs={{0,6},{1,7},{2,4},{3,5},{4,2},{5,3},{6,0},{7,1},{8,14},{9,15},{10,... | collective-permute-start | bytes 24584 | tf_op jit(solution)/shard_map/ppermute | solution.py:213
  91.0 0.8 collective-permute-start.16
  91.8 0.5 collective-permute-start.15
  92.3 1.6 %returns.5 = (bf16[1024,1024]{1,0:T(8,128)(2,1)}, bf16[1024,1024]{1,0:T(8,128)(2,1)}) custom-call(s32[1]{0:T(128)S(6)} %copy.24.reach.order.refs_0_, bf16[1024,1024]{1,0:T(8,128)(2,1)S(1)} %copy-done, bf16[1024,1024]{1,0:T(8,128)(2,1)S(1)} %copy-done.2, f32[1024,512]{1,0:T(8,128)S(1)} %get-tuple-element.67.refs_3_, ...), custom_call_target="tpu_custom_call", output_to_operand_aliasing={{0}: (16, {}), {1}: (17, {})} | custom-call | flops 1000000000 | bytes 1048576 | tf_op jit(solution)/shard_map/returns/pallas_call | solution.py:325
  93.9 0.0 collective-permute-done.17
  93.9 2.2 %collective-permute-done.16 = f32[8,256]{1,0:T(8,128)S(1)} collective-permute-done((f32[8,256]{1,0:T(8,128)S(1)}, f32[8,256]{1,0:T(8,128)S(1)}, u32[]{:S(2)}, u32[]{:S(2)}) %collective-permute-start.16) | collective-permute-done | bytes 8224 | tf_op jit(solution)/shard_map/ppermute | solution.py:213
  96.1 0.0 collective-permute-done.15
  96.1 2.0 %collective-permute-start.20 = (f32[8,256]{1,0:T(8,128)S(1)}, f32[8,256]{1,0:T(8,128)S(1)}, u32[]{:S(2)}, u32[]{:S(2)}) collective-permute-start(f32[8,256]{1,0:T(8,128)S(1)} %add_add_fusion.2), channel_id=1, source_target_pairs={{0,24},{8,16},{16,8},{24,0},{32,56},{40,48},{48,40},{56,32},{64,88... | collective-permute-start | bytes 24584 | tf_op jit(solution)/shard_map/ppermute | solution.py:213
  98.2 0.2 collective-permute-start.19
  98.3 2.0 %collective-permute-start.18 = (f32[8,256]{1,0:T(8,128)S(1)}, f32[8,256]{1,0:T(8,128)S(1)}, u32[]{:S(2)}, u32[]{:S(2)}) collective-permute-start(f32[8,256]{1,0:T(8,128)S(1)} %add_add_fusion.2), channel_id=1, source_target_pairs={{0,8},{8,0},{16,24},{24,16},{32,40},{40,32},{48,56},{56,48},{64,72... | collective-permute-start | bytes 24584 | tf_op jit(solution)/shard_map/ppermute | solution.py:213
  100.3 1.5 %returns.6 = (bf16[1024,1024]{1,0:T(8,128)(2,1)}, bf16[1024,1024]{1,0:T(8,128)(2,1)}) custom-call(s32[1]{0:T(128)S(6)} %copy.24.reach.order.refs_0_, bf16[1024,1024]{1,0:T(8,128)(2,1)S(1)} %copy-done, bf16[1024,1024]{1,0:T(8,128)(2,1)S(1)} %copy-done.2, f32[1024,512]{1,0:T(8,128)S(1)} %get-tuple-element.70.refs_3_, ...), custom_call_target="tpu_custom_call", output_to_operand_aliasing={{0}: (16, {}), {1}: (17, {})} | custom-call | flops 1000000000 | bytes 1048576 | tf_op jit(solution)/shard_map/returns/pallas_call | solution.py:325
  101.8 1.5 %collective-permute-done.19 = f32[8,256]{1,0:T(8,128)S(1)} collective-permute-done((f32[8,256]{1,0:T(8,128)S(1)}, f32[8,256]{1,0:T(8,128)S(1)}, u32[]{:S(2)}, u32[]{:S(2)}) %collective-permute-start.19) | collective-permute-done | bytes 8224 | tf_op jit(solution)/shard_map/ppermute | solution.py:213
  103.4 1.1 %collective-permute-start.23 = (f32[8,256]{1,0:T(8,128)S(1)}, f32[8,256]{1,0:T(8,128)S(1)}, u32[]{:S(2)}, u32[]{:S(2)}) collective-permute-start(f32[8,256]{1,0:T(8,128)S(1)} %add_add_fusion.1), channel_id=1, source_target_pairs={{0,96},{8,104},{16,112},{24,120},{32,64},{40,72},{48,80},{56,88},{... | collective-permute-start | bytes 24584 | tf_op jit(solution)/shard_map/ppermute | solution.py:213
  104.5 1.7 %collective-permute-start.22 = (f32[8,256]{1,0:T(8,128)S(1)}, f32[8,256]{1,0:T(8,128)S(1)}, u32[]{:S(2)}, u32[]{:S(2)}) collective-permute-start(f32[8,256]{1,0:T(8,128)S(1)} %add_add_fusion.1), channel_id=1, source_target_pairs={{0,64},{8,72},{16,80},{24,88},{32,96},{40,104},{48,112},{56,120},{... | collective-permute-start | bytes 24584 | tf_op jit(solution)/shard_map/ppermute | solution.py:213
  106.2 1.4 %collective-permute-start.21 = (f32[8,256]{1,0:T(8,128)S(1)}, f32[8,256]{1,0:T(8,128)S(1)}, u32[]{:S(2)}, u32[]{:S(2)}) collective-permute-start(f32[8,256]{1,0:T(8,128)S(1)} %add_add_fusion.1), channel_id=1, source_target_pairs={{0,32},{8,40},{16,48},{24,56},{32,0},{40,8},{48,16},{56,24},{64,96... | collective-permute-start | bytes 24584 | tf_op jit(solution)/shard_map/ppermute | solution.py:213
  107.5 1.5 %returns.7 = (bf16[1024,1024]{1,0:T(8,128)(2,1)}, bf16[1024,1024]{1,0:T(8,128)(2,1)}) custom-call(s32[1]{0:T(128)S(6)} %copy.24.reach.order.refs_0_, bf16[1024,1024]{1,0:T(8,128)(2,1)S(1)} %copy-done, bf16[1024,1024]{1,0:T(8,128)(2,1)S(1)} %copy-done.2, f32[1024,512]{1,0:T(8,128)S(1)} %get-tuple-element.70.refs_3_, ...), custom_call_target="tpu_custom_call", output_to_operand_aliasing={{0}: (16, {}), {1}: (17, {})} | custom-call | flops 1000000000 | bytes 1048576 | tf_op jit(solution)/shard_map/returns/pallas_call | solution.py:325
  109.0 0.6 collective-permute-done.22
  109.6 0.2 collective-permute-done.21
  109.8 0.6 fusion.2
  (22 shorter events, 0.1 us)
Async XLA Ops:
  1.3 14.0 %copy-start = (bf16[1024,1024]{1,0:T(8,128)(2,1)S(1)}, bf16[1024,1024]{1,0:T(8,128)(2,1)}, u32[]{:S(2)}) copy-start(bf16[1024,1024]{1,0:T(8,128)(2,1)} %refs_1_.7) | copy-start | bytes 6291460
  8.6 20.5 %collective-permute-start = (f32[2,2,128,128]{3,2,1,0:T(8,128)}, f32[2,2,128,128]{3,2,1,0:T(8,128)S(1)}, u32[]{:S(2)}, u32[]{:S(2)}) collective-permute-start(f32[2,2,128,128]{3,2,1,0:T(8,128)} %get-tuple-element.53), channel_id=1, source_target_pairs={{0,8},{8,0},{16,24},{24,16},{32,40},{40,32},{48,56},{56,48},{64,72... | collective-permute-start | bytes 786440 | tf_op jit(solution)/shard_map/ppermute | solution.py:213
  10.7 18.4 %collective-permute-start.2 = (f32[2,2,128,128]{3,2,1,0:T(8,128)}, f32[2,2,128,128]{3,2,1,0:T(8,128)S(1)}, u32[]{:S(2)}, u32[]{:S(2)}) collective-permute-start(f32[2,2,128,128]{3,2,1,0:T(8,128)} %get-tuple-element.54), channel_id=1, source_target_pairs={{0,16},{8,24},{16,0},{24,8},{32,48},{40,56},{48,32},{56,40},{64,80... | collective-permute-start | bytes 786440 | tf_op jit(solution)/shard_map/ppermute | solution.py:213
  14.3 14.8 %collective-permute-start.1 = (f32[2,2,128,128]{3,2,1,0:T(8,128)}, f32[2,2,128,128]{3,2,1,0:T(8,128)S(1)}, u32[]{:S(2)}, u32[]{:S(2)}) collective-permute-start(f32[2,2,128,128]{3,2,1,0:T(8,128)} %get-tuple-element.55), channel_id=1, source_target_pairs={{0,24},{8,16},{16,8},{24,0},{32,56},{40,48},{48,40},{56,32},{64,88... | collective-permute-start | bytes 786440 | tf_op jit(solution)/shard_map/ppermute | solution.py:213
  15.2 1.6 %copy-start.1 = (bf16[1024,1024]{1,0:T(8,128)(2,1)S(1)}, bf16[1024,1024]{1,0:T(8,128)(2,1)}, u32[]{:S(2)}) copy-start(bf16[1024,1024]{1,0:T(8,128)(2,1)} %refs_2_.7) | copy-start | bytes 6291460
  16.8 1.6 %copy-start.3 = (bf16[1024,1024]{1,0:T(8,128)(2,1)S(1)}, bf16[1024,1024]{1,0:T(8,128)(2,1)}, u32[]{:S(2)}) copy-start(bf16[1024,1024]{1,0:T(8,128)(2,1)} %q_ref.7) | copy-start | bytes 6291460
  18.4 1.6 %copy-start.5 = (bf16[1024,1024]{1,0:T(8,128)(2,1)S(1)}, bf16[1024,1024]{1,0:T(8,128)(2,1)}, u32[]{:S(2)}) copy-start(bf16[1024,1024]{1,0:T(8,128)(2,1)} %g_ref.7) | copy-start | bytes 6291460
  20.0 9.1 %copy-start.8 = (f32[2,2,128,128]{3,2,1,0:T(8,128)S(1)}, f32[2,2,128,128]{3,2,1,0:T(8,128)}, u32[]{:S(2)}) copy-start(f32[2,2,128,128]{3,2,1,0:T(8,128)} %get-tuple-element.52) | copy-start | bytes 786436
  29.2 13.7 %copy-start.10 = (f32[8,128,128]{2,1,0:T(8,128)S(1)}, f32[8,128,128]{2,1,0:T(8,128)}, u32[]{:S(2)}) copy-start(f32[8,128,128]{2,1,0:T(8,128)} %get-tuple-element.64) | copy-start | bytes 1572868
  29.2 13.8 %copy-start.9 = (f32[8,128,128]{2,1,0:T(8,128)S(1)}, f32[8,128,128]{2,1,0:T(8,128)}, u32[]{:S(2)}) copy-start(f32[8,128,128]{2,1,0:T(8,128)} %get-tuple-element.65) | copy-start | bytes 1572868
  29.2 7.9 %collective-permute-start.6 = (f32[2,2,128,128]{3,2,1,0:T(8,128)S(1)}, f32[2,2,128,128]{3,2,1,0:T(8,128)S(1)}, u32[]{:S(2)}, u32[]{:S(2)}) collective-permute-start(f32[2,2,128,128]{3,2,1,0:T(8,128)S(1)} %add_add_fusion), channel_id=1, source_target_pairs={{0,32},{8,40},{16,48},{24,56},{32,0},{40,8},{48,16},{56,24},{64,96... | collective-permute-start | bytes 786440 | tf_op jit(solution)/shard_map/ppermute | solution.py:213
  37.1 10.5 %collective-permute-start.10 = (f32[2,128,128]{2,1,0:T(8,128)S(1)}, f32[2,128,128]{2,1,0:T(8,128)S(1)}, u32[]{:S(2)}, u32[]{:S(2)}) collective-permute-start(f32[2,128,128]{2,1,0:T(8,128)S(1)} %get-tuple-element.98), channel_id=1, source_target_pairs={{0,96},{8,104},{16,112},{24,120},{32,64},{40,72},{48,80},{56,88},{... | collective-permute-start | bytes 393224 | tf_op jit(solution)/shard_map/ppermute | solution.py:213
  39.9 7.8 %collective-permute-start.9 = (f32[2,128,128]{2,1,0:T(8,128)S(1)}, f32[2,128,128]{2,1,0:T(8,128)S(1)}, u32[]{:S(2)}, u32[]{:S(2)}) collective-permute-start(f32[2,128,128]{2,1,0:T(8,128)S(1)} %get-tuple-element.99.rest_0_.refs_8_), channel_id=1, source_target_pairs={{0,24},{8,16},{16,8},{24,0},{32,56},{40,48},{48,40},{56,32},{64,88... | collective-permute-start | bytes 393224 | tf_op jit(solution)/shard_map/ppermute | solution.py:213
  42.8 36.6 %copy-start.4 = (bf16[1024,1024]{1,0:T(8,128)(2,1)S(1)}, bf16[1024,1024]{1,0:T(8,128)(2,1)}, u32[]{:S(2)}) copy-start(bf16[1024,1024]{1,0:T(8,128)(2,1)} %q_ref.7) | copy-start | bytes 6291460
  42.8 36.6 %copy-start.6 = (bf16[1024,1024]{1,0:T(8,128)(2,1)S(1)}, bf16[1024,1024]{1,0:T(8,128)(2,1)}, u32[]{:S(2)}) copy-start(bf16[1024,1024]{1,0:T(8,128)(2,1)} %g_ref.7) | copy-start | bytes 6291460
  42.8 36.6 %copy-start.7 = (s32[1024]{0:T(1024)S(1)}, s32[1024]{0:T(1024)}, u32[]{:S(2)}) copy-start(s32[1024]{0:T(1024)} %param.12) | copy-start | bytes 12292
  42.8 30.1 %collective-permute-start.3 = (f32[8,128,128]{2,1,0:T(8,128)S(1)}, f32[8,128,128]{2,1,0:T(8,128)S(1)}, u32[]{:S(2)}, u32[]{:S(2)}) collective-permute-start(f32[8,128,128]{2,1,0:T(8,128)S(1)} %copy-done.10), channel_id=1, source_target_pairs={{0,8},{8,0},{16,24},{24,16},{32,40},{40,32},{48,56},{56,48},{64,72... | collective-permute-start | bytes 1572872 | tf_op jit(solution)/shard_map/ppermute | solution.py:213
  42.9 31.2 %collective-permute-start.5 = (f32[8,128,128]{2,1,0:T(8,128)S(1)}, f32[8,128,128]{2,1,0:T(8,128)S(1)}, u32[]{:S(2)}, u32[]{:S(2)}) collective-permute-start(f32[8,128,128]{2,1,0:T(8,128)S(1)} %copy-done.9), channel_id=1, source_target_pairs={{0,16},{8,24},{16,0},{24,8},{32,48},{40,56},{48,32},{56,40},{64,80... | collective-permute-start | bytes 1572872 | tf_op jit(solution)/shard_map/ppermute | solution.py:213
  44.7 29.5 %collective-permute-start.4 = (f32[8,128,128]{2,1,0:T(8,128)S(1)}, f32[8,128,128]{2,1,0:T(8,128)S(1)}, u32[]{:S(2)}, u32[]{:S(2)}) collective-permute-start(f32[8,128,128]{2,1,0:T(8,128)S(1)} %copy-done.9), channel_id=1, source_target_pairs={{0,24},{8,16},{16,8},{24,0},{32,56},{40,48},{48,40},{56,32},{64,88... | collective-permute-start | bytes 1572872 | tf_op jit(solution)/shard_map/ppermute | solution.py:213
  47.6 22.4 %collective-permute-start.8 = (f32[2,128,128]{2,1,0:T(8,128)S(1)}, f32[2,128,128]{2,1,0:T(8,128)S(1)}, u32[]{:S(2)}, u32[]{:S(2)}) collective-permute-start(f32[2,128,128]{2,1,0:T(8,128)S(1)} %get-tuple-element.99.rest_0_.refs_8_), channel_id=1, source_target_pairs={{0,16},{8,24},{16,0},{24,8},{32,48},{40,56},{48,32},{56,40},{64,80... | collective-permute-start | bytes 393224 | tf_op jit(solution)/shard_map/ppermute | solution.py:213
  47.6 25.3 %collective-permute-start.7 = (f32[2,128,128]{2,1,0:T(8,128)S(1)}, f32[2,128,128]{2,1,0:T(8,128)S(1)}, u32[]{:S(2)}, u32[]{:S(2)}) collective-permute-start(f32[2,128,128]{2,1,0:T(8,128)S(1)} %get-tuple-element.99.rest_0_.refs_8_), channel_id=1, source_target_pairs={{0,8},{8,0},{16,24},{24,16},{32,40},{40,32},{48,56},{56,48},{64,72... | collective-permute-start | bytes 393224 | tf_op jit(solution)/shard_map/ppermute | solution.py:213
  70.0 6.9 %collective-permute-start.13 = (f32[2,128,128]{2,1,0:T(8,128)S(1)}, f32[2,128,128]{2,1,0:T(8,128)S(1)}, u32[]{:S(2)}, u32[]{:S(2)}) collective-permute-start(f32[2,128,128]{2,1,0:T(8,128)S(1)} %collective-permute-done.10.rest_4_.refs_12_), channel_id=1, source_target_pairs={{0,24},{8,16},{16,8},{24,0},{32,56},{40,48},{48,40},{56,32},{64,88... | collective-permute-start | bytes 393224 | tf_op jit(solution)/shard_map/ppermute | solution.py:213
  73.0 6.5 %collective-permute-start.12 = (f32[2,128,128]{2,1,0:T(8,128)S(1)}, f32[2,128,128]{2,1,0:T(8,128)S(1)}, u32[]{:S(2)}, u32[]{:S(2)}) collective-permute-start(f32[2,128,128]{2,1,0:T(8,128)S(1)} %collective-permute-done.10.rest_4_.refs_12_), channel_id=1, source_target_pairs={{0,16},{8,24},{16,0},{24,8},{32,48},{40,56},{48,32},{56,40},{64,80... | collective-permute-start | bytes 393224 | tf_op jit(solution)/shard_map/ppermute | solution.py:213
  73.0 6.5 %collective-permute-start.11 = (f32[2,128,128]{2,1,0:T(8,128)S(1)}, f32[2,128,128]{2,1,0:T(8,128)S(1)}, u32[]{:S(2)}, u32[]{:S(2)}) collective-permute-start(f32[2,128,128]{2,1,0:T(8,128)S(1)} %collective-permute-done.10.rest_4_.refs_12_), channel_id=1, source_target_pairs={{0,8},{8,0},{16,24},{24,16},{32,40},{40,32},{48,56},{56,48},{64,72... | collective-permute-start | bytes 393224 | tf_op jit(solution)/shard_map/ppermute | solution.py:213
  79.4 7.0 %copy-start.2 = (bf16[1024,1024]{1,0:T(8,128)(2,1)S(1)}, bf16[1024,1024]{1,0:T(8,128)(2,1)}, u32[]{:S(2)}) copy-start(bf16[1024,1024]{1,0:T(8,128)(2,1)} %refs_2_.7) | copy-start | bytes 6291460
  86.4 1.8 %collective-permute-start.14 = (f32[8,256]{1,0:T(8,128)S(1)}, f32[8,256]{1,0:T(8,128)S(1)}, u32[]{:S(2)}, u32[]{:S(2)}) collective-permute-start(f32[8,256]{1,0:T(8,128)S(1)} %get-tuple-element.73), channel_id=1, source_target_pairs={{0,1},{1,0},{2,3},{3,2},{4,5},{5,4},{6,7},{7,6},{8,9},{9,8},{10,11... | collective-permute-start | bytes 24584 | tf_op jit(solution)/shard_map/ppermute | solution.py:213
  88.1 5.8 %collective-permute-start.17 = (f32[8,256]{1,0:T(8,128)S(1)}, f32[8,256]{1,0:T(8,128)S(1)}, u32[]{:S(2)}, u32[]{:S(2)}) collective-permute-start(f32[8,256]{1,0:T(8,128)S(1)} %add.50), channel_id=1, source_target_pairs={{0,6},{1,7},{2,4},{3,5},{4,2},{5,3},{6,0},{7,1},{8,14},{9,15},{10,... | collective-permute-start | bytes 24584 | tf_op jit(solution)/shard_map/ppermute | solution.py:213
  91.0 5.2 %collective-permute-start.16 = (f32[8,256]{1,0:T(8,128)S(1)}, f32[8,256]{1,0:T(8,128)S(1)}, u32[]{:S(2)}, u32[]{:S(2)}) collective-permute-start(f32[8,256]{1,0:T(8,128)S(1)} %add.50), channel_id=1, source_target_pairs={{0,4},{1,5},{2,6},{3,7},{4,0},{5,1},{6,2},{7,3},{8,12},{9,13},{10,... | collective-permute-start | bytes 24584 | tf_op jit(solution)/shard_map/ppermute | solution.py:213
  91.8 4.4 %collective-permute-start.15 = (f32[8,256]{1,0:T(8,128)S(1)}, f32[8,256]{1,0:T(8,128)S(1)}, u32[]{:S(2)}, u32[]{:S(2)}) collective-permute-start(f32[8,256]{1,0:T(8,128)S(1)} %add.50), channel_id=1, source_target_pairs={{0,2},{1,3},{2,0},{3,1},{4,6},{5,7},{6,4},{7,5},{8,10},{9,11},{10,... | collective-permute-start | bytes 24584 | tf_op jit(solution)/shard_map/ppermute | solution.py:213
  96.1 5.7 %collective-permute-start.20 = (f32[8,256]{1,0:T(8,128)S(1)}, f32[8,256]{1,0:T(8,128)S(1)}, u32[]{:S(2)}, u32[]{:S(2)}) collective-permute-start(f32[8,256]{1,0:T(8,128)S(1)} %add_add_fusion.2), channel_id=1, source_target_pairs={{0,24},{8,16},{16,8},{24,0},{32,56},{40,48},{48,40},{56,32},{64,88... | collective-permute-start | bytes 24584 | tf_op jit(solution)/shard_map/ppermute | solution.py:213
  98.2 5.2 %collective-permute-start.19 = (f32[8,256]{1,0:T(8,128)S(1)}, f32[8,256]{1,0:T(8,128)S(1)}, u32[]{:S(2)}, u32[]{:S(2)}) collective-permute-start(f32[8,256]{1,0:T(8,128)S(1)} %add_add_fusion.2), channel_id=1, source_target_pairs={{0,16},{8,24},{16,0},{24,8},{32,48},{40,56},{48,32},{56,40},{64,80... | collective-permute-start | bytes 24584 | tf_op jit(solution)/shard_map/ppermute | solution.py:213
  98.3 5.0 %collective-permute-start.18 = (f32[8,256]{1,0:T(8,128)S(1)}, f32[8,256]{1,0:T(8,128)S(1)}, u32[]{:S(2)}, u32[]{:S(2)}) collective-permute-start(f32[8,256]{1,0:T(8,128)S(1)} %add_add_fusion.2), channel_id=1, source_target_pairs={{0,8},{8,0},{16,24},{24,16},{32,40},{40,32},{48,56},{56,48},{64,72... | collective-permute-start | bytes 24584 | tf_op jit(solution)/shard_map/ppermute | solution.py:213
  103.4 5.7 %collective-permute-start.23 = (f32[8,256]{1,0:T(8,128)S(1)}, f32[8,256]{1,0:T(8,128)S(1)}, u32[]{:S(2)}, u32[]{:S(2)}) collective-permute-start(f32[8,256]{1,0:T(8,128)S(1)} %add_add_fusion.1), channel_id=1, source_target_pairs={{0,96},{8,104},{16,112},{24,120},{32,64},{40,72},{48,80},{56,88},{... | collective-permute-start | bytes 24584 | tf_op jit(solution)/shard_map/ppermute | solution.py:213
  104.5 5.2 %collective-permute-start.22 = (f32[8,256]{1,0:T(8,128)S(1)}, f32[8,256]{1,0:T(8,128)S(1)}, u32[]{:S(2)}, u32[]{:S(2)}) collective-permute-start(f32[8,256]{1,0:T(8,128)S(1)} %add_add_fusion.1), channel_id=1, source_target_pairs={{0,64},{8,72},{16,80},{24,88},{32,96},{40,104},{48,112},{56,120},{... | collective-permute-start | bytes 24584 | tf_op jit(solution)/shard_map/ppermute | solution.py:213
  106.2 3.7 %collective-permute-start.21 = (f32[8,256]{1,0:T(8,128)S(1)}, f32[8,256]{1,0:T(8,128)S(1)}, u32[]{:S(2)}, u32[]{:S(2)}) collective-permute-start(f32[8,256]{1,0:T(8,128)S(1)} %add_add_fusion.1), channel_id=1, source_target_pairs={{0,32},{8,40},{16,48},{24,56},{32,0},{40,8},{48,16},{56,24},{64,96... | collective-permute-start | bytes 24584 | tf_op jit(solution)/shard_map/ppermute | solution.py:213

commit v4 on v3

--- a/solution.py
+++ b/solution.py
@@ -36,8 +36,8 @@
     return jnp.where(ids == index_row, 1.0, 0.0).astype(bf16)
 
 
-def states_kernel(reach, index_ref, table_ref, q_hbm, k_hbm, v_hbm, g_hbm, w_ref, near1_ref, near2_ref, *rest):
-    far_refs, buf, table, sem = rest[:4], rest[4], rest[5], rest[6]
+def states_kernel(reach, index_ref, table_ref, q_hbm, k_hbm, v_hbm, g_hbm, w_ref, near1_ref, near2_ref, keep_ref, send_ref, buf, table, sem):
+    far_refs = (keep_ref.at[0], keep_ref.at[1], send_ref.at[1], send_ref.at[0])
     sources = (q_hbm, k_hbm, v_hbm, g_hbm)
     wide = buf.shape[-1]
     each = wide // DH
@@ -80,7 +80,7 @@
     return rows <= cols if flip_sides else rows >= cols
 
 
-def query_kernel(order, q_ref, k_ref, v_ref, g_ref, w_ref, out_ref, lam_ref):
+def query_kernel(after, q_ref, k_ref, v_ref, g_ref, w_ref, out_ref, lam_ref):
     @pl.when(pl.program_id(0) == 0)
     def _():
         lam_ref[...] = jnp.zeros_like(lam_ref)
@@ -101,7 +101,7 @@
             state = state + mm(v, k, 0, 0)
 
 
-def key_value_kernel(order, q_ref, k_ref, v_ref, g_ref, w_ref, key_ref, value_ref):
+def key_value_kernel(after, q_ref, k_ref, v_ref, g_ref, w_ref, key_ref, value_ref):
     causal = causal_mask(True)
     state = jnp.zeros((DH, DH), f32)
     count = q_ref.shape[0] // CHUNK
@@ -123,13 +123,13 @@
             state = state + mm(g, q, 0, 0)
 
 
-def level_states(keep, y1_ref, y2a_ref, y2b_ref, y3_refs, y4_refs, bits, head, j, i):
-    ys = (y1_ref[head], y2a_ref[head] + y2b_ref[head], y3_refs[j][i], y4_refs[j][i])
+def level_states(keep, y1_ref, y2_ref, y34_refs, bits, head, j, i):
+    ys = (y1_ref[head], y2_ref[head], y34_refs[j][0, i], y34_refs[j][1, i])
     return [jnp.where(bits[l] == keep, ys[l], 0.0) for l in range(4)]
 
 
-def reads_kernel(reach, q_ref, g_ref, w_ref, qn_ref, lam0_ref, index_ref, y1_ref, y2a_ref, y2b_ref, *rest):
-    y3_refs, y4_refs, (out_hbm, table_ref, st, out_buf, sem) = rest[:4], rest[4:8], rest[8:]
+def reads_kernel(reach, q_ref, g_ref, w_ref, qn_ref, lam0_ref, index_ref, y1_ref, y2_ref, *rest):
+    y34_refs, (out_hbm, table_ref, st, out_buf, sem) = rest[:4], rest[4:]
     length = q_ref.shape[0]
     heads = y1_ref.shape[0]
     each = heads // 4
@@ -138,7 +138,7 @@
     for j in range(4):
         for i in range(each):
             head = (spot ^ j) * each + i
-            parts = level_states(1, y1_ref, y2a_ref, y2b_ref, y3_refs, y4_refs, bits, head, j, i)
+            parts = level_states(1, y1_ref, y2_ref, y34_refs, bits, head, j, i)
             st[head] = jnp.concatenate(parts, 1).astype(bf16)
     lane = lax.broadcasted_iota(jnp.int32, (1, DH), 1)
     table = None
@@ -146,26 +146,25 @@
     for t in range(length // tile):
         at = pl.ds(t * tile, tile)
         w = w_ref[at, :]
-        wide = [jnp.broadcast_to(w[:, l : l + 1], (tile, DH)) for l in range(1, 5)]
+        wide = [jnp.broadcast_to(SCALE * w[:, l : l + 1], (tile, DH)) for l in range(1, 5)]
         acc = [None] * 4
         for h in range(heads):
             c = slice(h * DH, (h + 1) * DH)
             reads = mm(g_ref[at, c], st[h], 1, 0)
             q = q_ref[at, c].astype(f32)
-            total = None
+            total = qn_ref[at, c]
             for l in range(4):
                 read = reads[:, l * DH : (l + 1) * DH]
                 product = q * read
                 acc[l] = product if acc[l] is None else acc[l] + product
-                term = wide[l] * read
-                total = term if total is None else total + term
-            out_buf[at, c] = (qn_ref[at, c] + SCALE * total).astype(bf16)
+                total = total + wide[l] * read
+            out_buf[at, c] = total.astype(bf16)
         copies.append(pltpu.make_async_copy(out_buf.at[at, :], out_hbm.at[at, :], sem.at[t]))
         copies[-1].start()
-        lam = jnp.where(lane == 0, jnp.sum(lam0_ref[at, :], 1, keepdims=True), 0.0)
-        for l in range(4):
-            here = (lane == l + 1) & (reach[0] > l)
-            lam = jnp.where(here, jnp.sum(acc[l], 1, keepdims=True), lam)
+        lam = jnp.zeros((tile, DH), f32)
+        for l, x in enumerate([lam0_ref[at, :]] + acc):
+            here = (lane == l) & (reach[0] >= l)
+            lam = jnp.where(here, jnp.sum(x, 1, keepdims=True), lam)
         lam = (SCALE * lam).T[:8]
         picked = one_hot(index_ref[:, at], table_ref.shape[1])
         for piece in thirds(lam):
@@ -176,8 +175,28 @@
         copy.wait()
 
 
-def returns_kernel(start, order, k_ref, v_ref, kn_ref, vn_ref, y1_ref, y2a_ref, y2b_ref, *rest):
-    y3_refs, y4_refs, rest = rest[:4], rest[4:8], rest[8:]
+def pair_kernel(keep_ref, got_ref, near_ref, near_got_ref, after, own_ref, send_ref, sum_ref):
+    own_ref[...] = keep_ref[0] + got_ref[0]
+    send_ref[...] = keep_ref[1] + got_ref[1]
+    sum_ref[...] = near_ref[...] + near_got_ref[...]
+
+
+def rows_kernel(own_ref, got_ref, after, near_in, rows_ref, near_out):
+    rows_ref[...] = own_ref[...] + got_ref[...]
+
+
+def cross_kernel(rows_ref, other_ref, after, after_too, out_ref):
+    out_ref[...] = rows_ref[1] + other_ref[1]
+
+
+def pack_kernel(y3_ref, y4_ref, *rest):
+    out_ref = rest[-1]
+    out_ref[0] = y3_ref[0]
+    out_ref[1] = y4_ref[...]
+
+
+def returns_kernel(start, order, k_ref, v_ref, kn_ref, vn_ref, y1_ref, y2_ref, *rest):
+    y34_refs = rest[:4]
     key_hbm, value_hbm, key_buf, value_buf, st, sem = rest[-6:]
     heads = y1_ref.shape[0]
     each = heads // 4
@@ -190,7 +209,7 @@
 
             @pl.when((head >= start) & (head < start + count))
             def _():
-                parts = level_states(0, y1_ref, y2a_ref, y2b_ref, y3_refs, y4_refs, bits, head, j, i)
+                parts = level_states(0, y1_ref, y2_ref, y34_refs, bits, head, j, i)
                 st[head] = (parts[0] + parts[1] + parts[2] + parts[3]).astype(bf16)
 
     for i in range(count):
@@ -213,6 +232,10 @@
     return lax.ppermute(x, axis, [(i, i ^ mask) for i in range(lax.axis_size(axis))])
 
 
+def in_hbm(x):
+    return pltpu.with_memory_space_constraint(x, pltpu.HBM)
+
+
 def tie(x, *deps):
     return lax.optimization_barrier((x, *deps))[0]
 
@@ -229,80 +252,95 @@
     scalar = pl.BlockSpec(memory_space=pltpu.SMEM)
     anywhere = pl.BlockSpec(memory_space=pl.ANY)
     limit = lambda mib: pltpu.CompilerParams(vmem_limit_bytes=mib * MIB)
-    cost = lambda us: pl.CostEstimate(flops=int(us * 10**9), bytes_accessed=MIB, transcendentals=0)
-
-    w_rows, near, near2, *far = pl.pallas_call(
+    cost = pl.CostEstimate(flops=10**8, bytes_accessed=MIB, transcendentals=0)
+
+    w_rows, near, near2, keep, send = pl.pallas_call(
         states_kernel,
         in_specs=[scalar, whole, whole] + [anywhere] * 4,
-        out_specs=[whole] * 7,
+        out_specs=[whole] * 5,
         out_shape=[sds((8, length), f32)]
         + [sds((heads, DH, DH), f32)] * 2
-        + [sds((2, each, DH, DH), f32)] * 4,
+        + [sds((2, 2, each, DH, DH), f32)] * 2,
         scratch_shapes=[
             pltpu.VMEM((4, 4, length, each * DH), bf16),
             pltpu.VMEM((8, names), f32),
             pltpu.SemaphoreType.DMA((4, 4)),
         ],
-        compiler_params=limit(60),
+        compiler_params=limit(20),
         name="states",
-    )(reach, index_row, level_table, queries, keys, values, out_grad)
+    )(reach, index_row, level_table, *[in_hbm(x) for x in (queries, keys, values, out_grad)])
     w_cols = w_rows.T
 
     token_spec = lambda start: pl.BlockSpec((length, DH), lambda h: (0, h + start))
     fixed = lambda shape: pl.BlockSpec(shape, lambda h: (0,) * len(shape))
 
-    def near_part(kernel, order, start, count, out_shape, out_specs, name):
+    near_params = pltpu.CompilerParams(
+        dimension_semantics=("arbitrary",), vmem_limit_bytes=12 * MIB
+    )
+    tokens = [in_hbm(x) for x in (queries, keys, values, out_grad)]
+
+    def key_value_part(order, start):
+        return pl.pallas_call(
+            key_value_kernel,
+            grid=(each,),
+            in_specs=[anywhere] + [token_spec(start)] * 4 + [fixed((length, 8))],
+            out_specs=[token_spec(0)] * 2,
+            out_shape=[sds((length, each * DH), f32)] * 2,
+            compiler_params=near_params,
+            cost_estimate=cost,
+            name="key_value",
+        )(order, *tokens, w_cols)
+
+    def local_step(kernel, ins, afters, outs, name, aliases=None):
         return pl.pallas_call(
             kernel,
-            grid=(count,),
-            in_specs=[scalar] + [token_spec(start)] * 4 + [fixed((length, 8))],
-            out_specs=out_specs,
-            out_shape=out_shape,
-            compiler_params=pltpu.CompilerParams(
-                dimension_semantics=("arbitrary",), vmem_limit_bytes=20 * MIB
-            ),
-            cost_estimate=cost(5),
+            in_specs=[whole] * len(ins) + [anywhere] * len(afters),
+            out_specs=[whole] * (len(outs) - len(aliases or {})) + [anywhere] * len(aliases or {}),
+            out_shape=[sds(x, f32) for x in outs],
+            input_output_aliases=aliases or {},
+            compiler_params=limit(6),
+            cost_estimate=cost,
             name=name,
-        )(order, queries, keys, values, out_grad, w_cols)
-
-    def key_value_part(order, start, count, name):
-        shape = sds((length, count * DH), f32)
-        return near_part(
-            key_value_kernel, order, start, count, [shape] * 2, [token_spec(0)] * 2, name
-        )
-
-    got = [flip(far[m], "seq", m) for m in (1, 3, 2)]
-    qn, lam0 = near_part(
+        )(*ins, *afters)
+
+    quarter = keep.shape[1:]
+    got, near_got = flip(send, "seq", 3), flip(near2, "seq", 1)
+    near_parts = [key_value_part(keep, 0)]
+    near_parts.append(key_value_part(near_parts[0][0], each))
+    own, send, near_sum = local_step(
+        pair_kernel,
+        [keep, got, near2, near_got],
+        [near_parts[1][0]],
+        [quarter, quarter, near2.shape],
+        "pair",
+    )
+    got, y2 = flip(send, "seq", 1), flip(near_sum, "seq", 3)
+    near_parts.append(key_value_part(own, 2 * each))
+    rows, near = local_step(
+        rows_kernel, [own, got], [near_parts[2][0], near], [quarter, near.shape], "rows", {3: 1}
+    )
+    other, y1 = flip(rows, "seq", 4), flip(near, "seq", 1)
+    near_parts.append(key_value_part(rows, 3 * each))
+    (far4,) = local_step(
+        cross_kernel, [rows, other], [y2, near_parts[3][0]], [quarter[1:]], "cross"
+    )
+    y4 = flip(far4, "seq", 12)
+    (y34,) = local_step(pack_kernel, [other, y4], [y1], [quarter], "pack")
+    y34s = [y34] + [flip(y34, "seq", m) for m in (1, 2, 3)]
+    qn, lam0 = pl.pallas_call(
         query_kernel,
-        tie(reach, *far),
-        0,
-        heads,
-        [sds((length, heads * DH), f32), sds((length, DH), f32)],
-        [token_spec(0), fixed((length, DH))],
-        "query",
-    )
-    got = lax.optimization_barrier((*got, qn))[:3]
-    rows = (far[0] + got[2]) + (got[0] + got[1])
-    other = flip(rows, "seq", 4)
-    near, near2 = lax.optimization_barrier((near, near2, rows))[:2]
-    y1 = flip(near, "seq", 1)
-    y2a = flip(near2, "seq", 3)
-    y2b = flip(near2, "seq", 2)
-    half = heads // 2
-    kn_a, vn_a = key_value_part(tie(reach, rows), 0, half, "key_value_a")
-    other = tie(other, kn_a)
-    y3 = other[0]
-    far4 = rows[1] + other[1]
-    y4 = flip(far4, "seq", 12)
-    y3s = [y3] + [flip(y3, "seq", m) for m in (1, 2, 3)]
-    kn_b, vn_b = key_value_part(tie(reach, far4), half, half, "key_value_b")
-    y4 = tie(y4, kn_b)
-    y4s = [y4] + [flip(y4, "seq", m) for m in (1, 2, 3)]
-    arrived = (y1, y2a, y2b, *y3s, *y4s)
+        grid=(heads,),
+        in_specs=[anywhere] + [token_spec(0)] * 4 + [fixed((length, 8))],
+        out_specs=[token_spec(0), fixed((length, DH))],
+        out_shape=[sds((length, heads * DH), f32), sds((length, DH), f32)],
+        compiler_params=near_params,
+        cost_estimate=cost,
+        name="query",
+    )(y34, *tokens, w_cols)
 
     query_grad, total = pl.pallas_call(
         reads_kernel,
-        in_specs=[scalar] + [whole] * 17,
+        in_specs=[scalar] + [whole] * 12,
         out_specs=[anywhere, whole],
         out_shape=[sds((length, heads * DH), bf16), sds((8, names), f32)],
         scratch_shapes=[
@@ -310,13 +348,14 @@
             pltpu.VMEM((length, heads * DH), bf16),
             pltpu.SemaphoreType.DMA((length // CHUNK,)),
         ],
-        compiler_params=limit(30),
-        cost_estimate=cost(6),
+        compiler_params=limit(24),
+        cost_estimate=cost,
         name="reads",
-    )(reach, queries, out_grad, w_cols, qn, lam0, index_row, *arrived)
+    )(reach, queries, out_grad, w_cols, qn, lam0, index_row, y1, y2, *y34s)
+    arrived = (y1, y2, *y34s)
 
     def returns(order, start, count, held):
-        kn, vn = (kn_a, vn_a) if start < half else (kn_b, vn_b)
+        kn, vn = near_parts[start // each]
         shape = sds((length, heads * DH), bf16)
 
         def kernel(*refs):
@@ -324,7 +363,7 @@
 
         return pl.pallas_call(
             kernel,
-            in_specs=[scalar] + [whole] * 15 + [anywhere] * len(held),
+            in_specs=[scalar] + [whole] * 10 + [anywhere] * len(held),
             out_specs=[anywhere] * 2,
             out_shape=[shape] * 2,
             scratch_shapes=[
@@ -333,9 +372,9 @@
                 pltpu.VMEM((heads, DH, DH), bf16),
                 pltpu.SemaphoreType.DMA((2,)),
             ],
-            input_output_aliases={16: 0, 17: 1} if held else {},
+            input_output_aliases={11: 0, 12: 1} if held else {},
             compiler_params=limit(20),
-            cost_estimate=cost(1),
+            cost_estimate=cost,
             name="returns",
         )(order, keys, values, kn, vn, *arrived, *held)
 

time: 111 us -> 93.5 us (0.84)
  starting transfers between devices: 35.6 us -> 28.2 us
  waiting for transfers between devices: 24.9 us -> 17.7 us
  local copies, waits for them, and re-layouts: 5.76 us -> 1.6 us
  Pallas kernels: 41.9 us -> 43.4 us
    ppermute x24 -> x20, starting transfers between devices: 35.6 us -> 28.2 us  [flip(): lax.ppermute(x, axis, [(i, i ^ mask) for i in range(lax.axis_size(axis))])]
    ppermute x24 -> x20, waiting for transfers between devices: 24.9 us -> 17.7 us  [flip(): lax.ppermute(x, axis, [(i, i ^ mask) for i in range(lax.axis_size(axis))])]
    unnamed x22 -> x14, local copies, waits for them, and re-layouts: 4.81 us -> 1.41 us
    pallas_call x8 -> x14, Pallas kernels: 34.6 us -> 37.3 us  [the longest x4 14.9 us: key_value_part(): pl.pallas_call(key_value_kernel, grid=(each,), in_specs=[anywhere] + [tok...]
    pallas_call x1, Pallas kernels: 7.27 us -> 6.11 us  [local(): pl.pallas_call(states_kernel, in_specs=[scalar, whole, whole] + [anywhere...]
  transfers between devices with their start and end apart: 24 -> 20, of which waited for: 7 -> 9; matrix products, arithmetic and copies ran while one was open for 1% -> 0% of each run, Pallas kernels for 25% -> 33%
where the time goes in v4:
time: 93.5 us; the launch traced here: 93.1 us
  Pallas kernels  43.4 us (46%)
  starting transfers between devices  28.2 us (30%)
  waiting for transfers between devices  17.7 us (19%)
  local copies, waits for them, and re-layouts  1.6 us (2%)
  between operations  1.56 us (2%)
    ppermute x20, starting transfers between devices, flip(): lax.ppermute(x, axis, [(i, i ^ mask) for i in range(lax.axis_size(axis))])  28.2 us
    ppermute x20, waiting for transfers between devices, flip(): lax.ppermute(x, axis, [(i, i ^ mask) for i in range(lax.axis_size(axis))])  17.7 us
    pallas_call x4, Pallas kernels, key_value_part(): pl.pallas_call(key_value_kernel, grid=(each,), in_specs=[anywhere] + [tok...  14.9 us
    pallas_call x1, Pallas kernels, local(): pl.pallas_call(query_kernel, grid=(heads,), in_specs=[anywhere] + [token_...  9.3 us
    pallas_call x1, Pallas kernels, local(): pl.pallas_call(reads_kernel, in_specs=[scalar] + [whole] * 12, out_specs=...  6.85 us
    pallas_call x1, Pallas kernels, local(): pl.pallas_call(states_kernel, in_specs=[scalar, whole, whole] + [anywhere...  6.11 us
    pallas_call x4, Pallas kernels, returns(): pl.pallas_call(kernel, in_specs=[scalar] + [whole] * 10 + [anywhere] * le...  6.09 us
  transfers between devices with their start and end apart: 20, of which 9 were waited for; matrix products, arithmetic and copies ran while one was open for 0% of the time, Pallas kernels for 33%

profile of v4, /device:TPU:0, one launch (start us, length us, event | category | flops | bytes accessed | tf_op | source)
XLA Modules:
  0.0 93.1 jit_solution(15629692794046536849)
XLA Ops:
  1.3 0.0 copy-start.4
  1.3 0.7 copy-done.4
  2.0 0.7 copy-done.6
  2.7 6.1 %states.1 = (f32[8,1024]{1,0:T(8,128)S(1)}, f32[8,128,128]{2,1,0:T(8,128)S(1)}, f32[8,128,128]{2,1,0:T(8,128)S(1)}, f32[2,2,2,128,128]{4,3,2,1,0:T(8,128)S(1)}, f32[2,2,2,128,128]{4,3,2,1,0:T(8,128)}) custom-call(s32[1]{0:T(128)S(6)} %copy.26.reach.refs_0_, s32[1,1024]{1,0:T(1,128)S(1)} %bitcast.8, f32[5,256]{1,0:T(8,128)S(1)} %copy-done.6, ...), custom_call_target="tpu_custom_call" | custom-call | tf_op jit(solution)/shard_map/states/pallas_call | solution.py:257
  8.8 4.3 %collective-permute-start = (f32[2,2,2,128,128]{4,3,2,1,0:T(8,128)}, f32[2,2,2,128,128]{4,3,2,1,0:T(8,128)S(1)}, u32[]{:S(2)}, u32[]{:S(2)}) collective-permute-start(f32[2,2,2,128,128]{4,3,2,1,0:T(8,128)} %get-tuple-element.50), channel_id=1, source_target_pairs={{0,24},{8,16},{16,8},{24,0},{32,56},{40,48},{48,40},{56,32},{64,88... | collective-permute-start | bytes 1572872 | tf_op jit(solution)/shard_map/ppermute | solution.py:232
  13.1 0.0 collective-permute-start.1
  13.1 0.2 copy.18
  13.3 3.7 %key_value.4 = (f32[1024,256]{1,0:T(8,128)S(1)}, f32[1024,256]{1,0:T(8,128)S(1)}) custom-call(f32[2,2,2,128,128]{4,3,2,1,0:T(8,128)S(1)} %get-tuple-element.49.after.keep_ref, bf16[1024,1024]{1,0:T(8,128)(2,1)} %q_ref.11, bf16[1024,1024]{1,0:T(8,128)(2,1)} %refs_1_.7, bf16[1024,1024]{1,0:T(8,128)(2,1)} %refs_2_.7, bf16[1024,1024]{1,0:T(8,128)(2,1)} %g_ref.11, ...), custom_call_target="tpu_custom_call" | custom-call | flops 100000000 | bytes 1048576 | tf_op jit(solution)/shard_map/key_value/pallas_call | solution.py:283
  17.0 3.7 %key_value.5 = (f32[1024,256]{1,0:T(8,128)S(1)}, f32[1024,256]{1,0:T(8,128)S(1)}) custom-call(f32[1024,256]{1,0:T(8,128)S(1)} %get-tuple-element.52.after.refs_3_, bf16[1024,1024]{1,0:T(8,128)(2,1)} %q_ref.11, bf16[1024,1024]{1,0:T(8,128)(2,1)} %refs_1_.7, bf16[1024,1024]{1,0:T(8,128)(2,1)} %refs_2_.7, bf16[1024,1024]{1,0:T(8,128)(2,1)} %g_ref.11, ...), custom_call_target="tpu_custom_call" | custom-call | flops 100000000 | bytes 1048576 | tf_op jit(solution)/shard_map/key_value/pallas_call | solution.py:283
  20.8 4.5 %collective-permute-done.got_ref = f32[2,2,2,128,128]{4,3,2,1,0:T(8,128)S(1)} collective-permute-done((f32[2,2,2,128,128]{4,3,2,1,0:T(8,128)}, f32[2,2,2,128,128]{4,3,2,1,0:T(8,128)S(1)}, u32[]{:S(2)}, u32[]{:S(2)}) %collective-permute-start) | collective-permute-done | bytes 524320 | tf_op jit(solution)/shard_map/ppermute | solution.py:232
  25.2 1.2 %collective-permute-done.1.near_got_ref = f32[8,128,128]{2,1,0:T(8,128)S(1)} collective-permute-done((f32[8,128,128]{2,1,0:T(8,128)S(1)}, f32[8,128,128]{2,1,0:T(8,128)S(1)}, u32[]{:S(2)}, u32[]{:S(2)}) %collective-permute-start.1) | collective-permute-done | bytes 524320 | tf_op jit(solution)/shard_map/ppermute | solution.py:232
  26.5 0.1 pair.1
  26.6 0.4 collective-permute-start.2
  26.9 1.5 %collective-permute-start.4 = (f32[8,128,128]{2,1,0:T(8,128)S(1)}, f32[8,128,128]{2,1,0:T(8,128)S(1)}, u32[]{:S(2)}, u32[]{:S(2)}) collective-permute-start(f32[8,128,128]{2,1,0:T(8,128)S(1)} %get-tuple-element.59), channel_id=1, source_target_pairs={{0,24},{8,16},{16,8},{24,0},{32,56},{40,48},{48,40},{56,32},{64,88... | collective-permute-start | bytes 1572872 | tf_op jit(solution)/shard_map/ppermute | solution.py:232
  28.4 3.7 %key_value.6 = (f32[1024,256]{1,0:T(8,128)S(1)}, f32[1024,256]{1,0:T(8,128)S(1)}) custom-call(f32[2,2,128,128]{3,2,1,0:T(8,128)S(1)} %get-tuple-element.54.after.own_ref, bf16[1024,1024]{1,0:T(8,128)(2,1)} %q_ref.11, bf16[1024,1024]{1,0:T(8,128)(2,1)} %refs_1_.7, bf16[1024,1024]{1,0:T(8,128)(2,1)} %refs_2_.7, bf16[1024,1024]{1,0:T(8,128)(2,1)} %g_ref.11, ...), custom_call_target="tpu_custom_call" | custom-call | flops 100000000 | bytes 1048576 | tf_op jit(solution)/shard_map/key_value/pallas_call | solution.py:283
  32.2 1.3 %collective-permute-done.2.got_ref = f32[2,2,128,128]{3,2,1,0:T(8,128)S(1)} collective-permute-done((f32[2,2,128,128]{3,2,1,0:T(8,128)S(1)}, f32[2,2,128,128]{3,2,1,0:T(8,128)S(1)}, u32[]{:S(2)}, u32[]{:S(2)}) %collective-permute-start.2) | collective-permute-done | bytes 262176 | tf_op jit(solution)/shard_map/ppermute | solution.py:232
  33.5 0.7 collective-permute-start.6
  34.2 1.6 %collective-permute-start.3 = (f32[2,2,128,128]{3,2,1,0:T(8,128)S(1)}, f32[2,2,128,128]{3,2,1,0:T(8,128)S(1)}, u32[]{:S(2)}, u32[]{:S(2)}) collective-permute-start(f32[2,2,128,128]{3,2,1,0:T(8,128)S(1)} %get-tuple-element.58.after.rows_ref), channel_id=1, source_target_pairs={{0,32},{8,40},{16,48},{24,56},{32,0},{40,8},{48,16},{56,24},{64,96... | collective-permute-start | bytes 786440 | tf_op jit(solution)/shard_map/ppermute | solution.py:232
  35.8 3.7 %key_value.7 = (f32[1024,256]{1,0:T(8,128)S(1)}, f32[1024,256]{1,0:T(8,128)S(1)}) custom-call(f32[2,2,128,128]{3,2,1,0:T(8,128)S(1)} %get-tuple-element.58.after.rows_ref, bf16[1024,1024]{1,0:T(8,128)(2,1)} %q_ref.11, bf16[1024,1024]{1,0:T(8,128)(2,1)} %refs_1_.7, bf16[1024,1024]{1,0:T(8,128)(2,1)} %refs_2_.7, bf16[1024,1024]{1,0:T(8,128)(2,1)} %g_ref.11, ...), custom_call_target="tpu_custom_call" | custom-call | flops 100000000 | bytes 1048576 | tf_op jit(solution)/shard_map/key_value/pallas_call | solution.py:283
  39.5 1.1 %collective-permute-done.4.after.y2_ref.refs_6_ = f32[8,128,128]{2,1,0:T(8,128)S(1)} collective-permute-done((f32[8,128,128]{2,1,0:T(8,128)S(1)}, f32[8,128,128]{2,1,0:T(8,128)S(1)}, u32[]{:S(2)}, u32[]{:S(2)}) %collective-permute-start.4) | collective-permute-done | bytes 524320 | tf_op jit(solution)/shard_map/ppermute | solution.py:232
  40.7 0.0 collective-permute-done.3.other_ref.y3_ref
  40.7 3.1 %collective-permute-start.5 = (f32[2,128,128]{2,1,0:T(8,128)S(1)}, f32[2,128,128]{2,1,0:T(8,128)S(1)}, u32[]{:S(2)}, u32[]{:S(2)}) collective-permute-start(f32[2,128,128]{2,1,0:T(8,128)S(1)} %cross.1), channel_id=1, source_target_pairs={{0,96},{8,104},{16,112},{24,120},{32,64},{40,72},{48,80},{56,88},{... | collective-permute-start | bytes 393224 | tf_op jit(solution)/shard_map/ppermute | solution.py:232
  43.8 3.2 %collective-permute-done.5.y4_ref = f32[2,128,128]{2,1,0:T(8,128)S(1)} collective-permute-done((f32[2,128,128]{2,1,0:T(8,128)S(1)}, f32[2,128,128]{2,1,0:T(8,128)S(1)}, u32[]{:S(2)}, u32[]{:S(2)}) %collective-permute-start.5) | collective-permute-done | bytes 131104 | tf_op jit(solution)/shard_map/ppermute | solution.py:232
  46.9 0.0 collective-permute-done.6.rest_0_.y1_ref.refs_5_
  47.0 0.0 copy-start.2
  47.0 0.0 copy-start.3
  47.0 0.0 copy-start.5
  47.0 1.9 %collective-permute-start.9 = (f32[2,2,128,128]{3,2,1,0:T(8,128)S(1)}, f32[2,2,128,128]{3,2,1,0:T(8,128)S(1)}, u32[]{:S(2)}, u32[]{:S(2)}) collective-permute-start(f32[2,2,128,128]{3,2,1,0:T(8,128)S(1)} %pack.1.after.rest_0_.refs_7_), channel_id=1, source_target_pairs={{0,24},{8,16},{16,8},{24,0},{32,56},{40,48},{48,40},{56,32},{64,88... | collective-permute-start | bytes 786440 | tf_op jit(solution)/shard_map/ppermute | solution.py:232
  48.9 1.6 %collective-permute-start.8 = (f32[2,2,128,128]{3,2,1,0:T(8,128)S(1)}, f32[2,2,128,128]{3,2,1,0:T(8,128)S(1)}, u32[]{:S(2)}, u32[]{:S(2)}) collective-permute-start(f32[2,2,128,128]{3,2,1,0:T(8,128)S(1)} %pack.1.after.rest_0_.refs_7_), channel_id=1, source_target_pairs={{0,16},{8,24},{16,0},{24,8},{32,48},{40,56},{48,32},{56,40},{64,80... | collective-permute-start | bytes 786440 | tf_op jit(solution)/shard_map/ppermute | solution.py:232
  50.5 0.7 collective-permute-start.7
  51.2 9.3 %query.1 = (f32[1024,1024]{1,0:T(8,128)S(1)}, f32[1024,128]{1,0:T(8,128)S(1)}) custom-call(f32[2,2,128,128]{3,2,1,0:T(8,128)S(1)} %pack.1.after.rest_0_.refs_7_, bf16[1024,1024]{1,0:T(8,128)(2,1)} %q_ref.11, bf16[1024,1024]{1,0:T(8,128)(2,1)} %refs_1_.7, bf16[1024,1024]{1,0:T(8,128)(2,1)} %refs_2_.7, bf16[1024,1024]{1,0:T(8,128)(2,1)} %g_ref.11, ...), custom_call_target="tpu_custom_call" | custom-call | flops 100000000 | bytes 1048576 | tf_op jit(solution)/shard_map/query/pallas_call | solution.py:330
  60.5 0.0 collective-permute-done.9.rest_3_.refs_10_
  60.5 0.0 collective-permute-done.8.rest_2_.refs_9_
  60.5 0.0 collective-permute-done.7.rest_1_.refs_8_
  60.5 0.0 copy-done.2
  60.5 0.0 copy-done.3
  60.6 0.0 copy-start
  60.6 0.0 copy-start.1
  60.6 6.9 %reads.1 = (bf16[1024,1024]{1,0:T(8,128)(2,1)}, f32[8,256]{1,0:T(8,128)S(1)}) custom-call(s32[1]{0:T(128)S(6)} %copy.26.reach.refs_0_, bf16[1024,1024]{1,0:T(8,128)(2,1)S(1)} %copy-done.2, bf16[1024,1024]{1,0:T(8,128)(2,1)S(1)} %copy-done.3, f32[1024,8]{1,0:T(8,128)S(1)} %bitcast.7, f32[1024,1024]{1,0:T(8,128)S(1)} %get-tuple-element.62.qn_ref, ...), custom_call_target="tpu_custom_call" | custom-call | flops 100000000 | bytes 1048576 | tf_op jit(solution)/shard_map/reads/pallas_call | solution.py:341
  67.4 0.1 collective-permute-start.10
  67.5 1.6 %returns.4 = (bf16[1024,1024]{1,0:T(8,128)(2,1)}, bf16[1024,1024]{1,0:T(8,128)(2,1)}) custom-call(s32[1]{0:T(128)S(6)} %copy.26.reach.refs_0_, bf16[1024,1024]{1,0:T(8,128)(2,1)S(1)} %copy-done, bf16[1024,1024]{1,0:T(8,128)(2,1)S(1)} %copy-done.1, f32[1024,256]{1,0:T(8,128)S(1)} %get-tuple-element.52.after.refs_3_, ...), custom_call_target="tpu_custom_call" | custom-call | flops 100000000 | bytes 1048576 | tf_op jit(solution)/shard_map/returns/pallas_call | solution.py:364
  69.1 0.0 collective-permute-done.10
  69.2 2.8 %collective-permute-start.13 = (f32[8,256]{1,0:T(8,128)S(1)}, f32[8,256]{1,0:T(8,128)S(1)}, u32[]{:S(2)}, u32[]{:S(2)}) collective-permute-start(f32[8,256]{1,0:T(8,128)S(1)} %add.30), channel_id=1, source_target_pairs={{0,6},{1,7},{2,4},{3,5},{4,2},{5,3},{6,0},{7,1},{8,14},{9,15},{10,... | collective-permute-start | bytes 24584 | tf_op jit(solution)/shard_map/ppermute | solution.py:232
  72.0 0.8 collective-permute-start.12
  72.8 0.5 collective-permute-start.11
  73.3 1.5 %returns.5 = (bf16[1024,1024]{1,0:T(8,128)(2,1)}, bf16[1024,1024]{1,0:T(8,128)(2,1)}) custom-call(s32[1]{0:T(128)S(6)} %copy.26.reach.refs_0_, bf16[1024,1024]{1,0:T(8,128)(2,1)S(1)} %copy-done, bf16[1024,1024]{1,0:T(8,128)(2,1)S(1)} %copy-done.1, f32[1024,256]{1,0:T(8,128)S(1)} %get-tuple-element.53.after.refs_3_, ...), custom_call_target="tpu_custom_call", output_to_operand_aliasing={{0}: (11, {}), {1}: (12, {})} | custom-call | flops 100000000 | bytes 1048576 | tf_op jit(solution)/shard_map/returns/pallas_call | solution.py:364
  74.8 0.0 collective-permute-done.13
  74.9 2.3 %collective-permute-done.12 = f32[8,256]{1,0:T(8,128)S(1)} collective-permute-done((f32[8,256]{1,0:T(8,128)S(1)}, f32[8,256]{1,0:T(8,128)S(1)}, u32[]{:S(2)}, u32[]{:S(2)}) %collective-permute-start.12) | collective-permute-done | bytes 8224 | tf_op jit(solution)/shard_map/ppermute | solution.py:232
  77.1 0.0 collective-permute-done.11
  77.2 1.9 %collective-permute-start.16 = (f32[8,256]{1,0:T(8,128)S(1)}, f32[8,256]{1,0:T(8,128)S(1)}, u32[]{:S(2)}, u32[]{:S(2)}) collective-permute-start(f32[8,256]{1,0:T(8,128)S(1)} %add_add_fusion.1), channel_id=1, source_target_pairs={{0,24},{8,16},{16,8},{24,0},{32,56},{40,48},{48,40},{56,32},{64,88... | collective-permute-start | bytes 24584 | tf_op jit(solution)/shard_map/ppermute | solution.py:232
  79.0 1.6 %collective-permute-start.15 = (f32[8,256]{1,0:T(8,128)S(1)}, f32[8,256]{1,0:T(8,128)S(1)}, u32[]{:S(2)}, u32[]{:S(2)}) collective-permute-start(f32[8,256]{1,0:T(8,128)S(1)} %add_add_fusion.1), channel_id=1, source_target_pairs={{0,16},{8,24},{16,0},{24,8},{32,48},{40,56},{48,32},{56,40},{64,80... | collective-permute-start | bytes 24584 | tf_op jit(solution)/shard_map/ppermute | solution.py:232
  80.7 0.7 collective-permute-start.14
  81.3 1.5 %returns.6 = (bf16[1024,1024]{1,0:T(8,128)(2,1)}, bf16[1024,1024]{1,0:T(8,128)(2,1)}) custom-call(s32[1]{0:T(128)S(6)} %copy.26.reach.refs_0_, bf16[1024,1024]{1,0:T(8,128)(2,1)S(1)} %copy-done, bf16[1024,1024]{1,0:T(8,128)(2,1)S(1)} %copy-done.1, f32[1024,256]{1,0:T(8,128)S(1)} %get-tuple-element.56.after.refs_3_, ...), custom_call_target="tpu_custom_call", output_to_operand_aliasing={{0}: (11, {}), {1}: (12, {})} | custom-call | flops 100000000 | bytes 1048576 | tf_op jit(solution)/shard_map/returns/pallas_call | solution.py:364
  82.9 0.0 collective-permute-done.16
  82.9 1.3 %collective-permute-done.15 = f32[8,256]{1,0:T(8,128)S(1)} collective-permute-done((f32[8,256]{1,0:T(8,128)S(1)}, f32[8,256]{1,0:T(8,128)S(1)}, u32[]{:S(2)}, u32[]{:S(2)}) %collective-permute-start.15) | collective-permute-done | bytes 8224 | tf_op jit(solution)/shard_map/ppermute | solution.py:232
  84.2 0.1 collective-permute-done.14
  84.3 3.0 %collective-permute-start.19 = (f32[8,256]{1,0:T(8,128)S(1)}, f32[8,256]{1,0:T(8,128)S(1)}, u32[]{:S(2)}, u32[]{:S(2)}) collective-permute-start(f32[8,256]{1,0:T(8,128)S(1)} %add_add_fusion), channel_id=1, source_target_pairs={{0,96},{8,104},{16,112},{24,120},{32,64},{40,72},{48,80},{56,88},{... | collective-permute-start | bytes 24584 | tf_op jit(solution)/shard_map/ppermute | solution.py:232
  87.3 0.0 collective-permute-start.18
  87.3 1.1 %collective-permute-start.17 = (f32[8,256]{1,0:T(8,128)S(1)}, f32[8,256]{1,0:T(8,128)S(1)}, u32[]{:S(2)}, u32[]{:S(2)}) collective-permute-start(f32[8,256]{1,0:T(8,128)S(1)} %add_add_fusion), channel_id=1, source_target_pairs={{0,32},{8,40},{16,48},{24,56},{32,0},{40,8},{48,16},{56,24},{64,96... | collective-permute-start | bytes 24584 | tf_op jit(solution)/shard_map/ppermute | solution.py:232
  88.4 1.5 %returns.7 = (bf16[1024,1024]{1,0:T(8,128)(2,1)}, bf16[1024,1024]{1,0:T(8,128)(2,1)}) custom-call(s32[1]{0:T(128)S(6)} %copy.26.reach.refs_0_, bf16[1024,1024]{1,0:T(8,128)(2,1)S(1)} %copy-done, bf16[1024,1024]{1,0:T(8,128)(2,1)S(1)} %copy-done.1, ...), custom_call_target="tpu_custom_call", output_to_operand_aliasing={{0}: (11, {}), {1}: (12, {})} | custom-call | flops 100000000 | bytes 1048576 | tf_op jit(solution)/shard_map/returns/pallas_call | solution.py:364
  89.9 0.0 collective-permute-done.19
  89.9 2.6 %collective-permute-done.18 = f32[8,256]{1,0:T(8,128)S(1)} collective-permute-done((f32[8,256]{1,0:T(8,128)S(1)}, f32[8,256]{1,0:T(8,128)S(1)}, u32[]{:S(2)}, u32[]{:S(2)}) %collective-permute-start.18) | collective-permute-done | bytes 8224 | tf_op jit(solution)/shard_map/ppermute | solution.py:232
  92.5 0.0 collective-permute-done.17
  92.5 0.6 fusion.1
  (10 shorter events, 0.1 us)
Async XLA Ops:
  1.3 0.7 copy-start.4
  2.0 0.7 copy-start.6
  8.8 16.4 %collective-permute-start = (f32[2,2,2,128,128]{4,3,2,1,0:T(8,128)}, f32[2,2,2,128,128]{4,3,2,1,0:T(8,128)S(1)}, u32[]{:S(2)}, u32[]{:S(2)}) collective-permute-start(f32[2,2,2,128,128]{4,3,2,1,0:T(8,128)} %get-tuple-element.50), channel_id=1, source_target_pairs={{0,24},{8,16},{16,8},{24,0},{32,56},{40,48},{48,40},{56,32},{64,88... | collective-permute-start | bytes 1572872 | tf_op jit(solution)/shard_map/ppermute | solution.py:232
  13.1 13.4 %collective-permute-start.1 = (f32[8,128,128]{2,1,0:T(8,128)S(1)}, f32[8,128,128]{2,1,0:T(8,128)S(1)}, u32[]{:S(2)}, u32[]{:S(2)}) collective-permute-start(f32[8,128,128]{2,1,0:T(8,128)S(1)} %get-tuple-element.51.near_ref), channel_id=1, source_target_pairs={{0,8},{8,0},{16,24},{24,16},{32,40},{40,32},{48,56},{56,48},{64,72... | collective-permute-start | bytes 1572872 | tf_op jit(solution)/shard_map/ppermute | solution.py:232
  26.6 6.9 %collective-permute-start.2 = (f32[2,2,128,128]{3,2,1,0:T(8,128)S(1)}, f32[2,2,128,128]{3,2,1,0:T(8,128)S(1)}, u32[]{:S(2)}, u32[]{:S(2)}) collective-permute-start(f32[2,2,128,128]{3,2,1,0:T(8,128)S(1)} %get-tuple-element.55), channel_id=1, source_target_pairs={{0,8},{8,0},{16,24},{24,16},{32,40},{40,32},{48,56},{56,48},{64,72... | collective-permute-start | bytes 786440 | tf_op jit(solution)/shard_map/ppermute | solution.py:232
  26.9 13.7 %collective-permute-start.4 = (f32[8,128,128]{2,1,0:T(8,128)S(1)}, f32[8,128,128]{2,1,0:T(8,128)S(1)}, u32[]{:S(2)}, u32[]{:S(2)}) collective-permute-start(f32[8,128,128]{2,1,0:T(8,128)S(1)} %get-tuple-element.59), channel_id=1, source_target_pairs={{0,24},{8,16},{16,8},{24,0},{32,56},{40,48},{48,40},{56,32},{64,88... | collective-permute-start | bytes 1572872 | tf_op jit(solution)/shard_map/ppermute | solution.py:232
  33.5 13.4 %collective-permute-start.6 = (f32[8,128,128]{2,1,0:T(8,128)S(1)}, f32[8,128,128]{2,1,0:T(8,128)S(1)}, u32[]{:S(2)}, u32[]{:S(2)}) collective-permute-start(f32[8,128,128]{2,1,0:T(8,128)S(1)} %get-tuple-element.61), channel_id=1, source_target_pairs={{0,8},{8,0},{16,24},{24,16},{32,40},{40,32},{48,56},{56,48},{64,72... | collective-permute-start | bytes 1572872 | tf_op jit(solution)/shard_map/ppermute | solution.py:232
  34.2 6.4 %collective-permute-start.3 = (f32[2,2,128,128]{3,2,1,0:T(8,128)S(1)}, f32[2,2,128,128]{3,2,1,0:T(8,128)S(1)}, u32[]{:S(2)}, u32[]{:S(2)}) collective-permute-start(f32[2,2,128,128]{3,2,1,0:T(8,128)S(1)} %get-tuple-element.58.after.rows_ref), channel_id=1, source_target_pairs={{0,32},{8,40},{16,48},{24,56},{32,0},{40,8},{48,16},{56,24},{64,96... | collective-permute-start | bytes 786440 | tf_op jit(solution)/shard_map/ppermute | solution.py:232
  40.7 6.3 %collective-permute-start.5 = (f32[2,128,128]{2,1,0:T(8,128)S(1)}, f32[2,128,128]{2,1,0:T(8,128)S(1)}, u32[]{:S(2)}, u32[]{:S(2)}) collective-permute-start(f32[2,128,128]{2,1,0:T(8,128)S(1)} %cross.1), channel_id=1, source_target_pairs={{0,96},{8,104},{16,112},{24,120},{32,64},{40,72},{48,80},{56,88},{... | collective-permute-start | bytes 393224 | tf_op jit(solution)/shard_map/ppermute | solution.py:232
  47.0 13.6 %copy-start.2 = (bf16[1024,1024]{1,0:T(8,128)(2,1)S(1)}, bf16[1024,1024]{1,0:T(8,128)(2,1)}, u32[]{:S(2)}) copy-start(bf16[1024,1024]{1,0:T(8,128)(2,1)} %q_ref.11) | copy-start | bytes 6291460
  47.0 13.6 %copy-start.3 = (bf16[1024,1024]{1,0:T(8,128)(2,1)S(1)}, bf16[1024,1024]{1,0:T(8,128)(2,1)}, u32[]{:S(2)}) copy-start(bf16[1024,1024]{1,0:T(8,128)(2,1)} %g_ref.11) | copy-start | bytes 6291460
  47.0 13.6 %copy-start.5 = (s32[1024]{0:T(1024)S(1)}, s32[1024]{0:T(1024)}, u32[]{:S(2)}) copy-start(s32[1024]{0:T(1024)} %param.12) | copy-start | bytes 12292
  47.0 13.5 %collective-permute-start.9 = (f32[2,2,128,128]{3,2,1,0:T(8,128)S(1)}, f32[2,2,128,128]{3,2,1,0:T(8,128)S(1)}, u32[]{:S(2)}, u32[]{:S(2)}) collective-permute-start(f32[2,2,128,128]{3,2,1,0:T(8,128)S(1)} %pack.1.after.rest_0_.refs_7_), channel_id=1, source_target_pairs={{0,24},{8,16},{16,8},{24,0},{32,56},{40,48},{48,40},{56,32},{64,88... | collective-permute-start | bytes 786440 | tf_op jit(solution)/shard_map/ppermute | solution.py:232
  48.9 11.6 %collective-permute-start.8 = (f32[2,2,128,128]{3,2,1,0:T(8,128)S(1)}, f32[2,2,128,128]{3,2,1,0:T(8,128)S(1)}, u32[]{:S(2)}, u32[]{:S(2)}) collective-permute-start(f32[2,2,128,128]{3,2,1,0:T(8,128)S(1)} %pack.1.after.rest_0_.refs_7_), channel_id=1, source_target_pairs={{0,16},{8,24},{16,0},{24,8},{32,48},{40,56},{48,32},{56,40},{64,80... | collective-permute-start | bytes 786440 | tf_op jit(solution)/shard_map/ppermute | solution.py:232
  50.5 10.0 %collective-permute-start.7 = (f32[2,2,128,128]{3,2,1,0:T(8,128)S(1)}, f32[2,2,128,128]{3,2,1,0:T(8,128)S(1)}, u32[]{:S(2)}, u32[]{:S(2)}) collective-permute-start(f32[2,2,128,128]{3,2,1,0:T(8,128)S(1)} %pack.1.after.rest_0_.refs_7_), channel_id=1, source_target_pairs={{0,8},{8,0},{16,24},{24,16},{32,40},{40,32},{48,56},{56,48},{64,72... | collective-permute-start | bytes 786440 | tf_op jit(solution)/shard_map/ppermute | solution.py:232
  60.6 7.0 %copy-start = (bf16[1024,1024]{1,0:T(8,128)(2,1)S(1)}, bf16[1024,1024]{1,0:T(8,128)(2,1)}, u32[]{:S(2)}) copy-start(bf16[1024,1024]{1,0:T(8,128)(2,1)} %refs_1_.7) | copy-start | bytes 6291460
  60.6 7.0 %copy-start.1 = (bf16[1024,1024]{1,0:T(8,128)(2,1)S(1)}, bf16[1024,1024]{1,0:T(8,128)(2,1)}, u32[]{:S(2)}) copy-start(bf16[1024,1024]{1,0:T(8,128)(2,1)} %refs_2_.7) | copy-start | bytes 6291460
  67.4 1.7 %collective-permute-start.10 = (f32[8,256]{1,0:T(8,128)S(1)}, f32[8,256]{1,0:T(8,128)S(1)}, u32[]{:S(2)}, u32[]{:S(2)}) collective-permute-start(f32[8,256]{1,0:T(8,128)S(1)} %get-tuple-element.65), channel_id=1, source_target_pairs={{0,1},{1,0},{2,3},{3,2},{4,5},{5,4},{6,7},{7,6},{8,9},{9,8},{10,11... | collective-permute-start | bytes 24584 | tf_op jit(solution)/shard_map/ppermute | solution.py:232
  69.2 5.7 %collective-permute-start.13 = (f32[8,256]{1,0:T(8,128)S(1)}, f32[8,256]{1,0:T(8,128)S(1)}, u32[]{:S(2)}, u32[]{:S(2)}) collective-permute-start(f32[8,256]{1,0:T(8,128)S(1)} %add.30), channel_id=1, source_target_pairs={{0,6},{1,7},{2,4},{3,5},{4,2},{5,3},{6,0},{7,1},{8,14},{9,15},{10,... | collective-permute-start | bytes 24584 | tf_op jit(solution)/shard_map/ppermute | solution.py:232
  72.0 5.2 %collective-permute-start.12 = (f32[8,256]{1,0:T(8,128)S(1)}, f32[8,256]{1,0:T(8,128)S(1)}, u32[]{:S(2)}, u32[]{:S(2)}) collective-permute-start(f32[8,256]{1,0:T(8,128)S(1)} %add.30), channel_id=1, source_target_pairs={{0,4},{1,5},{2,6},{3,7},{4,0},{5,1},{6,2},{7,3},{8,12},{9,13},{10,... | collective-permute-start | bytes 24584 | tf_op jit(solution)/shard_map/ppermute | solution.py:232
  72.8 4.4 %collective-permute-start.11 = (f32[8,256]{1,0:T(8,128)S(1)}, f32[8,256]{1,0:T(8,128)S(1)}, u32[]{:S(2)}, u32[]{:S(2)}) collective-permute-start(f32[8,256]{1,0:T(8,128)S(1)} %add.30), channel_id=1, source_target_pairs={{0,2},{1,3},{2,0},{3,1},{4,6},{5,7},{6,4},{7,5},{8,10},{9,11},{10,... | collective-permute-start | bytes 24584 | tf_op jit(solution)/shard_map/ppermute | solution.py:232
  77.2 5.7 %collective-permute-start.16 = (f32[8,256]{1,0:T(8,128)S(1)}, f32[8,256]{1,0:T(8,128)S(1)}, u32[]{:S(2)}, u32[]{:S(2)}) collective-permute-start(f32[8,256]{1,0:T(8,128)S(1)} %add_add_fusion.1), channel_id=1, source_target_pairs={{0,24},{8,16},{16,8},{24,0},{32,56},{40,48},{48,40},{56,32},{64,88... | collective-permute-start | bytes 24584 | tf_op jit(solution)/shard_map/ppermute | solution.py:232
  79.0 5.2 %collective-permute-start.15 = (f32[8,256]{1,0:T(8,128)S(1)}, f32[8,256]{1,0:T(8,128)S(1)}, u32[]{:S(2)}, u32[]{:S(2)}) collective-permute-start(f32[8,256]{1,0:T(8,128)S(1)} %add_add_fusion.1), channel_id=1, source_target_pairs={{0,16},{8,24},{16,0},{24,8},{32,48},{40,56},{48,32},{56,40},{64,80... | collective-permute-start | bytes 24584 | tf_op jit(solution)/shard_map/ppermute | solution.py:232
  80.7 3.7 %collective-permute-start.14 = (f32[8,256]{1,0:T(8,128)S(1)}, f32[8,256]{1,0:T(8,128)S(1)}, u32[]{:S(2)}, u32[]{:S(2)}) collective-permute-start(f32[8,256]{1,0:T(8,128)S(1)} %add_add_fusion.1), channel_id=1, source_target_pairs={{0,8},{8,0},{16,24},{24,16},{32,40},{40,32},{48,56},{56,48},{64,72... | collective-permute-start | bytes 24584 | tf_op jit(solution)/shard_map/ppermute | solution.py:232
  84.3 5.6 %collective-permute-start.19 = (f32[8,256]{1,0:T(8,128)S(1)}, f32[8,256]{1,0:T(8,128)S(1)}, u32[]{:S(2)}, u32[]{:S(2)}) collective-permute-start(f32[8,256]{1,0:T(8,128)S(1)} %add_add_fusion), channel_id=1, source_target_pairs={{0,96},{8,104},{16,112},{24,120},{32,64},{40,72},{48,80},{56,88},{... | collective-permute-start | bytes 24584 | tf_op jit(solution)/shard_map/ppermute | solution.py:232
  87.3 5.2 %collective-permute-start.18 = (f32[8,256]{1,0:T(8,128)S(1)}, f32[8,256]{1,0:T(8,128)S(1)}, u32[]{:S(2)}, u32[]{:S(2)}) collective-permute-start(f32[8,256]{1,0:T(8,128)S(1)} %add_add_fusion), channel_id=1, source_target_pairs={{0,64},{8,72},{16,80},{24,88},{32,96},{40,104},{48,112},{56,120},{... | collective-permute-start | bytes 24584 | tf_op jit(solution)/shard_map/ppermute | solution.py:232
  87.3 5.2 %collective-permute-start.17 = (f32[8,256]{1,0:T(8,128)S(1)}, f32[8,256]{1,0:T(8,128)S(1)}, u32[]{:S(2)}, u32[]{:S(2)}) collective-permute-start(f32[8,256]{1,0:T(8,128)S(1)} %add_add_fusion), channel_id=1, source_target_pairs={{0,32},{8,40},{16,48},{24,56},{32,0},{40,8},{48,16},{56,24},{64,96... | collective-permute-start | bytes 24584 | tf_op jit(solution)/shard_map/ppermute | solution.py:232

commit v5 on v4

--- a/solution.py
+++ b/solution.py
@@ -36,7 +36,11 @@
     return jnp.where(ids == index_row, 1.0, 0.0).astype(bf16)
 
 
-def states_kernel(reach, index_ref, table_ref, q_hbm, k_hbm, v_hbm, g_hbm, w_ref, near1_ref, near2_ref, keep_ref, send_ref, buf, table, sem):
+def states_kernel(
+    reach, index_ref, table_ref, q_hbm, k_hbm, v_hbm, g_hbm,
+    w_ref, near1_ref, near2_ref, keep_ref, send_ref,
+    buf, table, sem,
+):
     far_refs = (keep_ref.at[0], keep_ref.at[1], send_ref.at[1], send_ref.at[0])
     sources = (q_hbm, k_hbm, v_hbm, g_hbm)
     wide = buf.shape[-1]
@@ -74,53 +78,49 @@
             far_refs[j][1, i] = xs[3]
 
 
-def causal_mask(flip_sides):
+def group_kernel(after, q_ref, k_ref, v_ref, g_ref, w_ref, qn_ref, kn_ref, vn_ref, lam_ref):
     rows = lax.broadcasted_iota(jnp.int32, (CHUNK, CHUNK), 0)
     cols = lax.broadcasted_iota(jnp.int32, (CHUNK, CHUNK), 1)
-    return rows <= cols if flip_sides else rows >= cols
-
-
-def query_kernel(after, q_ref, k_ref, v_ref, g_ref, w_ref, out_ref, lam_ref):
+    causal = rows >= cols
+    count = q_ref.shape[0] // CHUNK
+
     @pl.when(pl.program_id(0) == 0)
     def _():
         lam_ref[...] = jnp.zeros_like(lam_ref)
 
-    causal = causal_mask(False)
     state = jnp.zeros((DH, DH), f32)
-    count = q_ref.shape[0] // CHUNK
+    held = []
     for i in range(count):
         at = pl.ds(i * CHUNK, CHUNK)
         k, v, g = k_ref[at, :], v_ref[at, :], g_ref[at, :]
-        near = jnp.where(causal, mm(g, v, 1, 1), 0.0).astype(bf16)
-        u = mm(near, k, 1, 0)
+        q = q_ref[at, :].astype(f32)
+        weight = w_ref[at, 0:1]
+        scaled = (q * weight).astype(bf16)
+        grad_probs = jnp.where(causal, mm(g, v, 1, 1), 0.0).astype(bf16)
+        scores = jnp.where(causal, mm(scaled, k, 1, 1), 0.0).astype(bf16)
+        u = mm(grad_probs, k, 1, 0)
         if i > 0:
             u = u + mm(g, state.astype(bf16), 1, 0)
-        lam_ref[at, :] += q_ref[at, :].astype(f32) * u
-        out_ref[at, :] = (SCALE * w_ref[at, 0:1]) * u
+        lam_ref[at, :] += q * u
+        qn_ref[at, :] = (SCALE * weight) * u
         if i < count - 1:
             state = state + mm(v, k, 0, 0)
-
-
-def key_value_kernel(after, q_ref, k_ref, v_ref, g_ref, w_ref, key_ref, value_ref):
-    causal = causal_mask(True)
+        held.append((scaled, grad_probs, scores))
     state = jnp.zeros((DH, DH), f32)
-    count = q_ref.shape[0] // CHUNK
     for i in reversed(range(count)):
         at = pl.ds(i * CHUNK, CHUNK)
         k, v, g = k_ref[at, :], v_ref[at, :], g_ref[at, :]
-        q = (q_ref[at, :].astype(f32) * w_ref[at, 0:1]).astype(bf16)
-        near_key = jnp.where(causal, mm(v, g, 1, 1), 0.0).astype(bf16)
-        near_value = jnp.where(causal, mm(k, q, 1, 1), 0.0).astype(bf16)
-        key = mm(near_key, q, 1, 0)
-        value = mm(near_value, g, 1, 0)
+        scaled, grad_probs, scores = held[i]
+        key = mm(grad_probs, scaled, 0, 0)
+        value = mm(scores, g, 0, 0)
         if i < count - 1:
-            held = state.astype(bf16)
-            key = key + mm(v, held, 1, 0)
-            value = value + mm(k, held, 1, 1)
-        key_ref[at, :] = SCALE * key
-        value_ref[at, :] = SCALE * value
+            rounded = state.astype(bf16)
+            key = key + mm(v, rounded, 1, 0)
+            value = value + mm(k, rounded, 1, 1)
+        kn_ref[at, :] = SCALE * key
+        vn_ref[at, :] = SCALE * value
         if i > 0:
-            state = state + mm(g, q, 0, 0)
+            state = state + mm(g, scaled, 0, 0)
 
 
 def level_states(keep, y1_ref, y2_ref, y34_refs, bits, head, j, i):
@@ -128,41 +128,77 @@
     return [jnp.where(bits[l] == keep, ys[l], 0.0) for l in range(4)]
 
 
-def reads_kernel(reach, q_ref, g_ref, w_ref, qn_ref, lam0_ref, index_ref, y1_ref, y2_ref, *rest):
+def reads_tile(at, levels, q_ref, g_ref, w_ref, st, old, new_ref):
+    tile = at.size
+    w = w_ref[at, :]
+    wide = [jnp.broadcast_to(SCALE * w[:, l : l + 1], (tile, DH)) for l in levels]
+    acc = [None] * len(levels)
+    for h in range(st.shape[0]):
+        c = slice(h * DH, (h + 1) * DH)
+        reads = mm(g_ref[at, c], st[h], 1, 0)
+        q = q_ref[at, c].astype(f32)
+        total = old(h)
+        for i in range(len(levels)):
+            read = reads[:, i * DH : (i + 1) * DH]
+            product = q * read
+            acc[i] = product if acc[i] is None else acc[i] + product
+            total = total + wide[i] * read
+        new_ref[at, c] = total.astype(new_ref.dtype)
+    return acc
+
+
+def near_reads_kernel(after, reach, q_ref, g_ref, w_ref, y1_ref, y2_ref, *rest):
+    count = (len(rest) - 3) // 2
+    qn_refs, lam_refs, (out_ref, lam_ref, st) = rest[:count], rest[count : 2 * count], rest[2 * count :]
+    heads = y1_ref.shape[0]
+    each = heads // count
+    bits, spot = place()
+    for h in range(heads):
+        parts = [jnp.where(b > 0, y_ref[h], 0.0) for b, y_ref in zip(bits, (y1_ref, y2_ref))]
+        st[h] = jnp.concatenate(parts, 1).astype(bf16)
+    lane = lax.broadcasted_iota(jnp.int32, (1, DH), 1)
+    for t in range(q_ref.shape[0] // CHUNK):
+        at = pl.ds(t * CHUNK, CHUNK)
+
+        def old(h):
+            i = h % each
+            return qn_refs[h // each][at, i * DH : (i + 1) * DH]
+
+        acc = reads_tile(at, (1, 2), q_ref, g_ref, w_ref, st, old, out_ref)
+        lam0 = lam_refs[0][at, :]
+        for ref in lam_refs[1:]:
+            lam0 = lam0 + ref[at, :]
+        lam = jnp.zeros((CHUNK, DH), f32)
+        for l, x in enumerate([lam0] + acc):
+            here = (lane == l) & (reach[0] >= l)
+            lam = jnp.where(here, jnp.sum(x, 1, keepdims=True), lam)
+        lam_ref[at, :] = lam
+
+
+def reads_kernel(reach, q_ref, g_ref, w_ref, qn_ref, lam_ref, index_ref, *rest):
     y34_refs, (out_hbm, table_ref, st, out_buf, sem) = rest[:4], rest[4:]
-    length = q_ref.shape[0]
-    heads = y1_ref.shape[0]
+    heads = st.shape[0]
     each = heads // 4
-    tile = CHUNK
     bits, spot = place()
     for j in range(4):
         for i in range(each):
             head = (spot ^ j) * each + i
-            parts = level_states(1, y1_ref, y2_ref, y34_refs, bits, head, j, i)
+            parts = [jnp.where(bits[l + 2] > 0, y34_refs[j][l, i], 0.0) for l in range(2)]
             st[head] = jnp.concatenate(parts, 1).astype(bf16)
     lane = lax.broadcasted_iota(jnp.int32, (1, DH), 1)
     table = None
     copies = []
-    for t in range(length // tile):
-        at = pl.ds(t * tile, tile)
-        w = w_ref[at, :]
-        wide = [jnp.broadcast_to(SCALE * w[:, l : l + 1], (tile, DH)) for l in range(1, 5)]
-        acc = [None] * 4
-        for h in range(heads):
-            c = slice(h * DH, (h + 1) * DH)
-            reads = mm(g_ref[at, c], st[h], 1, 0)
-            q = q_ref[at, c].astype(f32)
-            total = qn_ref[at, c]
-            for l in range(4):
-                read = reads[:, l * DH : (l + 1) * DH]
-                product = q * read
-                acc[l] = product if acc[l] is None else acc[l] + product
-                total = total + wide[l] * read
-            out_buf[at, c] = total.astype(bf16)
+    for t in range(q_ref.shape[0] // CHUNK):
+        at = pl.ds(t * CHUNK, CHUNK)
+
+        def old(h):
+            return qn_ref[at, h * DH : (h + 1) * DH]
+
+        acc = reads_tile(at, (3, 4), q_ref, g_ref, w_ref, st, old, out_buf)
         copies.append(pltpu.make_async_copy(out_buf.at[at, :], out_hbm.at[at, :], sem.at[t]))
         copies[-1].start()
-        lam = jnp.zeros((tile, DH), f32)
-        for l, x in enumerate([lam0_ref[at, :]] + acc):
+        lam = lam_ref[at, :]
+        for l, x in zip((3, 4), acc):
             here = (lane == l) & (reach[0] >= l)
             lam = jnp.where(here, jnp.sum(x, 1, keepdims=True), lam)
         lam = (SCALE * lam).T[:8]
@@ -279,17 +315,17 @@
     )
     tokens = [in_hbm(x) for x in (queries, keys, values, out_grad)]
 
-    def key_value_part(order, start):
+    def near_part(after, start):
         return pl.pallas_call(
-            key_value_kernel,
+            group_kernel,
             grid=(each,),
             in_specs=[anywhere] + [token_spec(start)] * 4 + [fixed((length, 8))],
-            out_specs=[token_spec(0)] * 2,
-            out_shape=[sds((length, each * DH), f32)] * 2,
+            out_specs=[token_spec(0)] * 3 + [fixed((length, DH))],
+            out_shape=[sds((length, each * DH), f32)] * 3 + [sds((length, DH), f32)],
             compiler_params=near_params,
             cost_estimate=cost,
-            name="key_value",
-        )(order, *tokens, w_cols)
+            name="group",
+        )(after, *tokens, w_cols)
 
     def local_step(kernel, ins, afters, outs, name, aliases=None):
         return pl.pallas_call(
@@ -305,8 +341,8 @@
 
     quarter = keep.shape[1:]
     got, near_got = flip(send, "seq", 3), flip(near2, "seq", 1)
-    near_parts = [key_value_part(keep, 0)]
-    near_parts.append(key_value_part(near_parts[0][0], each))
+    near_parts = [near_part(keep, 0)]
+    near_parts.append(near_part(near_parts[0][0], each))
     own, send, near_sum = local_step(
         pair_kernel,
         [keep, got, near2, near_got],
@@ -315,47 +351,50 @@
         "pair",
     )
     got, y2 = flip(send, "seq", 1), flip(near_sum, "seq", 3)
-    near_parts.append(key_value_part(own, 2 * each))
+    near_parts.append(near_part(own, 2 * each))
     rows, near = local_step(
         rows_kernel, [own, got], [near_parts[2][0], near], [quarter, near.shape], "rows", {3: 1}
     )
     other, y1 = flip(rows, "seq", 4), flip(near, "seq", 1)
-    near_parts.append(key_value_part(rows, 3 * each))
+    near_parts.append(near_part(rows, 3 * each))
     (far4,) = local_step(
         cross_kernel, [rows, other], [y2, near_parts[3][0]], [quarter[1:]], "cross"
     )
     y4 = flip(far4, "seq", 12)
     (y34,) = local_step(pack_kernel, [other, y4], [y1], [quarter], "pack")
     y34s = [y34] + [flip(y34, "seq", m) for m in (1, 2, 3)]
-    qn, lam0 = pl.pallas_call(
-        query_kernel,
-        grid=(heads,),
-        in_specs=[anywhere] + [token_spec(0)] * 4 + [fixed((length, 8))],
-        out_specs=[token_spec(0), fixed((length, DH))],
+    qn, lam = pl.pallas_call(
+        near_reads_kernel,
+        in_specs=[anywhere, scalar] + [whole] * (5 + 2 * len(near_parts)),
+        out_specs=[whole] * 2,
         out_shape=[sds((length, heads * DH), f32), sds((length, DH), f32)],
-        compiler_params=near_params,
+        scratch_shapes=[pltpu.VMEM((heads, DH, 2 * DH), bf16)],
+        compiler_params=limit(16),
         cost_estimate=cost,
-        name="query",
-    )(y34, *tokens, w_cols)
+        name="near_reads",
+    )(
+        y34, reach, queries, out_grad, w_cols, y1, y2,
+        *[p[0] for p in near_parts], *[p[3] for p in near_parts],
+    )
 
     query_grad, total = pl.pallas_call(
         reads_kernel,
-        in_specs=[scalar] + [whole] * 12,
+        in_specs=[scalar] + [whole] * 10,
         out_specs=[anywhere, whole],
         out_shape=[sds((length, heads * DH), bf16), sds((8, names), f32)],
         scratch_shapes=[
-            pltpu.VMEM((heads, DH, 4 * DH), bf16),
+            pltpu.VMEM((heads, DH, 2 * DH), bf16),
             pltpu.VMEM((length, heads * DH), bf16),
             pltpu.SemaphoreType.DMA((length // CHUNK,)),
         ],
         compiler_params=limit(24),
         cost_estimate=cost,
         name="reads",
-    )(reach, queries, out_grad, w_cols, qn, lam0, index_row, y1, y2, *y34s)
+    )(reach, queries, out_grad, w_cols, qn, lam, index_row, *y34s)
     arrived = (y1, y2, *y34s)
 
     def returns(order, start, count, held):
-        kn, vn = near_parts[start // each]
+        kn, vn = near_parts[start // each][1:3]
         shape = sds((length, heads * DH), bf16)
 
         def kernel(*refs):

time: 93.5 us -> 89.9 us (0.961)
  Pallas kernels: 43.4 us -> 38.4 us
  waiting for transfers between devices: 17.7 us -> 19 us
    pallas_call x6, Pallas kernels: 31 us -> 26 us  [the longest x4 19.5 us: near_part(): pl.pallas_call(group_kernel, grid=(each,), in_specs=[anywhere] + [token_s...]
    ppermute x20, waiting for transfers between devices: 17.7 us -> 19 us  [flip(): lax.ppermute(x, axis, [(i, i ^ mask) for i in range(lax.axis_size(axis))])]
  transfers between devices with their start and end apart: 20 -> 20, of which waited for: 9 -> 10; matrix products, arithmetic and copies ran while one was open for 0% -> 0% of each run, Pallas kernels for 33% -> 31%
where the time goes in v5:
time: 89.9 us; the launch traced here: 89.6 us
  Pallas kernels  38.4 us (43%)
  starting transfers between devices  28.5 us (32%)
  waiting for transfers between devices  19 us (21%)
  local copies, waits for them, and re-layouts  1.59 us (2%)
  between operations  1.51 us (2%)
    ppermute x20, starting transfers between devices, flip(): lax.ppermute(x, axis, [(i, i ^ mask) for i in range(lax.axis_size(axis))])  28.5 us
    pallas_call x4, Pallas kernels, near_part(): pl.pallas_call(group_kernel, grid=(each,), in_specs=[anywhere] + [token_s...  19.5 us
    ppermute x20, waiting for transfers between devices, flip(): lax.ppermute(x, axis, [(i, i ^ mask) for i in range(lax.axis_size(axis))])  19 us
    pallas_call x1, Pallas kernels, local(): pl.pallas_call(states_kernel, in_specs=[scalar, whole, whole] + [anywhere...  6.11 us
    pallas_call x4, Pallas kernels, returns(): pl.pallas_call(kernel, in_specs=[scalar] + [whole] * 10 + [anywhere] * le...  6.1 us
    pallas_call x1, Pallas kernels, local(): pl.pallas_call(reads_kernel, in_specs=[scalar] + [whole] * 10, out_specs=...  4.34 us
    pallas_call x1, Pallas kernels, local(): pl.pallas_call(near_reads_kernel, in_specs=[anywhere, scalar] + [whole] *...  2.16 us
  transfers between devices with their start and end apart: 20, of which 10 were waited for; matrix products, arithmetic and copies ran while one was open for 0% of the time, Pallas kernels for 31%

profile of v5, /device:TPU:0, one launch (start us, length us, event | category | flops | bytes accessed | tf_op | source)
XLA Modules:
  0.0 89.6 jit_solution(7027143092628121171)
XLA Ops:
  1.3 0.0 copy-start.4
  1.3 0.7 copy-done.4
  2.0 0.7 copy-done.6
  2.7 6.1 %states.1 = (f32[8,1024]{1,0:T(8,128)S(1)}, f32[8,128,128]{2,1,0:T(8,128)S(1)}, f32[8,128,128]{2,1,0:T(8,128)S(1)}, f32[2,2,2,128,128]{4,3,2,1,0:T(8,128)S(1)}, f32[2,2,2,128,128]{4,3,2,1,0:T(8,128)}) custom-call(s32[1]{0:T(128)S(6)} %copy.26.reach.refs_0_, s32[1,1024]{1,0:T(1,128)S(1)} %bitcast.8, f32[5,256]{1,0:T(8,128)S(1)} %copy-done.6, ...), custom_call_target="tpu_custom_call" | custom-call | tf_op jit(solution)/shard_map/states/pallas_call | solution.py:293
  8.8 4.3 %collective-permute-start = (f32[2,2,2,128,128]{4,3,2,1,0:T(8,128)}, f32[2,2,2,128,128]{4,3,2,1,0:T(8,128)S(1)}, u32[]{:S(2)}, u32[]{:S(2)}) collective-permute-start(f32[2,2,2,128,128]{4,3,2,1,0:T(8,128)} %get-tuple-element.58), channel_id=1, source_target_pairs={{0,24},{8,16},{16,8},{24,0},{32,56},{40,48},{48,40},{56,32},{64,88... | collective-permute-start | bytes 1572872 | tf_op jit(solution)/shard_map/ppermute | solution.py:268
  13.1 0.0 collective-permute-start.1
  13.1 0.2 copy.18
  13.3 4.8 %group.4 = (f32[1024,256]{1,0:T(8,128)S(1)}, f32[1024,256]{1,0:T(8,128)S(1)}, f32[1024,256]{1,0:T(8,128)S(1)}, f32[1024,128]{1,0:T(8,128)S(1)}) custom-call(f32[2,2,2,128,128]{4,3,2,1,0:T(8,128)S(1)} %get-tuple-element.57.after.keep_ref, bf16[1024,1024]{1,0:T(8,128)(2,1)} %q_ref.11, bf16[1024,1024]{1,0:T(8,128)(2,1)} %refs_1_.7, bf16[1024,1024]{1,0:T(8,128)(2,1)} %refs_2_.7, ...), custom_call_target="tpu_custom_call" | custom-call | flops 100000000 | bytes 1048576 | tf_op jit(solution)/shard_map/group/pallas_call | solution.py:319
  18.1 4.9 %group.5 = (f32[1024,256]{1,0:T(8,128)S(1)}, f32[1024,256]{1,0:T(8,128)S(1)}, f32[1024,256]{1,0:T(8,128)S(1)}, f32[1024,128]{1,0:T(8,128)S(1)}) custom-call(f32[1024,256]{1,0:T(8,128)S(1)} %get-tuple-element.60.after.rest_0_, bf16[1024,1024]{1,0:T(8,128)(2,1)} %q_ref.11, bf16[1024,1024]{1,0:T(8,128)(2,1)} %refs_1_.7, bf16[1024,1024]{1,0:T(8,128)(2,1)} %refs_2_.7, ...), custom_call_target="tpu_custom_call" | custom-call | flops 100000000 | bytes 1048576 | tf_op jit(solution)/shard_map/group/pallas_call | solution.py:319
  23.0 2.2 %collective-permute-done.got_ref = f32[2,2,2,128,128]{4,3,2,1,0:T(8,128)S(1)} collective-permute-done((f32[2,2,2,128,128]{4,3,2,1,0:T(8,128)}, f32[2,2,2,128,128]{4,3,2,1,0:T(8,128)S(1)}, u32[]{:S(2)}, u32[]{:S(2)}) %collective-permute-start) | collective-permute-done | bytes 524320 | tf_op jit(solution)/shard_map/ppermute | solution.py:268
  25.2 1.2 %collective-permute-done.1.near_got_ref = f32[8,128,128]{2,1,0:T(8,128)S(1)} collective-permute-done((f32[8,128,128]{2,1,0:T(8,128)S(1)}, f32[8,128,128]{2,1,0:T(8,128)S(1)}, u32[]{:S(2)}, u32[]{:S(2)}) %collective-permute-start.1) | collective-permute-done | bytes 524320 | tf_op jit(solution)/shard_map/ppermute | solution.py:268
  26.5 0.1 pair.1
  26.6 0.4 collective-permute-start.2
  26.9 1.5 %collective-permute-start.4 = (f32[8,128,128]{2,1,0:T(8,128)S(1)}, f32[8,128,128]{2,1,0:T(8,128)S(1)}, u32[]{:S(2)}, u32[]{:S(2)}) collective-permute-start(f32[8,128,128]{2,1,0:T(8,128)S(1)} %get-tuple-element.67), channel_id=1, source_target_pairs={{0,24},{8,16},{16,8},{24,0},{32,56},{40,48},{48,40},{56,32},{64,88... | collective-permute-start | bytes 1572872 | tf_op jit(solution)/shard_map/ppermute | solution.py:268
  28.4 4.8 %group.6 = (f32[1024,256]{1,0:T(8,128)S(1)}, f32[1024,256]{1,0:T(8,128)S(1)}, f32[1024,256]{1,0:T(8,128)S(1)}, f32[1024,128]{1,0:T(8,128)S(1)}) custom-call(f32[2,2,128,128]{3,2,1,0:T(8,128)S(1)} %get-tuple-element.62.after.own_ref, bf16[1024,1024]{1,0:T(8,128)(2,1)} %q_ref.11, bf16[1024,1024]{1,0:T(8,128)(2,1)} %refs_1_.7, bf16[1024,1024]{1,0:T(8,128)(2,1)} %refs_2_.7, ...), custom_call_target="tpu_custom_call" | custom-call | flops 100000000 | bytes 1048576 | tf_op jit(solution)/shard_map/group/pallas_call | solution.py:319
  33.3 0.2 collective-permute-done.2.got_ref
  33.5 1.2 %collective-permute-start.6 = (f32[8,128,128]{2,1,0:T(8,128)S(1)}, f32[8,128,128]{2,1,0:T(8,128)S(1)}, u32[]{:S(2)}, u32[]{:S(2)}) collective-permute-start(f32[8,128,128]{2,1,0:T(8,128)S(1)} %get-tuple-element.69), channel_id=1, source_target_pairs={{0,8},{8,0},{16,24},{24,16},{32,40},{40,32},{48,56},{56,48},{64,72... | collective-permute-start | bytes 1572872 | tf_op jit(solution)/shard_map/ppermute | solution.py:268
  34.8 1.6 %collective-permute-start.3 = (f32[2,2,128,128]{3,2,1,0:T(8,128)S(1)}, f32[2,2,128,128]{3,2,1,0:T(8,128)S(1)}, u32[]{:S(2)}, u32[]{:S(2)}) collective-permute-start(f32[2,2,128,128]{3,2,1,0:T(8,128)S(1)} %get-tuple-element.66.after.rows_ref), channel_id=1, source_target_pairs={{0,32},{8,40},{16,48},{24,56},{32,0},{40,8},{48,16},{56,24},{64,96... | collective-permute-start | bytes 786440 | tf_op jit(solution)/shard_map/ppermute | solution.py:268
  36.3 0.0 copy-start.3
  36.3 5.0 %group.7 = (f32[1024,256]{1,0:T(8,128)S(1)}, f32[1024,256]{1,0:T(8,128)S(1)}, f32[1024,256]{1,0:T(8,128)S(1)}, f32[1024,128]{1,0:T(8,128)S(1)}) custom-call(f32[2,2,128,128]{3,2,1,0:T(8,128)S(1)} %get-tuple-element.66.after.rows_ref, bf16[1024,1024]{1,0:T(8,128)(2,1)} %q_ref.11, bf16[1024,1024]{1,0:T(8,128)(2,1)} %refs_1_.7, bf16[1024,1024]{1,0:T(8,128)(2,1)} %refs_2_.7, ...), custom_call_target="tpu_custom_call" | custom-call | flops 100000000 | bytes 1048576 | tf_op jit(solution)/shard_map/group/pallas_call | solution.py:319
  41.3 0.0 copy-start.2
  41.3 0.0 collective-permute-done.4.after.y2_ref.refs_6_
  41.4 0.0 collective-permute-done.3.other_ref.y3_ref
  41.4 2.8 %collective-permute-start.5 = (f32[2,128,128]{2,1,0:T(8,128)S(1)}, f32[2,128,128]{2,1,0:T(8,128)S(1)}, u32[]{:S(2)}, u32[]{:S(2)}) collective-permute-start(f32[2,128,128]{2,1,0:T(8,128)S(1)} %cross.1), channel_id=1, source_target_pairs={{0,96},{8,104},{16,112},{24,120},{32,64},{40,72},{48,80},{56,88},{... | collective-permute-start | bytes 393224 | tf_op jit(solution)/shard_map/ppermute | solution.py:268
  44.2 3.4 %collective-permute-done.5.y4_ref = f32[2,128,128]{2,1,0:T(8,128)S(1)} collective-permute-done((f32[2,128,128]{2,1,0:T(8,128)S(1)}, f32[2,128,128]{2,1,0:T(8,128)S(1)}, u32[]{:S(2)}, u32[]{:S(2)}) %collective-permute-start.5) | collective-permute-done | bytes 131104 | tf_op jit(solution)/shard_map/ppermute | solution.py:268
  47.6 0.0 collective-permute-done.6.rest_0_.y1_ref.refs_5_
  47.7 1.6 %collective-permute-start.9 = (f32[2,2,128,128]{3,2,1,0:T(8,128)S(1)}, f32[2,2,128,128]{3,2,1,0:T(8,128)S(1)}, u32[]{:S(2)}, u32[]{:S(2)}) collective-permute-start(f32[2,2,128,128]{3,2,1,0:T(8,128)S(1)} %pack.1.after.rest_0_.refs_7_), channel_id=1, source_target_pairs={{0,24},{8,16},{16,8},{24,0},{32,56},{40,48},{48,40},{56,32},{64,88... | collective-permute-start | bytes 786440 | tf_op jit(solution)/shard_map/ppermute | solution.py:268
  49.3 1.4 %collective-permute-start.8 = (f32[2,2,128,128]{3,2,1,0:T(8,128)S(1)}, f32[2,2,128,128]{3,2,1,0:T(8,128)S(1)}, u32[]{:S(2)}, u32[]{:S(2)}) collective-permute-start(f32[2,2,128,128]{3,2,1,0:T(8,128)S(1)} %pack.1.after.rest_0_.refs_7_), channel_id=1, source_target_pairs={{0,16},{8,24},{16,0},{24,8},{32,48},{40,56},{48,32},{56,40},{64,80... | collective-permute-start | bytes 786440 | tf_op jit(solution)/shard_map/ppermute | solution.py:268
  50.7 1.1 %collective-permute-start.7 = (f32[2,2,128,128]{3,2,1,0:T(8,128)S(1)}, f32[2,2,128,128]{3,2,1,0:T(8,128)S(1)}, u32[]{:S(2)}, u32[]{:S(2)}) collective-permute-start(f32[2,2,128,128]{3,2,1,0:T(8,128)S(1)} %pack.1.after.rest_0_.refs_7_), channel_id=1, source_target_pairs={{0,8},{8,0},{16,24},{24,16},{32,40},{40,32},{48,56},{56,48},{64,72... | collective-permute-start | bytes 786440 | tf_op jit(solution)/shard_map/ppermute | solution.py:268
  51.8 0.0 copy-done.3
  51.8 0.0 copy-done.2
  51.9 2.2 %near_reads.1 = (f32[1024,1024]{1,0:T(8,128)S(1)}, f32[1024,128]{1,0:T(8,128)S(1)}) custom-call(f32[2,2,128,128]{3,2,1,0:T(8,128)S(1)} %pack.1.after.rest_0_.refs_7_, s32[1]{0:T(128)S(6)} %copy.26.reach.refs_0_, bf16[1024,1024]{1,0:T(8,128)(2,1)S(1)} %copy-done.2, bf16[1024,1024]{1,0:T(8,128)(2,1)S(1)} %copy-done.3, f32[1024,8]{1,0:T(8,128)S(1)} %bitcast.6, ...), custom_call_target="tpu_custom_call" | custom-call | flops 100000000 | bytes 1048576 | tf_op jit(solution)/shard_map/near_reads/pallas_call | solution.py:366
  54.0 5.5 %collective-permute-done.9.rest_3_.refs_10_ = f32[2,2,128,128]{3,2,1,0:T(8,128)S(1)} collective-permute-done((f32[2,2,128,128]{3,2,1,0:T(8,128)S(1)}, f32[2,2,128,128]{3,2,1,0:T(8,128)S(1)}, u32[]{:S(2)}, u32[]{:S(2)}) %collective-permute-start.9) | collective-permute-done | bytes 262176 | tf_op jit(solution)/shard_map/ppermute | solution.py:268
  59.5 0.0 collective-permute-done.8.rest_2_.refs_9_
  59.5 0.7 collective-permute-done.7.rest_1_.refs_8_
  60.1 0.0 copy-done.5
  60.1 4.3 %reads.1 = (bf16[1024,1024]{1,0:T(8,128)(2,1)}, f32[8,256]{1,0:T(8,128)S(1)}) custom-call(s32[1]{0:T(128)S(6)} %copy.26.reach.refs_0_, bf16[1024,1024]{1,0:T(8,128)(2,1)S(1)} %copy-done.2, bf16[1024,1024]{1,0:T(8,128)(2,1)S(1)} %copy-done.3, f32[1024,8]{1,0:T(8,128)S(1)} %bitcast.7, f32[1024,1024]{1,0:T(8,128)S(1)} %get-tuple-element.74.qn_ref, ...), custom_call_target="tpu_custom_call" | custom-call | flops 100000000 | bytes 1048576 | tf_op jit(solution)/shard_map/reads/pallas_call | solution.py:380
  64.5 0.1 collective-permute-start.10
  64.6 0.0 copy-done
  64.6 0.0 copy-done.1
  64.6 1.6 %returns.4 = (bf16[1024,1024]{1,0:T(8,128)(2,1)}, bf16[1024,1024]{1,0:T(8,128)(2,1)}) custom-call(s32[1]{0:T(128)S(6)} %copy.26.reach.refs_0_, bf16[1024,1024]{1,0:T(8,128)(2,1)S(1)} %copy-done, bf16[1024,1024]{1,0:T(8,128)(2,1)S(1)} %copy-done.1, f32[1024,256]{1,0:T(8,128)S(1)} %get-tuple-element.79.refs_3_, f32[1024,256]{1,0:T(8,128)S(1)} %get-tuple-element.80.refs_4_, ...), custom_call_target="tpu_custom_call" | custom-call | flops 100000000 | bytes 1048576 | tf_op jit(solution)/shard_map/returns/pallas_call | solution.py:403
  66.2 0.0 collective-permute-done.10
  66.2 2.8 %collective-permute-start.13 = (f32[8,256]{1,0:T(8,128)S(1)}, f32[8,256]{1,0:T(8,128)S(1)}, u32[]{:S(2)}, u32[]{:S(2)}) collective-permute-start(f32[8,256]{1,0:T(8,128)S(1)} %add.30), channel_id=1, source_target_pairs={{0,6},{1,7},{2,4},{3,5},{4,2},{5,3},{6,0},{7,1},{8,14},{9,15},{10,... | collective-permute-start | bytes 24584 | tf_op jit(solution)/shard_map/ppermute | solution.py:268
  69.1 0.8 collective-permute-start.12
  69.9 0.5 collective-permute-start.11
  70.4 1.5 %returns.5 = (bf16[1024,1024]{1,0:T(8,128)(2,1)}, bf16[1024,1024]{1,0:T(8,128)(2,1)}) custom-call(s32[1]{0:T(128)S(6)} %copy.26.reach.refs_0_, bf16[1024,1024]{1,0:T(8,128)(2,1)S(1)} %copy-done, bf16[1024,1024]{1,0:T(8,128)(2,1)S(1)} %copy-done.1, f32[1024,256]{1,0:T(8,128)S(1)} %get-tuple-element.85.refs_3_, ...), custom_call_target="tpu_custom_call", output_to_operand_aliasing={{0}: (11, {}), {1}: (12, {})} | custom-call | flops 100000000 | bytes 1048576 | tf_op jit(solution)/shard_map/returns/pallas_call | solution.py:403
  71.9 0.0 collective-permute-done.13
  71.9 2.3 %collective-permute-done.12 = f32[8,256]{1,0:T(8,128)S(1)} collective-permute-done((f32[8,256]{1,0:T(8,128)S(1)}, f32[8,256]{1,0:T(8,128)S(1)}, u32[]{:S(2)}, u32[]{:S(2)}) %collective-permute-start.12) | collective-permute-done | bytes 8224 | tf_op jit(solution)/shard_map/ppermute | solution.py:268
  74.2 0.0 collective-permute-done.11
  74.2 1.4 %collective-permute-start.16 = (f32[8,256]{1,0:T(8,128)S(1)}, f32[8,256]{1,0:T(8,128)S(1)}, u32[]{:S(2)}, u32[]{:S(2)}) collective-permute-start(f32[8,256]{1,0:T(8,128)S(1)} %add_add_fusion.1), channel_id=1, source_target_pairs={{0,24},{8,16},{16,8},{24,0},{32,56},{40,48},{48,40},{56,32},{64,88... | collective-permute-start | bytes 24584 | tf_op jit(solution)/shard_map/ppermute | solution.py:268
  75.7 1.7 %collective-permute-start.15 = (f32[8,256]{1,0:T(8,128)S(1)}, f32[8,256]{1,0:T(8,128)S(1)}, u32[]{:S(2)}, u32[]{:S(2)}) collective-permute-start(f32[8,256]{1,0:T(8,128)S(1)} %add_add_fusion.1), channel_id=1, source_target_pairs={{0,16},{8,24},{16,0},{24,8},{32,48},{40,56},{48,32},{56,40},{64,80... | collective-permute-start | bytes 24584 | tf_op jit(solution)/shard_map/ppermute | solution.py:268
  77.3 1.0 %collective-permute-start.14 = (f32[8,256]{1,0:T(8,128)S(1)}, f32[8,256]{1,0:T(8,128)S(1)}, u32[]{:S(2)}, u32[]{:S(2)}) collective-permute-start(f32[8,256]{1,0:T(8,128)S(1)} %add_add_fusion.1), channel_id=1, source_target_pairs={{0,8},{8,0},{16,24},{24,16},{32,40},{40,32},{48,56},{56,48},{64,72... | collective-permute-start | bytes 24584 | tf_op jit(solution)/shard_map/ppermute | solution.py:268
  78.4 1.5 %returns.6 = (bf16[1024,1024]{1,0:T(8,128)(2,1)}, bf16[1024,1024]{1,0:T(8,128)(2,1)}) custom-call(s32[1]{0:T(128)S(6)} %copy.26.reach.refs_0_, bf16[1024,1024]{1,0:T(8,128)(2,1)S(1)} %copy-done, bf16[1024,1024]{1,0:T(8,128)(2,1)S(1)} %copy-done.1, f32[1024,256]{1,0:T(8,128)S(1)} %get-tuple-element.93.refs_3_, ...), custom_call_target="tpu_custom_call", output_to_operand_aliasing={{0}: (11, {}), {1}: (12, {})} | custom-call | flops 100000000 | bytes 1048576 | tf_op jit(solution)/shard_map/returns/pallas_call | solution.py:403
  79.9 0.0 collective-permute-done.16
  79.9 0.9 collective-permute-done.15
  80.8 0.2 collective-permute-done.14
  81.0 2.9 %collective-permute-start.19 = (f32[8,256]{1,0:T(8,128)S(1)}, f32[8,256]{1,0:T(8,128)S(1)}, u32[]{:S(2)}, u32[]{:S(2)}) collective-permute-start(f32[8,256]{1,0:T(8,128)S(1)} %add_add_fusion), channel_id=1, source_target_pairs={{0,96},{8,104},{16,112},{24,120},{32,64},{40,72},{48,80},{56,88},{... | collective-permute-start | bytes 24584 | tf_op jit(solution)/shard_map/ppermute | solution.py:268
  83.9 0.0 collective-permute-start.18
  83.9 1.2 %collective-permute-start.17 = (f32[8,256]{1,0:T(8,128)S(1)}, f32[8,256]{1,0:T(8,128)S(1)}, u32[]{:S(2)}, u32[]{:S(2)}) collective-permute-start(f32[8,256]{1,0:T(8,128)S(1)} %add_add_fusion), channel_id=1, source_target_pairs={{0,32},{8,40},{16,48},{24,56},{32,0},{40,8},{48,16},{56,24},{64,96... | collective-permute-start | bytes 24584 | tf_op jit(solution)/shard_map/ppermute | solution.py:268
  85.1 1.5 %returns.7 = (bf16[1024,1024]{1,0:T(8,128)(2,1)}, bf16[1024,1024]{1,0:T(8,128)(2,1)}) custom-call(s32[1]{0:T(128)S(6)} %copy.26.reach.refs_0_, bf16[1024,1024]{1,0:T(8,128)(2,1)S(1)} %copy-done, bf16[1024,1024]{1,0:T(8,128)(2,1)S(1)} %copy-done.1, f32[1024,256]{1,0:T(8,128)S(1)} %get-tuple-element.101.refs_3_, ...), custom_call_target="tpu_custom_call", output_to_operand_aliasing={{0}: (11, {}), {1}: (12, {})} | custom-call | flops 100000000 | bytes 1048576 | tf_op jit(solution)/shard_map/returns/pallas_call | solution.py:403
  86.6 0.0 collective-permute-done.19
  86.6 2.4 %collective-permute-done.18 = f32[8,256]{1,0:T(8,128)S(1)} collective-permute-done((f32[8,256]{1,0:T(8,128)S(1)}, f32[8,256]{1,0:T(8,128)S(1)}, u32[]{:S(2)}, u32[]{:S(2)}) %collective-permute-start.18) | collective-permute-done | bytes 8224 | tf_op jit(solution)/shard_map/ppermute | solution.py:268
  89.0 0.0 collective-permute-done.17
  89.0 0.6 fusion.1
  (10 shorter events, 0.1 us)
Async XLA Ops:
  1.3 0.7 copy-start.4
  2.0 0.7 copy-start.6
  8.8 16.4 %collective-permute-start = (f32[2,2,2,128,128]{4,3,2,1,0:T(8,128)}, f32[2,2,2,128,128]{4,3,2,1,0:T(8,128)S(1)}, u32[]{:S(2)}, u32[]{:S(2)}) collective-permute-start(f32[2,2,2,128,128]{4,3,2,1,0:T(8,128)} %get-tuple-element.58), channel_id=1, source_target_pairs={{0,24},{8,16},{16,8},{24,0},{32,56},{40,48},{48,40},{56,32},{64,88... | collective-permute-start | bytes 1572872 | tf_op jit(solution)/shard_map/ppermute | solution.py:268
  13.1 13.4 %collective-permute-start.1 = (f32[8,128,128]{2,1,0:T(8,128)S(1)}, f32[8,128,128]{2,1,0:T(8,128)S(1)}, u32[]{:S(2)}, u32[]{:S(2)}) collective-permute-start(f32[8,128,128]{2,1,0:T(8,128)S(1)} %get-tuple-element.59.near_ref), channel_id=1, source_target_pairs={{0,8},{8,0},{16,24},{24,16},{32,40},{40,32},{48,56},{56,48},{64,72... | collective-permute-start | bytes 1572872 | tf_op jit(solution)/shard_map/ppermute | solution.py:268
  26.6 6.9 %collective-permute-start.2 = (f32[2,2,128,128]{3,2,1,0:T(8,128)S(1)}, f32[2,2,128,128]{3,2,1,0:T(8,128)S(1)}, u32[]{:S(2)}, u32[]{:S(2)}) collective-permute-start(f32[2,2,128,128]{3,2,1,0:T(8,128)S(1)} %get-tuple-element.63), channel_id=1, source_target_pairs={{0,8},{8,0},{16,24},{24,16},{32,40},{40,32},{48,56},{56,48},{64,72... | collective-permute-start | bytes 786440 | tf_op jit(solution)/shard_map/ppermute | solution.py:268
  26.9 14.4 %collective-permute-start.4 = (f32[8,128,128]{2,1,0:T(8,128)S(1)}, f32[8,128,128]{2,1,0:T(8,128)S(1)}, u32[]{:S(2)}, u32[]{:S(2)}) collective-permute-start(f32[8,128,128]{2,1,0:T(8,128)S(1)} %get-tuple-element.67), channel_id=1, source_target_pairs={{0,24},{8,16},{16,8},{24,0},{32,56},{40,48},{48,40},{56,32},{64,88... | collective-permute-start | bytes 1572872 | tf_op jit(solution)/shard_map/ppermute | solution.py:268
  33.5 14.1 %collective-permute-start.6 = (f32[8,128,128]{2,1,0:T(8,128)S(1)}, f32[8,128,128]{2,1,0:T(8,128)S(1)}, u32[]{:S(2)}, u32[]{:S(2)}) collective-permute-start(f32[8,128,128]{2,1,0:T(8,128)S(1)} %get-tuple-element.69), channel_id=1, source_target_pairs={{0,8},{8,0},{16,24},{24,16},{32,40},{40,32},{48,56},{56,48},{64,72... | collective-permute-start | bytes 1572872 | tf_op jit(solution)/shard_map/ppermute | solution.py:268
  34.8 6.6 %collective-permute-start.3 = (f32[2,2,128,128]{3,2,1,0:T(8,128)S(1)}, f32[2,2,128,128]{3,2,1,0:T(8,128)S(1)}, u32[]{:S(2)}, u32[]{:S(2)}) collective-permute-start(f32[2,2,128,128]{3,2,1,0:T(8,128)S(1)} %get-tuple-element.66.after.rows_ref), channel_id=1, source_target_pairs={{0,32},{8,40},{16,48},{24,56},{32,0},{40,8},{48,16},{56,24},{64,96... | collective-permute-start | bytes 786440 | tf_op jit(solution)/shard_map/ppermute | solution.py:268
  36.3 15.5 %copy-start.3 = (bf16[1024,1024]{1,0:T(8,128)(2,1)S(1)}, bf16[1024,1024]{1,0:T(8,128)(2,1)}, u32[]{:S(2)}) copy-start(bf16[1024,1024]{1,0:T(8,128)(2,1)} %g_ref.11) | copy-start | bytes 6291460
  41.3 10.5 %copy-start.2 = (bf16[1024,1024]{1,0:T(8,128)(2,1)S(1)}, bf16[1024,1024]{1,0:T(8,128)(2,1)}, u32[]{:S(2)}) copy-start(bf16[1024,1024]{1,0:T(8,128)(2,1)} %q_ref.11) | copy-start | bytes 6291460
  41.4 6.3 %collective-permute-start.5 = (f32[2,128,128]{2,1,0:T(8,128)S(1)}, f32[2,128,128]{2,1,0:T(8,128)S(1)}, u32[]{:S(2)}, u32[]{:S(2)}) collective-permute-start(f32[2,128,128]{2,1,0:T(8,128)S(1)} %cross.1), channel_id=1, source_target_pairs={{0,96},{8,104},{16,112},{24,120},{32,64},{40,72},{48,80},{56,88},{... | collective-permute-start | bytes 393224 | tf_op jit(solution)/shard_map/ppermute | solution.py:268
  47.7 11.8 %collective-permute-start.9 = (f32[2,2,128,128]{3,2,1,0:T(8,128)S(1)}, f32[2,2,128,128]{3,2,1,0:T(8,128)S(1)}, u32[]{:S(2)}, u32[]{:S(2)}) collective-permute-start(f32[2,2,128,128]{3,2,1,0:T(8,128)S(1)} %pack.1.after.rest_0_.refs_7_), channel_id=1, source_target_pairs={{0,24},{8,16},{16,8},{24,0},{32,56},{40,48},{48,40},{56,32},{64,88... | collective-permute-start | bytes 786440 | tf_op jit(solution)/shard_map/ppermute | solution.py:268
  49.3 10.2 %collective-permute-start.8 = (f32[2,2,128,128]{3,2,1,0:T(8,128)S(1)}, f32[2,2,128,128]{3,2,1,0:T(8,128)S(1)}, u32[]{:S(2)}, u32[]{:S(2)}) collective-permute-start(f32[2,2,128,128]{3,2,1,0:T(8,128)S(1)} %pack.1.after.rest_0_.refs_7_), channel_id=1, source_target_pairs={{0,16},{8,24},{16,0},{24,8},{32,48},{40,56},{48,32},{56,40},{64,80... | collective-permute-start | bytes 786440 | tf_op jit(solution)/shard_map/ppermute | solution.py:268
  50.7 9.4 %collective-permute-start.7 = (f32[2,2,128,128]{3,2,1,0:T(8,128)S(1)}, f32[2,2,128,128]{3,2,1,0:T(8,128)S(1)}, u32[]{:S(2)}, u32[]{:S(2)}) collective-permute-start(f32[2,2,128,128]{3,2,1,0:T(8,128)S(1)} %pack.1.after.rest_0_.refs_7_), channel_id=1, source_target_pairs={{0,8},{8,0},{16,24},{24,16},{32,40},{40,32},{48,56},{56,48},{64,72... | collective-permute-start | bytes 786440 | tf_op jit(solution)/shard_map/ppermute | solution.py:268
  51.9 8.3 %copy-start.5 = (s32[1024]{0:T(1024)S(1)}, s32[1024]{0:T(1024)}, u32[]{:S(2)}) copy-start(s32[1024]{0:T(1024)} %param.12) | copy-start | bytes 12292
  60.1 4.4 %copy-start = (bf16[1024,1024]{1,0:T(8,128)(2,1)S(1)}, bf16[1024,1024]{1,0:T(8,128)(2,1)}, u32[]{:S(2)}) copy-start(bf16[1024,1024]{1,0:T(8,128)(2,1)} %refs_1_.7) | copy-start | bytes 6291460
  60.1 4.5 %copy-start.1 = (bf16[1024,1024]{1,0:T(8,128)(2,1)S(1)}, bf16[1024,1024]{1,0:T(8,128)(2,1)}, u32[]{:S(2)}) copy-start(bf16[1024,1024]{1,0:T(8,128)(2,1)} %refs_2_.7) | copy-start | bytes 6291460
  64.5 1.7 %collective-permute-start.10 = (f32[8,256]{1,0:T(8,128)S(1)}, f32[8,256]{1,0:T(8,128)S(1)}, u32[]{:S(2)}, u32[]{:S(2)}) collective-permute-start(f32[8,256]{1,0:T(8,128)S(1)} %get-tuple-element.77), channel_id=1, source_target_pairs={{0,1},{1,0},{2,3},{3,2},{4,5},{5,4},{6,7},{7,6},{8,9},{9,8},{10,11... | collective-permute-start | bytes 24584 | tf_op jit(solution)/shard_map/ppermute | solution.py:268
  66.2 5.7 %collective-permute-start.13 = (f32[8,256]{1,0:T(8,128)S(1)}, f32[8,256]{1,0:T(8,128)S(1)}, u32[]{:S(2)}, u32[]{:S(2)}) collective-permute-start(f32[8,256]{1,0:T(8,128)S(1)} %add.30), channel_id=1, source_target_pairs={{0,6},{1,7},{2,4},{3,5},{4,2},{5,3},{6,0},{7,1},{8,14},{9,15},{10,... | collective-permute-start | bytes 24584 | tf_op jit(solution)/shard_map/ppermute | solution.py:268
  69.1 5.2 %collective-permute-start.12 = (f32[8,256]{1,0:T(8,128)S(1)}, f32[8,256]{1,0:T(8,128)S(1)}, u32[]{:S(2)}, u32[]{:S(2)}) collective-permute-start(f32[8,256]{1,0:T(8,128)S(1)} %add.30), channel_id=1, source_target_pairs={{0,4},{1,5},{2,6},{3,7},{4,0},{5,1},{6,2},{7,3},{8,12},{9,13},{10,... | collective-permute-start | bytes 24584 | tf_op jit(solution)/shard_map/ppermute | solution.py:268
  69.9 4.3 %collective-permute-start.11 = (f32[8,256]{1,0:T(8,128)S(1)}, f32[8,256]{1,0:T(8,128)S(1)}, u32[]{:S(2)}, u32[]{:S(2)}) collective-permute-start(f32[8,256]{1,0:T(8,128)S(1)} %add.30), channel_id=1, source_target_pairs={{0,2},{1,3},{2,0},{3,1},{4,6},{5,7},{6,4},{7,5},{8,10},{9,11},{10,... | collective-permute-start | bytes 24584 | tf_op jit(solution)/shard_map/ppermute | solution.py:268
  74.2 5.7 %collective-permute-start.16 = (f32[8,256]{1,0:T(8,128)S(1)}, f32[8,256]{1,0:T(8,128)S(1)}, u32[]{:S(2)}, u32[]{:S(2)}) collective-permute-start(f32[8,256]{1,0:T(8,128)S(1)} %add_add_fusion.1), channel_id=1, source_target_pairs={{0,24},{8,16},{16,8},{24,0},{32,56},{40,48},{48,40},{56,32},{64,88... | collective-permute-start | bytes 24584 | tf_op jit(solution)/shard_map/ppermute | solution.py:268
  75.7 5.2 %collective-permute-start.15 = (f32[8,256]{1,0:T(8,128)S(1)}, f32[8,256]{1,0:T(8,128)S(1)}, u32[]{:S(2)}, u32[]{:S(2)}) collective-permute-start(f32[8,256]{1,0:T(8,128)S(1)} %add_add_fusion.1), channel_id=1, source_target_pairs={{0,16},{8,24},{16,0},{24,8},{32,48},{40,56},{48,32},{56,40},{64,80... | collective-permute-start | bytes 24584 | tf_op jit(solution)/shard_map/ppermute | solution.py:268
  77.3 3.7 %collective-permute-start.14 = (f32[8,256]{1,0:T(8,128)S(1)}, f32[8,256]{1,0:T(8,128)S(1)}, u32[]{:S(2)}, u32[]{:S(2)}) collective-permute-start(f32[8,256]{1,0:T(8,128)S(1)} %add_add_fusion.1), channel_id=1, source_target_pairs={{0,8},{8,0},{16,24},{24,16},{32,40},{40,32},{48,56},{56,48},{64,72... | collective-permute-start | bytes 24584 | tf_op jit(solution)/shard_map/ppermute | solution.py:268
  81.0 5.6 %collective-permute-start.19 = (f32[8,256]{1,0:T(8,128)S(1)}, f32[8,256]{1,0:T(8,128)S(1)}, u32[]{:S(2)}, u32[]{:S(2)}) collective-permute-start(f32[8,256]{1,0:T(8,128)S(1)} %add_add_fusion), channel_id=1, source_target_pairs={{0,96},{8,104},{16,112},{24,120},{32,64},{40,72},{48,80},{56,88},{... | collective-permute-start | bytes 24584 | tf_op jit(solution)/shard_map/ppermute | solution.py:268
  83.9 5.2 %collective-permute-start.18 = (f32[8,256]{1,0:T(8,128)S(1)}, f32[8,256]{1,0:T(8,128)S(1)}, u32[]{:S(2)}, u32[]{:S(2)}) collective-permute-start(f32[8,256]{1,0:T(8,128)S(1)} %add_add_fusion), channel_id=1, source_target_pairs={{0,64},{8,72},{16,80},{24,88},{32,96},{40,104},{48,112},{56,120},{... | collective-permute-start | bytes 24584 | tf_op jit(solution)/shard_map/ppermute | solution.py:268
  83.9 5.2 %collective-permute-start.17 = (f32[8,256]{1,0:T(8,128)S(1)}, f32[8,256]{1,0:T(8,128)S(1)}, u32[]{:S(2)}, u32[]{:S(2)}) collective-permute-start(f32[8,256]{1,0:T(8,128)S(1)} %add_add_fusion), channel_id=1, source_target_pairs={{0,32},{8,40},{16,48},{24,56},{32,0},{40,8},{48,16},{56,24},{64,96... | collective-permute-start | bytes 24584 | tf_op jit(solution)/shard_map/ppermute | solution.py:268

commit v6 on v5

--- a/solution.py
+++ b/solution.py
@@ -128,133 +128,172 @@
     return [jnp.where(bits[l] == keep, ys[l], 0.0) for l in range(4)]
 
 
-def reads_tile(at, levels, q_ref, g_ref, w_ref, st, old, new_ref):
+def reads_tile(at, levels, heads, q_ref, g_ref, w_ref, held, old, put):
     tile = at.size
     w = w_ref[at, :]
     wide = [jnp.broadcast_to(SCALE * w[:, l : l + 1], (tile, DH)) for l in levels]
     acc = [None] * len(levels)
-    for h in range(st.shape[0]):
-        c = slice(h * DH, (h + 1) * DH)
-        reads = mm(g_ref[at, c], st[h], 1, 0)
+    for n, head in enumerate(heads):
+        c = pl.ds(head * DH if isinstance(head, int) else pl.multiple_of(head * DH, DH), DH)
+        reads = mm(g_ref[at, c], held[n], 1, 0)
         q = q_ref[at, c].astype(f32)
-        total = old(h)
+        total = old(n, c)
         for i in range(len(levels)):
             read = reads[:, i * DH : (i + 1) * DH]
             product = q * read
             acc[i] = product if acc[i] is None else acc[i] + product
             total = total + wide[i] * read
-        new_ref[at, c] = total.astype(new_ref.dtype)
+        put(n, c, total)
     return acc
 
 
-def near_reads_kernel(after, reach, q_ref, g_ref, w_ref, y1_ref, y2_ref, *rest):
-    count = (len(rest) - 3) // 2
-    qn_refs, lam_refs, (out_ref, lam_ref, st) = rest[:count], rest[count : 2 * count], rest[2 * count :]
+def put_levels(lam, levels, acc, reach):
+    lane = lax.broadcasted_iota(jnp.int32, (1, DH), 1)
+    for l, x in zip(levels, acc):
+        here = (lane == l) & (reach[0] >= l)
+        lam = lam + jnp.where(here, jnp.sum(x, 1, keepdims=True), 0.0)
+    return lam
+
+
+def head_spots(refs):
+    return [
+        (ref, slice(i * DH, (i + 1) * DH)) for ref in refs for i in range(ref.shape[1] // DH)
+    ]
+
+
+def near_reads_kernel(reach, y34_ref, q_ref, g_ref, w_ref, y1_ref, y2_ref, *rest):
+    count = (len(rest) - 4) // 2
+    qn_refs, lam_refs = rest[:count], rest[count : 2 * count]
+    out_ref, lam_ref, late_ref, st = rest[2 * count :]
     heads = y1_ref.shape[0]
-    each = heads // count
+    spots = head_spots(qn_refs)
     bits, spot = place()
+    late_ref[...] = y34_ref[...]
     for h in range(heads):
         parts = [jnp.where(b > 0, y_ref[h], 0.0) for b, y_ref in zip(bits, (y1_ref, y2_ref))]
         st[h] = jnp.concatenate(parts, 1).astype(bf16)
-    lane = lax.broadcasted_iota(jnp.int32, (1, DH), 1)
     for t in range(q_ref.shape[0] // CHUNK):
         at = pl.ds(t * CHUNK, CHUNK)
 
-        def old(h):
-            i = h % each
-            return qn_refs[h // each][at, i * DH : (i + 1) * DH]
-
-        acc = reads_tile(at, (1, 2), q_ref, g_ref, w_ref, st, old, out_ref)
+        def old(n, c):
+            ref, cols = spots[n]
+            return ref[at, cols]
+
+        def put(n, c, total):
+            out_ref[at, c] = total
+
+        acc = reads_tile(at, (1, 2), range(heads), q_ref, g_ref, w_ref, st, old, put)
         lam0 = lam_refs[0][at, :]
         for ref in lam_refs[1:]:
             lam0 = lam0 + ref[at, :]
-        lam = jnp.zeros((CHUNK, DH), f32)
-        for l, x in enumerate([lam0] + acc):
-            here = (lane == l) & (reach[0] >= l)
-            lam = jnp.where(here, jnp.sum(x, 1, keepdims=True), lam)
-        lam_ref[at, :] = lam
-
-
-def reads_kernel(reach, q_ref, g_ref, w_ref, qn_ref, lam_ref, index_ref, *rest):
-    y34_refs, (out_hbm, table_ref, st, out_buf, sem) = rest[:4], rest[4:]
-    heads = st.shape[0]
+        lam_ref[at, :] = put_levels(jnp.zeros((CHUNK, DH), f32), (0, 1, 2), [lam0] + acc, reach)
+
+
+def far_reads(spots, reach, q_ref, g_ref, w_ref, qn_ref, lam_ref, y34_refs, out_hbm, st, out_buf, sem, finish):
+    each = y34_refs[0].shape[1]
+    bits, spot = place()
+    for n, y34_ref in enumerate(y34_refs):
+        for i in range(each):
+            parts = [jnp.where(bits[l + 2] > 0, y34_ref[l, i], 0.0) for l in range(2)]
+            st[n * each + i] = jnp.concatenate(parts, 1).astype(bf16)
+    heads = [(spot ^ j) * each + i for j in spots for i in range(each)]
+    copies = []
+    for t in range(q_ref.shape[0] // CHUNK):
+        at = pl.ds(t * CHUNK, CHUNK)
+
+        def old(n, c):
+            return qn_ref[at, c]
+
+        def put(n, c, total):
+            out_buf[at, n * DH : (n + 1) * DH] = total.astype(bf16)
+
+        acc = reads_tile(at, (3, 4), heads, q_ref, g_ref, w_ref, st, old, put)
+        for n, j in enumerate(spots):
+            wide = each * DH
+            cols = pl.ds(pl.multiple_of((spot ^ j) * wide, wide), wide)
+            copies.append(
+                pltpu.make_async_copy(
+                    out_buf.at[at, pl.ds(n * wide, wide)], out_hbm.at[at, cols], sem.at[t, n]
+                )
+            )
+            copies[-1].start()
+        finish(at, put_levels(lam_ref[at, :], (3, 4), acc, reach))
+    for copy in copies:
+        copy.wait()
+
+
+FIRST_SPOTS = (0, 1, 3)
+
+
+def first_reads_kernel(reach, q_ref, g_ref, w_ref, qn_ref, lam_ref, *rest):
+    y34_refs, (out_hbm, lam_out, st, out_buf, sem) = rest[:3], rest[3:]
+
+    def finish(at, lam):
+        lam_out[at, :] = lam
+
+    far_reads(FIRST_SPOTS, reach, q_ref, g_ref, w_ref, qn_ref, lam_ref, y34_refs, out_hbm, st, out_buf, sem, finish)
+
+
+def last_reads_kernel(reach, q_ref, g_ref, w_ref, qn_ref, lam_ref, y34_ref, index_ref, held, out_hbm, table_ref, st, out_buf, sem):
+    table_ref[...] = jnp.zeros_like(table_ref)
+
+    def finish(at, lam):
+        lam = (SCALE * lam).T[:8]
+        picked = one_hot(index_ref[:, at], table_ref.shape[1])
+        table_ref[...] += sum(mm(piece, picked, 1, 1) for piece in thirds(lam))
+
+    far_reads((2,), reach, q_ref, g_ref, w_ref, qn_ref, lam_ref, (y34_ref,), out_hbm, st, out_buf, sem, finish)
+
+
+def pair_kernel(keep_ref, got_ref, near_ref, near_got_ref, after, own_ref, send_ref, sum_ref):
+    own_ref[...] = keep_ref[0] + got_ref[0]
+    send_ref[...] = keep_ref[1] + got_ref[1]
+    sum_ref[...] = near_ref[...] + near_got_ref[...]
+
+
+def gate_kernel(after, near_in, near_out):
+    pass
+
+
+def rows_kernel(own_ref, got_ref, after, three_ref, four_ref):
+    three_ref[...] = own_ref[0] + got_ref[0]
+    four_ref[...] = own_ref[1] + got_ref[1]
+
+
+def cross_kernel(rows_ref, other_ref, after, after_too, out_ref):
+    out_ref[...] = rows_ref[...] + other_ref[...]
+
+
+def pack_kernel(y3_ref, y4_ref, *rest):
+    out_ref = rest[-1]
+    out_ref[0] = y3_ref[...]
+    out_ref[1] = y4_ref[...]
+
+
+def returns_kernel(start, parts, order, k_ref, v_ref, *rest):
+    kn_spots, vn_spots = head_spots(rest[:parts]), head_spots(rest[parts : 2 * parts])
+    y1_ref, y2_ref, *y34_refs = rest[2 * parts : 2 * parts + 6]
+    key_hbm, value_hbm, key_buf, value_buf, st, sem = rest[-6:]
+    heads = y1_ref.shape[0]
     each = heads // 4
+    count = key_buf.shape[1] // DH
     bits, spot = place()
     for j in range(4):
         for i in range(each):
             head = (spot ^ j) * each + i
-            parts = [jnp.where(bits[l + 2] > 0, y34_refs[j][l, i], 0.0) for l in range(2)]
-            st[head] = jnp.concatenate(parts, 1).astype(bf16)
-    lane = lax.broadcasted_iota(jnp.int32, (1, DH), 1)
-    table = None
-    copies = []
-    for t in range(q_ref.shape[0] // CHUNK):
-        at = pl.ds(t * CHUNK, CHUNK)
-
-        def old(h):
-            return qn_ref[at, h * DH : (h + 1) * DH]
-
-        acc = reads_tile(at, (3, 4), q_ref, g_ref, w_ref, st, old, out_buf)
-        copies.append(pltpu.make_async_copy(out_buf.at[at, :], out_hbm.at[at, :], sem.at[t]))
-        copies[-1].start()
-        lam = lam_ref[at, :]
-        for l, x in zip((3, 4), acc):
-            here = (lane == l) & (reach[0] >= l)
-            lam = jnp.where(here, jnp.sum(x, 1, keepdims=True), lam)
-        lam = (SCALE * lam).T[:8]
-        picked = one_hot(index_ref[:, at], table_ref.shape[1])
-        for piece in thirds(lam):
-            part = mm(piece, picked, 1, 1)
-            table = part if table is None else table + part
-    table_ref[...] = table
-    for copy in copies:
-        copy.wait()
-
-
-def pair_kernel(keep_ref, got_ref, near_ref, near_got_ref, after, own_ref, send_ref, sum_ref):
-    own_ref[...] = keep_ref[0] + got_ref[0]
-    send_ref[...] = keep_ref[1] + got_ref[1]
-    sum_ref[...] = near_ref[...] + near_got_ref[...]
-
-
-def rows_kernel(own_ref, got_ref, after, near_in, rows_ref, near_out):
-    rows_ref[...] = own_ref[...] + got_ref[...]
-
-
-def cross_kernel(rows_ref, other_ref, after, after_too, out_ref):
-    out_ref[...] = rows_ref[1] + other_ref[1]
-
-
-def pack_kernel(y3_ref, y4_ref, *rest):
-    out_ref = rest[-1]
-    out_ref[0] = y3_ref[0]
-    out_ref[1] = y4_ref[...]
-
-
-def returns_kernel(start, order, k_ref, v_ref, kn_ref, vn_ref, y1_ref, y2_ref, *rest):
-    y34_refs = rest[:4]
-    key_hbm, value_hbm, key_buf, value_buf, st, sem = rest[-6:]
-    heads = y1_ref.shape[0]
-    each = heads // 4
-    count = key_buf.shape[1] // DH
-    near_start = start % (kn_ref.shape[1] // DH)
-    bits, spot = place()
-    for j in range(4):
-        for i in range(each):
-            head = (spot ^ j) * each + i
 
             @pl.when((head >= start) & (head < start + count))
             def _():
-                parts = level_states(0, y1_ref, y2_ref, y34_refs, bits, head, j, i)
-                st[head] = (parts[0] + parts[1] + parts[2] + parts[3]).astype(bf16)
+                levels = level_states(0, y1_ref, y2_ref, y34_refs, bits, head, j, i)
+                st[head] = (levels[0] + levels[1] + levels[2] + levels[3]).astype(bf16)
 
     for i in range(count):
         head = start + i
         c = slice(head * DH, (head + 1) * DH)
-        n = slice((near_start + i) * DH, (near_start + i + 1) * DH)
         o = slice(i * DH, (i + 1) * DH)
-        key_buf[:, o] = (kn_ref[:, n] + SCALE * mm(v_ref[:, c], st[head], 1, 0)).astype(bf16)
-        value_buf[:, o] = (vn_ref[:, n] + SCALE * mm(k_ref[:, c], st[head], 1, 1)).astype(bf16)
+        (kn_ref, kc), (vn_ref, vc) = kn_spots[i], vn_spots[i]
+        key_buf[:, o] = (kn_ref[:, kc] + SCALE * mm(v_ref[:, c], st[head], 1, 0)).astype(bf16)
+        value_buf[:, o] = (vn_ref[:, vc] + SCALE * mm(k_ref[:, c], st[head], 1, 1)).astype(bf16)
     cols = pl.ds(start * DH, count * DH)
     key_copy = pltpu.make_async_copy(key_buf, key_hbm.at[:, cols], sem.at[0])
     value_copy = pltpu.make_async_copy(value_buf, value_hbm.at[:, cols], sem.at[1])
@@ -315,13 +354,13 @@
     )
     tokens = [in_hbm(x) for x in (queries, keys, values, out_grad)]
 
-    def near_part(after, start):
+    def near_part(after, start, count=each):
         return pl.pallas_call(
             group_kernel,
-            grid=(each,),
+            grid=(count,),
             in_specs=[anywhere] + [token_spec(start)] * 4 + [fixed((length, 8))],
             out_specs=[token_spec(0)] * 3 + [fixed((length, DH))],
-            out_shape=[sds((length, each * DH), f32)] * 3 + [sds((length, DH), f32)],
+            out_shape=[sds((length, count * DH), f32)] * 3 + [sds((length, DH), f32)],
             compiler_params=near_params,
             cost_estimate=cost,
             name="group",
@@ -352,57 +391,78 @@
     )
     got, y2 = flip(send, "seq", 1), flip(near_sum, "seq", 3)
     near_parts.append(near_part(own, 2 * each))
-    rows, near = local_step(
-        rows_kernel, [own, got], [near_parts[2][0], near], [quarter, near.shape], "rows", {3: 1}
-    )
-    other, y1 = flip(rows, "seq", 4), flip(near, "seq", 1)
-    near_parts.append(near_part(rows, 3 * each))
+    (near,) = local_step(gate_kernel, [], [near_parts[2][0], near], [near.shape], "gate", {1: 0})
+    y1 = flip(near, "seq", 1)
+    three, four = local_step(
+        rows_kernel, [own, got], [near_parts[2][0]], [quarter[1:]] * 2, "rows"
+    )
+    other4, y3 = flip(four, "seq", 4), flip(three, "seq", 4)
+    near_parts.append(near_part(four, 3 * each, each // 2))
     (far4,) = local_step(
-        cross_kernel, [rows, other], [y2, near_parts[3][0]], [quarter[1:]], "cross"
+        cross_kernel, [four, other4], [y2, near_parts[3][0]], [quarter[1:]], "cross"
     )
     y4 = flip(far4, "seq", 12)
-    (y34,) = local_step(pack_kernel, [other, y4], [y1], [quarter], "pack")
-    y34s = [y34] + [flip(y34, "seq", m) for m in (1, 2, 3)]
-    qn, lam = pl.pallas_call(
+    near_parts.append(near_part(far4, 3 * each + each // 2, each // 2))
+    (y34,) = local_step(pack_kernel, [y3, y4], [y1, near_parts[4][0]], [quarter], "pack")
+    y34_one, y34_three = flip(y34, "seq", 1), flip(y34, "seq", 3)
+    qn, lam, y34_late = pl.pallas_call(
         near_reads_kernel,
-        in_specs=[anywhere, scalar] + [whole] * (5 + 2 * len(near_parts)),
-        out_specs=[whole] * 2,
-        out_shape=[sds((length, heads * DH), f32), sds((length, DH), f32)],
+        in_specs=[scalar] + [whole] * (6 + 2 * len(near_parts)),
+        out_specs=[whole] * 3,
+        out_shape=[sds((length, heads * DH), f32), sds((length, DH), f32), sds(quarter, f32)],
         scratch_shapes=[pltpu.VMEM((heads, DH, 2 * DH), bf16)],
         compiler_params=limit(16),
         cost_estimate=cost,
         name="near_reads",
     )(
-        y34, reach, queries, out_grad, w_cols, y1, y2,
+        reach, y34, queries, out_grad, w_cols, y1, y2,
         *[p[0] for p in near_parts], *[p[3] for p in near_parts],
     )
-
-    query_grad, total = pl.pallas_call(
-        reads_kernel,
-        in_specs=[scalar] + [whole] * 10,
-        out_specs=[anywhere, whole],
-        out_shape=[sds((length, heads * DH), bf16), sds((8, names), f32)],
-        scratch_shapes=[
-            pltpu.VMEM((heads, DH, 2 * DH), bf16),
-            pltpu.VMEM((length, heads * DH), bf16),
-            pltpu.SemaphoreType.DMA((length // CHUNK,)),
-        ],
-        compiler_params=limit(24),
-        cost_estimate=cost,
-        name="reads",
-    )(reach, queries, out_grad, w_cols, qn, lam, index_row, *y34s)
-    arrived = (y1, y2, *y34s)
-
-    def returns(order, start, count, held):
-        kn, vn = near_parts[start // each][1:3]
-        shape = sds((length, heads * DH), bf16)
-
-        def kernel(*refs):
-            returns_kernel(start, *refs)
-
+    y34_two = flip(y34_late, "seq", 2)
+    y34s = [y34, y34_one, y34_two, y34_three]
+
+    def far_part(kernel, count, ins, afters, more_out, aliases, name):
         return pl.pallas_call(
             kernel,
-            in_specs=[scalar] + [whole] * 10 + [anywhere] * len(held),
+            in_specs=[scalar] + [whole] * (5 + len(ins)) + [anywhere] * len(afters),
+            out_specs=[anywhere, whole],
+            out_shape=[sds((length, heads * DH), bf16), more_out],
+            input_output_aliases=aliases,
+            scratch_shapes=[
+                pltpu.VMEM((count * each, DH, 2 * DH), bf16),
+                pltpu.VMEM((length, count * each * DH), bf16),
+                pltpu.SemaphoreType.DMA((length // CHUNK, count)),
+            ],
+            compiler_params=limit(16),
+            cost_estimate=cost,
+            name=name,
+        )(reach, queries, out_grad, w_cols, qn, lam, *ins, *afters)
+
+    query_grad, lam = far_part(
+        first_reads_kernel,
+        len(FIRST_SPOTS),
+        [y34s[j] for j in FIRST_SPOTS],
+        [],
+        sds((length, DH), f32),
+        {},
+        "first_reads",
+    )
+    query_grad, total = far_part(
+        last_reads_kernel, 1, [y34_two, index_row], [query_grad], sds((8, names), f32), {8: 0}, "last_reads"
+    )
+    arrived = (y1, y2, *y34s)
+
+    def returns(order, start, count, held):
+        pieces = near_parts[3:] if start == 3 * each else [near_parts[start // each]]
+        ins = [keys, values] + [p[1] for p in pieces] + [p[2] for p in pieces] + list(arrived)
+        shape = sds((length, heads * DH), bf16)
+
+        def kernel(*refs):
+            returns_kernel(start, len(pieces), *refs)
+
+        return pl.pallas_call(
+            kernel,
+            in_specs=[scalar] + [whole] * len(ins) + [anywhere] * len(held),
             out_specs=[anywhere] * 2,
             out_shape=[shape] * 2,
             scratch_shapes=[
@@ -411,11 +471,11 @@
                 pltpu.VMEM((heads, DH, DH), bf16),
                 pltpu.SemaphoreType.DMA((2,)),
             ],
-            input_output_aliases={11: 0, 12: 1} if held else {},
+            input_output_aliases={len(ins) + 1: 0, len(ins) + 2: 1} if held else {},
             compiler_params=limit(20),
             cost_estimate=cost,
             name="returns",
-        )(order, keys, values, kn, vn, *arrived, *held)
+        )(order, *ins, *held)
 
     got = [flip(total, "head", 1)]
     held = returns(tie(reach, total), 0, each, ())

time: 89.9 us -> 89.2 us (level)
  waiting for transfers between devices: 19 us -> 14.1 us
  starting transfers between devices: 28.5 us -> 30.8 us
  Pallas kernels: 38.4 us -> 40.3 us
    ppermute x20 -> x21, waiting for transfers between devices: 19 us -> 14.1 us  [flip(): lax.ppermute(x, axis, [(i, i ^ mask) for i in range(lax.axis_size(axis))])]
    ppermute x20 -> x21, starting transfers between devices: 28.5 us -> 30.8 us  [flip(): lax.ppermute(x, axis, [(i, i ^ mask) for i in range(lax.axis_size(axis))])]
    pallas_call x10 -> x12, Pallas kernels: 32.1 us -> 34 us  [the longest x5 20.4 us: near_part(): pl.pallas_call(group_kernel, grid=(count,), in_specs=[anywhere] + [token_...]
  transfers between devices with their start and end apart: 20 -> 21, of which waited for: 10 -> 10; matrix products, arithmetic and copies ran while one was open for 0% -> 0% of each run, Pallas kernels for 31% -> 35%
where the time goes in v6:
time: 89.2 us; the launch traced here: 88.9 us
  Pallas kernels  40.3 us (45%)
  starting transfers between devices  30.8 us (35%)
  waiting for transfers between devices  14.1 us (16%)
  local copies, waits for them, and re-layouts  1.59 us (2%)
  between operations  1.53 us (2%)
    ppermute x21, starting transfers between devices, flip(): lax.ppermute(x, axis, [(i, i ^ mask) for i in range(lax.axis_size(axis))])  30.8 us
    pallas_call x5, Pallas kernels, near_part(): pl.pallas_call(group_kernel, grid=(count,), in_specs=[anywhere] + [token_...  20.4 us
    ppermute x21, waiting for transfers between devices, flip(): lax.ppermute(x, axis, [(i, i ^ mask) for i in range(lax.axis_size(axis))])  14.1 us
    pallas_call x4, Pallas kernels, returns(): pl.pallas_call(kernel, in_specs=[scalar] + [whole] * len(ins) + [anywhere...  6.31 us
    pallas_call x1, Pallas kernels, local(): pl.pallas_call(states_kernel, in_specs=[scalar, whole, whole] + [anywhere...  6.11 us
    pallas_call x2, Pallas kernels, far_part(): pl.pallas_call(kernel, in_specs=[scalar] + [whole] * (5 + len(ins)) + [an...  5.26 us
    pallas_call x1, Pallas kernels, local(): pl.pallas_call(near_reads_kernel, in_specs=[scalar] + [whole] * (6 + 2 *...  2.02 us
  transfers between devices with their start and end apart: 21, of which 10 were waited for; matrix products, arithmetic and copies ran while one was open for 0% of the time, Pallas kernels for 35%

profile of v6, /device:TPU:0, one launch (start us, length us, event | category | flops | bytes accessed | tf_op | source)
XLA Modules:
  0.0 88.9 jit_solution(11965191378794784002)
XLA Ops:
  1.3 0.0 copy-start.4
  1.3 0.7 copy-done.4
  2.0 0.7 copy-done.6
  2.7 6.1 %states.1 = (f32[8,1024]{1,0:T(8,128)S(1)}, f32[8,128,128]{2,1,0:T(8,128)S(1)}, f32[8,128,128]{2,1,0:T(8,128)S(1)}, f32[2,2,2,128,128]{4,3,2,1,0:T(8,128)S(1)}, f32[2,2,2,128,128]{4,3,2,1,0:T(8,128)}) custom-call(s32[1]{0:T(128)S(6)} %copy.28.reach.refs_0_, s32[1,1024]{1,0:T(1,128)S(1)} %bitcast.10, f32[5,256]{1,0:T(8,128)S(1)} %copy-done.6, ...), custom_call_target="tpu_custom_call" | custom-call | tf_op jit(solution)/shard_map/states/pallas_call | solution.py:332
  8.8 4.3 %collective-permute-start = (f32[2,2,2,128,128]{4,3,2,1,0:T(8,128)}, f32[2,2,2,128,128]{4,3,2,1,0:T(8,128)S(1)}, u32[]{:S(2)}, u32[]{:S(2)}) collective-permute-start(f32[2,2,2,128,128]{4,3,2,1,0:T(8,128)} %get-tuple-element.65), channel_id=1, source_target_pairs={{0,24},{8,16},{16,8},{24,0},{32,56},{40,48},{48,40},{56,32},{64,88... | collective-permute-start | bytes 1572872 | tf_op jit(solution)/shard_map/ppermute | solution.py:307
  13.1 0.0 collective-permute-start.1
  13.1 0.2 copy.19
  13.3 4.8 %group.5 = (f32[1024,256]{1,0:T(8,128)S(1)}, f32[1024,256]{1,0:T(8,128)S(1)}, f32[1024,256]{1,0:T(8,128)S(1)}, f32[1024,128]{1,0:T(8,128)S(1)}) custom-call(f32[2,2,2,128,128]{4,3,2,1,0:T(8,128)S(1)} %get-tuple-element.64.after.keep_ref, bf16[1024,1024]{1,0:T(8,128)(2,1)} %q_ref.15, bf16[1024,1024]{1,0:T(8,128)(2,1)} %refs_1_.7, bf16[1024,1024]{1,0:T(8,128)(2,1)} %refs_2_.7, ...), custom_call_target="tpu_custom_call" | custom-call | flops 100000000 | bytes 1048576 | tf_op jit(solution)/shard_map/group/pallas_call | solution.py:358
  18.1 4.9 %group.6 = (f32[1024,256]{1,0:T(8,128)S(1)}, f32[1024,256]{1,0:T(8,128)S(1)}, f32[1024,256]{1,0:T(8,128)S(1)}, f32[1024,128]{1,0:T(8,128)S(1)}) custom-call(f32[1024,256]{1,0:T(8,128)S(1)} %get-tuple-element.67.after.rest_0_, bf16[1024,1024]{1,0:T(8,128)(2,1)} %q_ref.15, bf16[1024,1024]{1,0:T(8,128)(2,1)} %refs_1_.7, bf16[1024,1024]{1,0:T(8,128)(2,1)} %refs_2_.7, ...), custom_call_target="tpu_custom_call" | custom-call | flops 100000000 | bytes 1048576 | tf_op jit(solution)/shard_map/group/pallas_call | solution.py:358
  23.0 2.2 %collective-permute-done.got_ref = f32[2,2,2,128,128]{4,3,2,1,0:T(8,128)S(1)} collective-permute-done((f32[2,2,2,128,128]{4,3,2,1,0:T(8,128)}, f32[2,2,2,128,128]{4,3,2,1,0:T(8,128)S(1)}, u32[]{:S(2)}, u32[]{:S(2)}) %collective-permute-start) | collective-permute-done | bytes 524320 | tf_op jit(solution)/shard_map/ppermute | solution.py:307
  25.2 1.2 %collective-permute-done.1.near_got_ref = f32[8,128,128]{2,1,0:T(8,128)S(1)} collective-permute-done((f32[8,128,128]{2,1,0:T(8,128)S(1)}, f32[8,128,128]{2,1,0:T(8,128)S(1)}, u32[]{:S(2)}, u32[]{:S(2)}) %collective-permute-start.1) | collective-permute-done | bytes 524320 | tf_op jit(solution)/shard_map/ppermute | solution.py:307
  26.5 0.1 pair.1
  26.6 1.8 %collective-permute-start.5 = (f32[8,128,128]{2,1,0:T(8,128)S(1)}, f32[8,128,128]{2,1,0:T(8,128)S(1)}, u32[]{:S(2)}, u32[]{:S(2)}) collective-permute-start(f32[8,128,128]{2,1,0:T(8,128)S(1)} %get-tuple-element.74), channel_id=1, source_target_pairs={{0,24},{8,16},{16,8},{24,0},{32,56},{40,48},{48,40},{56,32},{64,88... | collective-permute-start | bytes 1572872 | tf_op jit(solution)/shard_map/ppermute | solution.py:307
  28.4 0.0 collective-permute-start.2
  28.4 4.8 %group.7 = (f32[1024,256]{1,0:T(8,128)S(1)}, f32[1024,256]{1,0:T(8,128)S(1)}, f32[1024,256]{1,0:T(8,128)S(1)}, f32[1024,128]{1,0:T(8,128)S(1)}) custom-call(f32[2,2,128,128]{3,2,1,0:T(8,128)S(1)} %get-tuple-element.69.after.own_ref, bf16[1024,1024]{1,0:T(8,128)(2,1)} %q_ref.15, bf16[1024,1024]{1,0:T(8,128)(2,1)} %refs_1_.7, bf16[1024,1024]{1,0:T(8,128)(2,1)} %refs_2_.7, ...), custom_call_target="tpu_custom_call" | custom-call | flops 100000000 | bytes 1048576 | tf_op jit(solution)/shard_map/group/pallas_call | solution.py:358
  33.2 2.1 %collective-permute-start.7 = (f32[8,128,128]{2,1,0:T(8,128)S(1)}, f32[8,128,128]{2,1,0:T(8,128)S(1)}, u32[]{:S(2)}, u32[]{:S(2)}) collective-permute-start(f32[8,128,128]{2,1,0:T(8,128)S(1)} %gate.1), channel_id=1, source_target_pairs={{0,8},{8,0},{16,24},{24,16},{32,40},{40,32},{48,56},{56,48},{64,72... | collective-permute-start | bytes 1572872 | tf_op jit(solution)/shard_map/ppermute | solution.py:307
  35.3 0.5 collective-permute-done.2.got_ref
  35.9 1.6 %collective-permute-start.4 = (f32[2,128,128]{2,1,0:T(8,128)S(1)}, f32[2,128,128]{2,1,0:T(8,128)S(1)}, u32[]{:S(2)}, u32[]{:S(2)}) collective-permute-start(f32[2,128,128]{2,1,0:T(8,128)S(1)} %get-tuple-element.73.after.rows_ref), channel_id=1, source_target_pairs={{0,32},{8,40},{16,48},{24,56},{32,0},{40,8},{48,16},{56,24},{64,96... | collective-permute-start | bytes 393224 | tf_op jit(solution)/shard_map/ppermute | solution.py:307
  37.5 0.5 collective-permute-start.3
  38.0 2.8 %group.8 = (f32[1024,128]{1,0:T(8,128)S(1)}, f32[1024,128]{1,0:T(8,128)S(1)}, f32[1024,128]{1,0:T(8,128)S(1)}, f32[1024,128]{1,0:T(8,128)S(1)}) custom-call(f32[2,128,128]{2,1,0:T(8,128)S(1)} %get-tuple-element.73.after.rows_ref, bf16[1024,1024]{1,0:T(8,128)(2,1)} %q_ref.15, bf16[1024,1024]{1,0:T(8,128)(2,1)} %refs_1_.7, bf16[1024,1024]{1,0:T(8,128)(2,1)} %refs_2_.7, ...), custom_call_target="tpu_custom_call" | custom-call | flops 100000000 | bytes 1048576 | tf_op jit(solution)/shard_map/group/pallas_call | solution.py:358
  40.9 0.1 collective-permute-done.4.other_ref
  40.9 0.0 collective-permute-done.5.after.y2_ref.refs_6_.refs_8_
  41.0 3.1 %collective-permute-start.6 = (f32[2,128,128]{2,1,0:T(8,128)S(1)}, f32[2,128,128]{2,1,0:T(8,128)S(1)}, u32[]{:S(2)}, u32[]{:S(2)}) collective-permute-start(f32[2,128,128]{2,1,0:T(8,128)S(1)} %cross.1.after), channel_id=1, source_target_pairs={{0,96},{8,104},{16,112},{24,120},{32,64},{40,72},{48,80},{56,88},{... | collective-permute-start | bytes 393224 | tf_op jit(solution)/shard_map/ppermute | solution.py:307
  44.1 3.0 %group.9 = (f32[1024,128]{1,0:T(8,128)S(1)}, f32[1024,128]{1,0:T(8,128)S(1)}, f32[1024,128]{1,0:T(8,128)S(1)}, f32[1024,128]{1,0:T(8,128)S(1)}) custom-call(f32[2,128,128]{2,1,0:T(8,128)S(1)} %cross.1.after, bf16[1024,1024]{1,0:T(8,128)(2,1)} %q_ref.15, bf16[1024,1024]{1,0:T(8,128)(2,1)} %refs_1_.7, bf16[1024,1024]{1,0:T(8,128)(2,1)} %refs_2_.7, ...), custom_call_target="tpu_custom_call" | custom-call | flops 100000000 | bytes 1048576 | tf_op jit(solution)/shard_map/group/pallas_call | solution.py:358
  47.1 0.0 collective-permute-done.3.y3_ref
  47.1 0.0 collective-permute-done.7.rest_0_.y1_ref.refs_5_.refs_7_
  47.1 0.1 collective-permute-done.6.y4_ref
  47.2 1.5 %collective-permute-start.9 = (f32[2,2,128,128]{3,2,1,0:T(8,128)S(1)}, f32[2,2,128,128]{3,2,1,0:T(8,128)S(1)}, u32[]{:S(2)}, u32[]{:S(2)}) collective-permute-start(f32[2,2,128,128]{3,2,1,0:T(8,128)S(1)} %pack.1.y34_ref.rest_0_.refs_7_.refs_9_), channel_id=1, source_target_pairs={{0,24},{8,16},{16,8},{24,0},{32,56},{40,48},{48,40},{56,32},{64,88... | collective-permute-start | bytes 786440 | tf_op jit(solution)/shard_map/ppermute | solution.py:307
  48.7 0.0 collective-permute-start.8
  48.7 0.0 copy-done.2
  48.7 0.0 copy-done.3
  48.7 2.0 %near_reads.1 = (f32[1024,1024]{1,0:T(8,128)S(1)}, f32[1024,128]{1,0:T(8,128)S(1)}, f32[2,2,128,128]{3,2,1,0:T(8,128)S(1)}) custom-call(s32[1]{0:T(128)S(6)} %copy.28.reach.refs_0_, f32[2,2,128,128]{3,2,1,0:T(8,128)S(1)} %pack.1.y34_ref.rest_0_.refs_7_.refs_9_, bf16[1024,1024]{1,0:T(8,128)(2,1)S(1)} %copy-done.2, bf16[1024,1024]{1,0:T(8,128)(2,1)S(1)} %copy-done.3, ...), custom_call_target="tpu_custom_call" | custom-call | flops 100000000 | bytes 1048576 | tf_op jit(solution)/shard_map/near_reads/pallas_call | solution.py:408
  50.8 3.4 %collective-permute-start.10 = (f32[2,2,128,128]{3,2,1,0:T(8,128)S(1)}, f32[2,2,128,128]{3,2,1,0:T(8,128)S(1)}, u32[]{:S(2)}, u32[]{:S(2)}) collective-permute-start(f32[2,2,128,128]{3,2,1,0:T(8,128)S(1)} %get-tuple-element.86), channel_id=1, source_target_pairs={{0,16},{8,24},{16,0},{24,8},{32,48},{40,56},{48,32},{56,40},{64,80... | collective-permute-start | bytes 786440 | tf_op jit(solution)/shard_map/ppermute | solution.py:307
  54.1 3.6 %collective-permute-done.9.rest_2_.refs_10_.refs_12_ = f32[2,2,128,128]{3,2,1,0:T(8,128)S(1)} collective-permute-done((f32[2,2,128,128]{3,2,1,0:T(8,128)S(1)}, f32[2,2,128,128]{3,2,1,0:T(8,128)S(1)}, u32[]{:S(2)}, u32[]{:S(2)}) %collective-permute-start.9) | collective-permute-done | bytes 262176 | tf_op jit(solution)/shard_map/ppermute | solution.py:307
  57.7 0.0 collective-permute-done.8.rest_1_.refs_8_.refs_10_
  57.7 2.8 %first_reads.1 = (bf16[1024,1024]{1,0:T(8,128)(2,1)}, f32[1024,128]{1,0:T(8,128)S(1)}) custom-call(s32[1]{0:T(128)S(6)} %copy.28.reach.refs_0_, bf16[1024,1024]{1,0:T(8,128)(2,1)S(1)} %copy-done.2, bf16[1024,1024]{1,0:T(8,128)(2,1)S(1)} %copy-done.3, f32[1024,8]{1,0:T(8,128)S(1)} %bitcast.8, f32[1024,1024]{1,0:T(8,128)S(1)} %get-tuple-element.83.qn_ref, ...), custom_call_target="tpu_custom_call" | custom-call | flops 100000000 | bytes 1048576 | tf_op jit(solution)/shard_map/first_reads/pallas_call | solution.py:425
  60.5 0.7 collective-permute-done.10.y34_ref.refs_9_.refs_11_
  61.2 0.0 copy-done.5
  61.3 2.5 %last_reads.1 = (bf16[1024,1024]{1,0:T(8,128)(2,1)}, f32[8,256]{1,0:T(8,128)S(1)}) custom-call(s32[1]{0:T(128)S(6)} %copy.28.reach.refs_0_, bf16[1024,1024]{1,0:T(8,128)(2,1)S(1)} %copy-done.2, bf16[1024,1024]{1,0:T(8,128)(2,1)S(1)} %copy-done.3, f32[1024,8]{1,0:T(8,128)S(1)} %bitcast.9, ...), custom_call_target="tpu_custom_call", output_to_operand_aliasing={{0}: (8, {})} | custom-call | flops 100000000 | bytes 1048576 | tf_op jit(solution)/shard_map/last_reads/pallas_call | solution.py:425
  63.7 0.1 collective-permute-start.11
  63.8 1.6 %returns.4 = (bf16[1024,1024]{1,0:T(8,128)(2,1)}, bf16[1024,1024]{1,0:T(8,128)(2,1)}) custom-call(s32[1]{0:T(128)S(6)} %copy.28.reach.refs_0_, bf16[1024,1024]{1,0:T(8,128)(2,1)S(1)} %copy-done, bf16[1024,1024]{1,0:T(8,128)(2,1)S(1)} %copy-done.1, f32[1024,256]{1,0:T(8,128)S(1)} %get-tuple-element.91.refs_3_, f32[1024,256]{1,0:T(8,128)S(1)} %get-tuple-element.92.refs_4_, ...), custom_call_target="tpu_custom_call" | custom-call | flops 100000000 | bytes 1048576 | tf_op jit(solution)/shard_map/returns/pallas_call | solution.py:463
  65.4 0.0 collective-permute-done.11
  65.5 2.8 %collective-permute-start.14 = (f32[8,256]{1,0:T(8,128)S(1)}, f32[8,256]{1,0:T(8,128)S(1)}, u32[]{:S(2)}, u32[]{:S(2)}) collective-permute-start(f32[8,256]{1,0:T(8,128)S(1)} %add.30), channel_id=1, source_target_pairs={{0,6},{1,7},{2,4},{3,5},{4,2},{5,3},{6,0},{7,1},{8,14},{9,15},{10,... | collective-permute-start | bytes 24584 | tf_op jit(solution)/shard_map/ppermute | solution.py:307
  68.3 0.8 collective-permute-start.13
  69.1 0.6 collective-permute-start.12
  69.6 1.7 %returns.5 = (bf16[1024,1024]{1,0:T(8,128)(2,1)}, bf16[1024,1024]{1,0:T(8,128)(2,1)}) custom-call(s32[1]{0:T(128)S(6)} %copy.28.reach.refs_0_, bf16[1024,1024]{1,0:T(8,128)(2,1)S(1)} %copy-done, bf16[1024,1024]{1,0:T(8,128)(2,1)S(1)} %copy-done.1, f32[1024,256]{1,0:T(8,128)S(1)} %get-tuple-element.97.refs_3_, ...), custom_call_target="tpu_custom_call", output_to_operand_aliasing={{0}: (11, {}), {1}: (12, {})} | custom-call | flops 100000000 | bytes 1048576 | tf_op jit(solution)/shard_map/returns/pallas_call | solution.py:463
  71.4 0.0 collective-permute-done.14
  71.4 2.1 %collective-permute-done.13 = f32[8,256]{1,0:T(8,128)S(1)} collective-permute-done((f32[8,256]{1,0:T(8,128)S(1)}, f32[8,256]{1,0:T(8,128)S(1)}, u32[]{:S(2)}, u32[]{:S(2)}) %collective-permute-start.13) | collective-permute-done | bytes 8224 | tf_op jit(solution)/shard_map/ppermute | solution.py:307
  73.4 0.0 collective-permute-done.12
  73.5 1.5 %collective-permute-start.17 = (f32[8,256]{1,0:T(8,128)S(1)}, f32[8,256]{1,0:T(8,128)S(1)}, u32[]{:S(2)}, u32[]{:S(2)}) collective-permute-start(f32[8,256]{1,0:T(8,128)S(1)} %add_add_fusion.1), channel_id=1, source_target_pairs={{0,24},{8,16},{16,8},{24,0},{32,56},{40,48},{48,40},{56,32},{64,88... | collective-permute-start | bytes 24584 | tf_op jit(solution)/shard_map/ppermute | solution.py:307
  74.9 0.8 collective-permute-start.16
  75.7 1.9 %collective-permute-start.15 = (f32[8,256]{1,0:T(8,128)S(1)}, f32[8,256]{1,0:T(8,128)S(1)}, u32[]{:S(2)}, u32[]{:S(2)}) collective-permute-start(f32[8,256]{1,0:T(8,128)S(1)} %add_add_fusion.1), channel_id=1, source_target_pairs={{0,8},{8,0},{16,24},{24,16},{32,40},{40,32},{48,56},{56,48},{64,72... | collective-permute-start | bytes 24584 | tf_op jit(solution)/shard_map/ppermute | solution.py:307
  77.6 1.5 %returns.6 = (bf16[1024,1024]{1,0:T(8,128)(2,1)}, bf16[1024,1024]{1,0:T(8,128)(2,1)}) custom-call(s32[1]{0:T(128)S(6)} %copy.28.reach.refs_0_, bf16[1024,1024]{1,0:T(8,128)(2,1)S(1)} %copy-done, bf16[1024,1024]{1,0:T(8,128)(2,1)S(1)} %copy-done.1, f32[1024,256]{1,0:T(8,128)S(1)} %get-tuple-element.105.refs_3_, ...), custom_call_target="tpu_custom_call", output_to_operand_aliasing={{0}: (11, {}), {1}: (12, {})} | custom-call | flops 100000000 | bytes 1048576 | tf_op jit(solution)/shard_map/returns/pallas_call | solution.py:463
  79.2 0.0 collective-permute-done.17
  79.2 0.9 %collective-permute-done.16 = f32[8,256]{1,0:T(8,128)S(1)} collective-permute-done((f32[8,256]{1,0:T(8,128)S(1)}, f32[8,256]{1,0:T(8,128)S(1)}, u32[]{:S(2)}, u32[]{:S(2)}) %collective-permute-start.16) | collective-permute-done | bytes 8224 | tf_op jit(solution)/shard_map/ppermute | solution.py:307
  80.1 0.0 collective-permute-done.15
  80.1 3.1 %collective-permute-start.20 = (f32[8,256]{1,0:T(8,128)S(1)}, f32[8,256]{1,0:T(8,128)S(1)}, u32[]{:S(2)}, u32[]{:S(2)}) collective-permute-start(f32[8,256]{1,0:T(8,128)S(1)} %add_add_fusion), channel_id=1, source_target_pairs={{0,96},{8,104},{16,112},{24,120},{32,64},{40,72},{48,80},{56,88},{... | collective-permute-start | bytes 24584 | tf_op jit(solution)/shard_map/ppermute | solution.py:307
  83.2 0.5 collective-permute-start.19
  83.7 0.6 collective-permute-start.18
  84.3 1.5 %returns.7 = (bf16[1024,1024]{1,0:T(8,128)(2,1)}, bf16[1024,1024]{1,0:T(8,128)(2,1)}) custom-call(s32[1]{0:T(128)S(6)} %copy.28.reach.refs_0_, bf16[1024,1024]{1,0:T(8,128)(2,1)S(1)} %copy-done, bf16[1024,1024]{1,0:T(8,128)(2,1)S(1)} %copy-done.1, f32[1024,128]{1,0:T(8,128)S(1)} %get-tuple-element.113.refs_3_, ...), custom_call_target="tpu_custom_call", output_to_operand_aliasing={{0}: (13, {}), {1}: (14, {})} | custom-call | flops 100000000 | bytes 1048576 | tf_op jit(solution)/shard_map/returns/pallas_call | solution.py:463
  85.8 0.0 collective-permute-done.20
  85.8 2.6 %collective-permute-done.19 = f32[8,256]{1,0:T(8,128)S(1)} collective-permute-done((f32[8,256]{1,0:T(8,128)S(1)}, f32[8,256]{1,0:T(8,128)S(1)}, u32[]{:S(2)}, u32[]{:S(2)}) %collective-permute-start.19) | collective-permute-done | bytes 8224 | tf_op jit(solution)/shard_map/ppermute | solution.py:307
  88.3 0.0 collective-permute-done.18
  88.3 0.6 fusion.1
  (15 shorter events, 0.1 us)
Async XLA Ops:
  1.3 0.7 copy-start.4
  2.0 0.7 copy-start.6
  8.8 16.4 %collective-permute-start = (f32[2,2,2,128,128]{4,3,2,1,0:T(8,128)}, f32[2,2,2,128,128]{4,3,2,1,0:T(8,128)S(1)}, u32[]{:S(2)}, u32[]{:S(2)}) collective-permute-start(f32[2,2,2,128,128]{4,3,2,1,0:T(8,128)} %get-tuple-element.65), channel_id=1, source_target_pairs={{0,24},{8,16},{16,8},{24,0},{32,56},{40,48},{48,40},{56,32},{64,88... | collective-permute-start | bytes 1572872 | tf_op jit(solution)/shard_map/ppermute | solution.py:307
  13.1 13.4 %collective-permute-start.1 = (f32[8,128,128]{2,1,0:T(8,128)S(1)}, f32[8,128,128]{2,1,0:T(8,128)S(1)}, u32[]{:S(2)}, u32[]{:S(2)}) collective-permute-start(f32[8,128,128]{2,1,0:T(8,128)S(1)} %get-tuple-element.66.near_ref), channel_id=1, source_target_pairs={{0,8},{8,0},{16,24},{24,16},{32,40},{40,32},{48,56},{56,48},{64,72... | collective-permute-start | bytes 1572872 | tf_op jit(solution)/shard_map/ppermute | solution.py:307
  26.6 14.4 %collective-permute-start.5 = (f32[8,128,128]{2,1,0:T(8,128)S(1)}, f32[8,128,128]{2,1,0:T(8,128)S(1)}, u32[]{:S(2)}, u32[]{:S(2)}) collective-permute-start(f32[8,128,128]{2,1,0:T(8,128)S(1)} %get-tuple-element.74), channel_id=1, source_target_pairs={{0,24},{8,16},{16,8},{24,0},{32,56},{40,48},{48,40},{56,32},{64,88... | collective-permute-start | bytes 1572872 | tf_op jit(solution)/shard_map/ppermute | solution.py:307
  28.4 7.5 %collective-permute-start.2 = (f32[2,2,128,128]{3,2,1,0:T(8,128)S(1)}, f32[2,2,128,128]{3,2,1,0:T(8,128)S(1)}, u32[]{:S(2)}, u32[]{:S(2)}) collective-permute-start(f32[2,2,128,128]{3,2,1,0:T(8,128)S(1)} %get-tuple-element.70), channel_id=1, source_target_pairs={{0,8},{8,0},{16,24},{24,16},{32,40},{40,32},{48,56},{56,48},{64,72... | collective-permute-start | bytes 786440 | tf_op jit(solution)/shard_map/ppermute | solution.py:307
  33.2 13.9 %collective-permute-start.7 = (f32[8,128,128]{2,1,0:T(8,128)S(1)}, f32[8,128,128]{2,1,0:T(8,128)S(1)}, u32[]{:S(2)}, u32[]{:S(2)}) collective-permute-start(f32[8,128,128]{2,1,0:T(8,128)S(1)} %gate.1), channel_id=1, source_target_pairs={{0,8},{8,0},{16,24},{24,16},{32,40},{40,32},{48,56},{56,48},{64,72... | collective-permute-start | bytes 1572872 | tf_op jit(solution)/shard_map/ppermute | solution.py:307
  35.9 5.0 %collective-permute-start.4 = (f32[2,128,128]{2,1,0:T(8,128)S(1)}, f32[2,128,128]{2,1,0:T(8,128)S(1)}, u32[]{:S(2)}, u32[]{:S(2)}) collective-permute-start(f32[2,128,128]{2,1,0:T(8,128)S(1)} %get-tuple-element.73.after.rows_ref), channel_id=1, source_target_pairs={{0,32},{8,40},{16,48},{24,56},{32,0},{40,8},{48,16},{56,24},{64,96... | collective-permute-start | bytes 393224 | tf_op jit(solution)/shard_map/ppermute | solution.py:307
  37.5 9.5 %collective-permute-start.3 = (f32[2,128,128]{2,1,0:T(8,128)S(1)}, f32[2,128,128]{2,1,0:T(8,128)S(1)}, u32[]{:S(2)}, u32[]{:S(2)}) collective-permute-start(f32[2,128,128]{2,1,0:T(8,128)S(1)} %get-tuple-element.72), channel_id=1, source_target_pairs={{0,32},{8,40},{16,48},{24,56},{32,0},{40,8},{48,16},{56,24},{64,96... | collective-permute-start | bytes 393224 | tf_op jit(solution)/shard_map/ppermute | solution.py:307
  41.0 6.3 %collective-permute-start.6 = (f32[2,128,128]{2,1,0:T(8,128)S(1)}, f32[2,128,128]{2,1,0:T(8,128)S(1)}, u32[]{:S(2)}, u32[]{:S(2)}) collective-permute-start(f32[2,128,128]{2,1,0:T(8,128)S(1)} %cross.1.after), channel_id=1, source_target_pairs={{0,96},{8,104},{16,112},{24,120},{32,64},{40,72},{48,80},{56,88},{... | collective-permute-start | bytes 393224 | tf_op jit(solution)/shard_map/ppermute | solution.py:307
  44.1 4.7 %copy-start.2 = (bf16[1024,1024]{1,0:T(8,128)(2,1)S(1)}, bf16[1024,1024]{1,0:T(8,128)(2,1)}, u32[]{:S(2)}) copy-start(bf16[1024,1024]{1,0:T(8,128)(2,1)} %q_ref.15) | copy-start | bytes 6291460
  44.1 4.7 %copy-start.3 = (bf16[1024,1024]{1,0:T(8,128)(2,1)S(1)}, bf16[1024,1024]{1,0:T(8,128)(2,1)}, u32[]{:S(2)}) copy-start(bf16[1024,1024]{1,0:T(8,128)(2,1)} %g_ref.15) | copy-start | bytes 6291460
  47.2 10.5 %collective-permute-start.9 = (f32[2,2,128,128]{3,2,1,0:T(8,128)S(1)}, f32[2,2,128,128]{3,2,1,0:T(8,128)S(1)}, u32[]{:S(2)}, u32[]{:S(2)}) collective-permute-start(f32[2,2,128,128]{3,2,1,0:T(8,128)S(1)} %pack.1.y34_ref.rest_0_.refs_7_.refs_9_), channel_id=1, source_target_pairs={{0,24},{8,16},{16,8},{24,0},{32,56},{40,48},{48,40},{56,32},{64,88... | collective-permute-start | bytes 786440 | tf_op jit(solution)/shard_map/ppermute | solution.py:307
  48.7 9.0 %collective-permute-start.8 = (f32[2,2,128,128]{3,2,1,0:T(8,128)S(1)}, f32[2,2,128,128]{3,2,1,0:T(8,128)S(1)}, u32[]{:S(2)}, u32[]{:S(2)}) collective-permute-start(f32[2,2,128,128]{3,2,1,0:T(8,128)S(1)} %pack.1.y34_ref.rest_0_.refs_7_.refs_9_), channel_id=1, source_target_pairs={{0,8},{8,0},{16,24},{24,16},{32,40},{40,32},{48,56},{56,48},{64,72... | collective-permute-start | bytes 786440 | tf_op jit(solution)/shard_map/ppermute | solution.py:307
  50.8 10.5 %collective-permute-start.10 = (f32[2,2,128,128]{3,2,1,0:T(8,128)S(1)}, f32[2,2,128,128]{3,2,1,0:T(8,128)S(1)}, u32[]{:S(2)}, u32[]{:S(2)}) collective-permute-start(f32[2,2,128,128]{3,2,1,0:T(8,128)S(1)} %get-tuple-element.86), channel_id=1, source_target_pairs={{0,16},{8,24},{16,0},{24,8},{32,48},{40,56},{48,32},{56,40},{64,80... | collective-permute-start | bytes 786440 | tf_op jit(solution)/shard_map/ppermute | solution.py:307
  57.7 3.5 %copy-start.5 = (s32[1024]{0:T(1024)S(1)}, s32[1024]{0:T(1024)}, u32[]{:S(2)}) copy-start(s32[1024]{0:T(1024)} %param.12) | copy-start | bytes 12292
  61.2 2.6 %copy-start = (bf16[1024,1024]{1,0:T(8,128)(2,1)S(1)}, bf16[1024,1024]{1,0:T(8,128)(2,1)}, u32[]{:S(2)}) copy-start(bf16[1024,1024]{1,0:T(8,128)(2,1)} %refs_1_.7) | copy-start | bytes 6291460
  61.3 2.6 %copy-start.1 = (bf16[1024,1024]{1,0:T(8,128)(2,1)S(1)}, bf16[1024,1024]{1,0:T(8,128)(2,1)}, u32[]{:S(2)}) copy-start(bf16[1024,1024]{1,0:T(8,128)(2,1)} %refs_2_.7) | copy-start | bytes 6291460
  63.7 1.7 %collective-permute-start.11 = (f32[8,256]{1,0:T(8,128)S(1)}, f32[8,256]{1,0:T(8,128)S(1)}, u32[]{:S(2)}, u32[]{:S(2)}) collective-permute-start(f32[8,256]{1,0:T(8,128)S(1)} %get-tuple-element.89), channel_id=1, source_target_pairs={{0,1},{1,0},{2,3},{3,2},{4,5},{5,4},{6,7},{7,6},{8,9},{9,8},{10,11... | collective-permute-start | bytes 24584 | tf_op jit(solution)/shard_map/ppermute | solution.py:307
  65.5 5.9 %collective-permute-start.14 = (f32[8,256]{1,0:T(8,128)S(1)}, f32[8,256]{1,0:T(8,128)S(1)}, u32[]{:S(2)}, u32[]{:S(2)}) collective-permute-start(f32[8,256]{1,0:T(8,128)S(1)} %add.30), channel_id=1, source_target_pairs={{0,6},{1,7},{2,4},{3,5},{4,2},{5,3},{6,0},{7,1},{8,14},{9,15},{10,... | collective-permute-start | bytes 24584 | tf_op jit(solution)/shard_map/ppermute | solution.py:307
  68.3 5.2 %collective-permute-start.13 = (f32[8,256]{1,0:T(8,128)S(1)}, f32[8,256]{1,0:T(8,128)S(1)}, u32[]{:S(2)}, u32[]{:S(2)}) collective-permute-start(f32[8,256]{1,0:T(8,128)S(1)} %add.30), channel_id=1, source_target_pairs={{0,4},{1,5},{2,6},{3,7},{4,0},{5,1},{6,2},{7,3},{8,12},{9,13},{10,... | collective-permute-start | bytes 24584 | tf_op jit(solution)/shard_map/ppermute | solution.py:307
  69.1 4.4 %collective-permute-start.12 = (f32[8,256]{1,0:T(8,128)S(1)}, f32[8,256]{1,0:T(8,128)S(1)}, u32[]{:S(2)}, u32[]{:S(2)}) collective-permute-start(f32[8,256]{1,0:T(8,128)S(1)} %add.30), channel_id=1, source_target_pairs={{0,2},{1,3},{2,0},{3,1},{4,6},{5,7},{6,4},{7,5},{8,10},{9,11},{10,... | collective-permute-start | bytes 24584 | tf_op jit(solution)/shard_map/ppermute | solution.py:307
  73.5 5.7 %collective-permute-start.17 = (f32[8,256]{1,0:T(8,128)S(1)}, f32[8,256]{1,0:T(8,128)S(1)}, u32[]{:S(2)}, u32[]{:S(2)}) collective-permute-start(f32[8,256]{1,0:T(8,128)S(1)} %add_add_fusion.1), channel_id=1, source_target_pairs={{0,24},{8,16},{16,8},{24,0},{32,56},{40,48},{48,40},{56,32},{64,88... | collective-permute-start | bytes 24584 | tf_op jit(solution)/shard_map/ppermute | solution.py:307
  74.9 5.2 %collective-permute-start.16 = (f32[8,256]{1,0:T(8,128)S(1)}, f32[8,256]{1,0:T(8,128)S(1)}, u32[]{:S(2)}, u32[]{:S(2)}) collective-permute-start(f32[8,256]{1,0:T(8,128)S(1)} %add_add_fusion.1), channel_id=1, source_target_pairs={{0,16},{8,24},{16,0},{24,8},{32,48},{40,56},{48,32},{56,40},{64,80... | collective-permute-start | bytes 24584 | tf_op jit(solution)/shard_map/ppermute | solution.py:307
  75.7 4.3 %collective-permute-start.15 = (f32[8,256]{1,0:T(8,128)S(1)}, f32[8,256]{1,0:T(8,128)S(1)}, u32[]{:S(2)}, u32[]{:S(2)}) collective-permute-start(f32[8,256]{1,0:T(8,128)S(1)} %add_add_fusion.1), channel_id=1, source_target_pairs={{0,8},{8,0},{16,24},{24,16},{32,40},{40,32},{48,56},{56,48},{64,72... | collective-permute-start | bytes 24584 | tf_op jit(solution)/shard_map/ppermute | solution.py:307
  80.1 5.7 %collective-permute-start.20 = (f32[8,256]{1,0:T(8,128)S(1)}, f32[8,256]{1,0:T(8,128)S(1)}, u32[]{:S(2)}, u32[]{:S(2)}) collective-permute-start(f32[8,256]{1,0:T(8,128)S(1)} %add_add_fusion), channel_id=1, source_target_pairs={{0,96},{8,104},{16,112},{24,120},{32,64},{40,72},{48,80},{56,88},{... | collective-permute-start | bytes 24584 | tf_op jit(solution)/shard_map/ppermute | solution.py:307
  83.2 5.2 %collective-permute-start.19 = (f32[8,256]{1,0:T(8,128)S(1)}, f32[8,256]{1,0:T(8,128)S(1)}, u32[]{:S(2)}, u32[]{:S(2)}) collective-permute-start(f32[8,256]{1,0:T(8,128)S(1)} %add_add_fusion), channel_id=1, source_target_pairs={{0,64},{8,72},{16,80},{24,88},{32,96},{40,104},{48,112},{56,120},{... | collective-permute-start | bytes 24584 | tf_op jit(solution)/shard_map/ppermute | solution.py:307
  83.7 4.7 %collective-permute-start.18 = (f32[8,256]{1,0:T(8,128)S(1)}, f32[8,256]{1,0:T(8,128)S(1)}, u32[]{:S(2)}, u32[]{:S(2)}) collective-permute-start(f32[8,256]{1,0:T(8,128)S(1)} %add_add_fusion), channel_id=1, source_target_pairs={{0,32},{8,40},{16,48},{24,56},{32,0},{40,8},{48,16},{56,24},{64,96... | collective-permute-start | bytes 24584 | tf_op jit(solution)/shard_map/ppermute | solution.py:307

commit v7 on v6

--- a/solution.py
+++ b/solution.py
@@ -24,11 +24,13 @@
     return bits, jnp.bitwise_and(group, 3)
 
 
-def thirds(x):
-    one = x.astype(bf16)
-    rest = x - one.astype(f32)
-    two = rest.astype(bf16)
-    return one, two, (rest - two.astype(f32)).astype(bf16)
+def exact_dot(x, y, cx, cy):
+    one = x.astype(bf16).astype(f32)
+    rest = x - one
+    two = rest.astype(bf16).astype(f32)
+    stacked = jnp.concatenate([one, two, rest - two, jnp.zeros_like(x)], 0).astype(bf16)
+    out = mm(stacked, y, cx, cy)
+    return out[0:8] + out[8:16] + out[16:24]
 
 
 def one_hot(index_row, size):
@@ -58,8 +60,7 @@
     table[0 : table_ref.shape[0], :] = table_ref[...]
     level = lax.broadcasted_iota(jnp.int32, table.shape, 0)
     picked = one_hot(index_ref[...], table.shape[1])
-    pieces = thirds(jnp.where(level <= reach[0], table[...], 0.0))
-    w = mm(pieces[0], picked, 1, 0) + mm(pieces[1], picked, 1, 0) + mm(pieces[2], picked, 1, 0)
+    w = exact_dot(jnp.where(level <= reach[0], table[...], 0.0), picked, 1, 0)
     w_ref[...] = w
     for j in range(4):
         for a in range(4):
@@ -226,21 +227,21 @@
 
 
 def first_reads_kernel(reach, q_ref, g_ref, w_ref, qn_ref, lam_ref, *rest):
-    y34_refs, (out_hbm, lam_out, st, out_buf, sem) = rest[:3], rest[3:]
+    y34_refs, index_ref, (out_hbm, lam_out, picked_out, st, out_buf, sem) = rest[:3], rest[3], rest[4:]
 
     def finish(at, lam):
         lam_out[at, :] = lam
+        picked_out[at, :] = one_hot(index_ref[:, at], picked_out.shape[1]).T
 
     far_reads(FIRST_SPOTS, reach, q_ref, g_ref, w_ref, qn_ref, lam_ref, y34_refs, out_hbm, st, out_buf, sem, finish)
 
 
-def last_reads_kernel(reach, q_ref, g_ref, w_ref, qn_ref, lam_ref, y34_ref, index_ref, held, out_hbm, table_ref, st, out_buf, sem):
+def last_reads_kernel(reach, q_ref, g_ref, w_ref, qn_ref, lam_ref, y34_ref, picked_ref, held, out_hbm, table_ref, st, out_buf, sem):
     table_ref[...] = jnp.zeros_like(table_ref)
 
     def finish(at, lam):
         lam = (SCALE * lam).T[:8]
-        picked = one_hot(index_ref[:, at], table_ref.shape[1])
-        table_ref[...] += sum(mm(piece, picked, 1, 1) for piece in thirds(lam))
+        table_ref[...] += exact_dot(lam, picked_ref[at, :], 1, 0)
 
     far_reads((2,), reach, q_ref, g_ref, w_ref, qn_ref, lam_ref, (y34_ref,), out_hbm, st, out_buf, sem, finish)
 
@@ -425,8 +426,8 @@
         return pl.pallas_call(
             kernel,
             in_specs=[scalar] + [whole] * (5 + len(ins)) + [anywhere] * len(afters),
-            out_specs=[anywhere, whole],
-            out_shape=[sds((length, heads * DH), bf16), more_out],
+            out_specs=[anywhere] + [whole] * len(more_out),
+            out_shape=[sds((length, heads * DH), bf16)] + more_out,
             input_output_aliases=aliases,
             scratch_shapes=[
                 pltpu.VMEM((count * each, DH, 2 * DH), bf16),
@@ -438,17 +439,17 @@
             name=name,
         )(reach, queries, out_grad, w_cols, qn, lam, *ins, *afters)
 
-    query_grad, lam = far_part(
+    query_grad, lam, picked = far_part(
         first_reads_kernel,
         len(FIRST_SPOTS),
-        [y34s[j] for j in FIRST_SPOTS],
+        [y34s[j] for j in FIRST_SPOTS] + [index_row],
         [],
-        sds((length, DH), f32),
+        [sds((length, DH), f32), sds((length, names), bf16)],
         {},
         "first_reads",
     )
     query_grad, total = far_part(
-        last_reads_kernel, 1, [y34_two, index_row], [query_grad], sds((8, names), f32), {8: 0}, "last_reads"
+        last_reads_kernel, 1, [y34_two, picked], [query_grad], [sds((8, names), f32)], {8: 0}, "last_reads"
     )
     arrived = (y1, y2, *y34s)
 

time: 89.2 us -> 89 us (level)
  transfers between devices with their start and end apart: 21 -> 21, of which waited for: 10 -> 10; matrix products, arithmetic and copies ran while one was open for 0% -> 0% of each run, Pallas kernels for 35% -> 36%
where the time goes in v7:
time: 89 us; the launch traced here: 88.7 us
  Pallas kernels  40.2 us (45%)
  starting transfers between devices  30.8 us (35%)
  waiting for transfers between devices  14 us (16%)
  local copies, waits for them, and re-layouts  1.59 us (2%)
  between operations  1.53 us (2%)
    ppermute x21, starting transfers between devices, flip(): lax.ppermute(x, axis, [(i, i ^ mask) for i in range(lax.axis_size(axis))])  30.8 us
    pallas_call x5, Pallas kernels, near_part(): pl.pallas_call(group_kernel, grid=(count,), in_specs=[anywhere] + [token_...  20.4 us
    ppermute x21, waiting for transfers between devices, flip(): lax.ppermute(x, axis, [(i, i ^ mask) for i in range(lax.axis_size(axis))])  14 us
    pallas_call x4, Pallas kernels, returns(): pl.pallas_call(kernel, in_specs=[scalar] + [whole] * len(ins) + [anywhere...  6.32 us
    pallas_call x1, Pallas kernels, local(): pl.pallas_call(states_kernel, in_specs=[scalar, whole, whole] + [anywhere...  6.1 us
    pallas_call x2, Pallas kernels, far_part(): pl.pallas_call(kernel, in_specs=[scalar] + [whole] * (5 + len(ins)) + [an...  5.16 us
    pallas_call x1, Pallas kernels, local(): pl.pallas_call(near_reads_kernel, in_specs=[scalar] + [whole] * (6 + 2 *...  2.02 us
  transfers between devices with their start and end apart: 21, of which 10 were waited for; matrix products, arithmetic and copies ran while one was open for 0% of the time, Pallas kernels for 36%

profile of v7, /device:TPU:0, one launch (start us, length us, event | category | flops | bytes accessed | tf_op | source)
XLA Modules:
  0.0 88.7 jit_solution(16105256560800784372)
XLA Ops:
  1.3 0.0 copy-start.4
  1.3 0.7 copy-done.4
  2.0 0.7 copy-done.6
  2.7 6.1 %states.1 = (f32[8,1024]{1,0:T(8,128)S(1)}, f32[8,128,128]{2,1,0:T(8,128)S(1)}, f32[8,128,128]{2,1,0:T(8,128)S(1)}, f32[2,2,2,128,128]{4,3,2,1,0:T(8,128)S(1)}, f32[2,2,2,128,128]{4,3,2,1,0:T(8,128)}) custom-call(s32[1]{0:T(128)S(6)} %copy.28.reach.refs_0_, s32[1,1024]{1,0:T(1,128)S(1)} %bitcast.10, f32[5,256]{1,0:T(8,128)S(1)} %copy-done.6, ...), custom_call_target="tpu_custom_call" | custom-call | tf_op jit(solution)/shard_map/states/pallas_call | solution.py:333
  8.8 4.3 %collective-permute-start = (f32[2,2,2,128,128]{4,3,2,1,0:T(8,128)}, f32[2,2,2,128,128]{4,3,2,1,0:T(8,128)S(1)}, u32[]{:S(2)}, u32[]{:S(2)}) collective-permute-start(f32[2,2,2,128,128]{4,3,2,1,0:T(8,128)} %get-tuple-element.66), channel_id=1, source_target_pairs={{0,24},{8,16},{16,8},{24,0},{32,56},{40,48},{48,40},{56,32},{64,88... | collective-permute-start | bytes 1572872 | tf_op jit(solution)/shard_map/ppermute | solution.py:308
  13.1 0.0 collective-permute-start.1
  13.1 0.2 copy.19
  13.3 4.8 %group.5 = (f32[1024,256]{1,0:T(8,128)S(1)}, f32[1024,256]{1,0:T(8,128)S(1)}, f32[1024,256]{1,0:T(8,128)S(1)}, f32[1024,128]{1,0:T(8,128)S(1)}) custom-call(f32[2,2,2,128,128]{4,3,2,1,0:T(8,128)S(1)} %get-tuple-element.65.after.keep_ref, bf16[1024,1024]{1,0:T(8,128)(2,1)} %q_ref.15, bf16[1024,1024]{1,0:T(8,128)(2,1)} %refs_1_.7, bf16[1024,1024]{1,0:T(8,128)(2,1)} %refs_2_.7, ...), custom_call_target="tpu_custom_call" | custom-call | flops 100000000 | bytes 1048576 | tf_op jit(solution)/shard_map/group/pallas_call | solution.py:359
  18.1 4.9 %group.6 = (f32[1024,256]{1,0:T(8,128)S(1)}, f32[1024,256]{1,0:T(8,128)S(1)}, f32[1024,256]{1,0:T(8,128)S(1)}, f32[1024,128]{1,0:T(8,128)S(1)}) custom-call(f32[1024,256]{1,0:T(8,128)S(1)} %get-tuple-element.68.after.rest_0_, bf16[1024,1024]{1,0:T(8,128)(2,1)} %q_ref.15, bf16[1024,1024]{1,0:T(8,128)(2,1)} %refs_1_.7, bf16[1024,1024]{1,0:T(8,128)(2,1)} %refs_2_.7, ...), custom_call_target="tpu_custom_call" | custom-call | flops 100000000 | bytes 1048576 | tf_op jit(solution)/shard_map/group/pallas_call | solution.py:359
  23.0 2.2 %collective-permute-done.got_ref = f32[2,2,2,128,128]{4,3,2,1,0:T(8,128)S(1)} collective-permute-done((f32[2,2,2,128,128]{4,3,2,1,0:T(8,128)}, f32[2,2,2,128,128]{4,3,2,1,0:T(8,128)S(1)}, u32[]{:S(2)}, u32[]{:S(2)}) %collective-permute-start) | collective-permute-done | bytes 524320 | tf_op jit(solution)/shard_map/ppermute | solution.py:308
  25.2 1.2 %collective-permute-done.1.near_got_ref = f32[8,128,128]{2,1,0:T(8,128)S(1)} collective-permute-done((f32[8,128,128]{2,1,0:T(8,128)S(1)}, f32[8,128,128]{2,1,0:T(8,128)S(1)}, u32[]{:S(2)}, u32[]{:S(2)}) %collective-permute-start.1) | collective-permute-done | bytes 524320 | tf_op jit(solution)/shard_map/ppermute | solution.py:308
  26.4 0.1 pair.1
  26.6 1.8 %collective-permute-start.5 = (f32[8,128,128]{2,1,0:T(8,128)S(1)}, f32[8,128,128]{2,1,0:T(8,128)S(1)}, u32[]{:S(2)}, u32[]{:S(2)}) collective-permute-start(f32[8,128,128]{2,1,0:T(8,128)S(1)} %get-tuple-element.75), channel_id=1, source_target_pairs={{0,24},{8,16},{16,8},{24,0},{32,56},{40,48},{48,40},{56,32},{64,88... | collective-permute-start | bytes 1572872 | tf_op jit(solution)/shard_map/ppermute | solution.py:308
  28.3 0.0 collective-permute-start.2
  28.3 4.8 %group.7 = (f32[1024,256]{1,0:T(8,128)S(1)}, f32[1024,256]{1,0:T(8,128)S(1)}, f32[1024,256]{1,0:T(8,128)S(1)}, f32[1024,128]{1,0:T(8,128)S(1)}) custom-call(f32[2,2,128,128]{3,2,1,0:T(8,128)S(1)} %get-tuple-element.70.after.own_ref, bf16[1024,1024]{1,0:T(8,128)(2,1)} %q_ref.15, bf16[1024,1024]{1,0:T(8,128)(2,1)} %refs_1_.7, bf16[1024,1024]{1,0:T(8,128)(2,1)} %refs_2_.7, ...), custom_call_target="tpu_custom_call" | custom-call | flops 100000000 | bytes 1048576 | tf_op jit(solution)/shard_map/group/pallas_call | solution.py:359
  33.2 2.1 %collective-permute-start.7 = (f32[8,128,128]{2,1,0:T(8,128)S(1)}, f32[8,128,128]{2,1,0:T(8,128)S(1)}, u32[]{:S(2)}, u32[]{:S(2)}) collective-permute-start(f32[8,128,128]{2,1,0:T(8,128)S(1)} %gate.1), channel_id=1, source_target_pairs={{0,8},{8,0},{16,24},{24,16},{32,40},{40,32},{48,56},{56,48},{64,72... | collective-permute-start | bytes 1572872 | tf_op jit(solution)/shard_map/ppermute | solution.py:308
  35.3 0.5 collective-permute-done.2.got_ref
  35.9 1.7 %collective-permute-start.4 = (f32[2,128,128]{2,1,0:T(8,128)S(1)}, f32[2,128,128]{2,1,0:T(8,128)S(1)}, u32[]{:S(2)}, u32[]{:S(2)}) collective-permute-start(f32[2,128,128]{2,1,0:T(8,128)S(1)} %get-tuple-element.74.after.rows_ref), channel_id=1, source_target_pairs={{0,32},{8,40},{16,48},{24,56},{32,0},{40,8},{48,16},{56,24},{64,96... | collective-permute-start | bytes 393224 | tf_op jit(solution)/shard_map/ppermute | solution.py:308
  37.5 0.5 collective-permute-start.3
  38.0 2.8 %group.8 = (f32[1024,128]{1,0:T(8,128)S(1)}, f32[1024,128]{1,0:T(8,128)S(1)}, f32[1024,128]{1,0:T(8,128)S(1)}, f32[1024,128]{1,0:T(8,128)S(1)}) custom-call(f32[2,128,128]{2,1,0:T(8,128)S(1)} %get-tuple-element.74.after.rows_ref, bf16[1024,1024]{1,0:T(8,128)(2,1)} %q_ref.15, bf16[1024,1024]{1,0:T(8,128)(2,1)} %refs_1_.7, bf16[1024,1024]{1,0:T(8,128)(2,1)} %refs_2_.7, ...), custom_call_target="tpu_custom_call" | custom-call | flops 100000000 | bytes 1048576 | tf_op jit(solution)/shard_map/group/pallas_call | solution.py:359
  40.8 0.1 collective-permute-done.4.other_ref
  40.9 0.0 collective-permute-done.5.after.y2_ref.refs_6_.refs_8_
  40.9 3.1 %collective-permute-start.6 = (f32[2,128,128]{2,1,0:T(8,128)S(1)}, f32[2,128,128]{2,1,0:T(8,128)S(1)}, u32[]{:S(2)}, u32[]{:S(2)}) collective-permute-start(f32[2,128,128]{2,1,0:T(8,128)S(1)} %cross.1.after), channel_id=1, source_target_pairs={{0,96},{8,104},{16,112},{24,120},{32,64},{40,72},{48,80},{56,88},{... | collective-permute-start | bytes 393224 | tf_op jit(solution)/shard_map/ppermute | solution.py:308
  44.0 3.0 %group.9 = (f32[1024,128]{1,0:T(8,128)S(1)}, f32[1024,128]{1,0:T(8,128)S(1)}, f32[1024,128]{1,0:T(8,128)S(1)}, f32[1024,128]{1,0:T(8,128)S(1)}) custom-call(f32[2,128,128]{2,1,0:T(8,128)S(1)} %cross.1.after, bf16[1024,1024]{1,0:T(8,128)(2,1)} %q_ref.15, bf16[1024,1024]{1,0:T(8,128)(2,1)} %refs_1_.7, bf16[1024,1024]{1,0:T(8,128)(2,1)} %refs_2_.7, ...), custom_call_target="tpu_custom_call" | custom-call | flops 100000000 | bytes 1048576 | tf_op jit(solution)/shard_map/group/pallas_call | solution.py:359
  47.0 0.0 collective-permute-done.3.y3_ref
  47.1 0.0 collective-permute-done.7.rest_0_.y1_ref.refs_5_.refs_7_
  47.1 0.1 collective-permute-done.6.y4_ref
  47.2 1.5 %collective-permute-start.9 = (f32[2,2,128,128]{3,2,1,0:T(8,128)S(1)}, f32[2,2,128,128]{3,2,1,0:T(8,128)S(1)}, u32[]{:S(2)}, u32[]{:S(2)}) collective-permute-start(f32[2,2,128,128]{3,2,1,0:T(8,128)S(1)} %pack.1.y34_ref.rest_0_.refs_7_.refs_9_), channel_id=1, source_target_pairs={{0,24},{8,16},{16,8},{24,0},{32,56},{40,48},{48,40},{56,32},{64,88... | collective-permute-start | bytes 786440 | tf_op jit(solution)/shard_map/ppermute | solution.py:308
  48.7 0.0 collective-permute-start.8
  48.7 0.0 copy-start.5
  48.7 2.0 %near_reads.1 = (f32[1024,1024]{1,0:T(8,128)S(1)}, f32[1024,128]{1,0:T(8,128)S(1)}, f32[2,2,128,128]{3,2,1,0:T(8,128)S(1)}) custom-call(s32[1]{0:T(128)S(6)} %copy.28.reach.refs_0_, f32[2,2,128,128]{3,2,1,0:T(8,128)S(1)} %pack.1.y34_ref.rest_0_.refs_7_.refs_9_, bf16[1024,1024]{1,0:T(8,128)(2,1)S(1)} %copy-done.2, bf16[1024,1024]{1,0:T(8,128)(2,1)S(1)} %copy-done.3, ...), custom_call_target="tpu_custom_call" | custom-call | flops 100000000 | bytes 1048576 | tf_op jit(solution)/shard_map/near_reads/pallas_call | solution.py:409
  50.8 3.3 %collective-permute-start.10 = (f32[2,2,128,128]{3,2,1,0:T(8,128)S(1)}, f32[2,2,128,128]{3,2,1,0:T(8,128)S(1)}, u32[]{:S(2)}, u32[]{:S(2)}) collective-permute-start(f32[2,2,128,128]{3,2,1,0:T(8,128)S(1)} %get-tuple-element.87), channel_id=1, source_target_pairs={{0,16},{8,24},{16,0},{24,8},{32,48},{40,56},{48,32},{56,40},{64,80... | collective-permute-start | bytes 786440 | tf_op jit(solution)/shard_map/ppermute | solution.py:308
  54.1 3.6 %collective-permute-done.9.rest_2_.refs_10_.refs_12_ = f32[2,2,128,128]{3,2,1,0:T(8,128)S(1)} collective-permute-done((f32[2,2,128,128]{3,2,1,0:T(8,128)S(1)}, f32[2,2,128,128]{3,2,1,0:T(8,128)S(1)}, u32[]{:S(2)}, u32[]{:S(2)}) %collective-permute-start.9) | collective-permute-done | bytes 262176 | tf_op jit(solution)/shard_map/ppermute | solution.py:308
  57.7 0.0 collective-permute-done.8.rest_1_.refs_8_.refs_10_
  57.7 0.0 copy-done.5
  57.7 2.9 %first_reads.1 = (bf16[1024,1024]{1,0:T(8,128)(2,1)}, f32[1024,128]{1,0:T(8,128)S(1)}, bf16[1024,256]{1,0:T(8,128)(2,1)S(1)}) custom-call(s32[1]{0:T(128)S(6)} %copy.28.reach.refs_0_, bf16[1024,1024]{1,0:T(8,128)(2,1)S(1)} %copy-done.2, bf16[1024,1024]{1,0:T(8,128)(2,1)S(1)} %copy-done.3, f32[1024,8]{1,0:T(8,128)S(1)} %bitcast.8, ...), custom_call_target="tpu_custom_call" | custom-call | flops 100000000 | bytes 1048576 | tf_op jit(solution)/shard_map/first_reads/pallas_call | solution.py:426
  60.6 0.6 collective-permute-done.10.y34_ref.refs_9_.refs_11_
  61.2 2.3 %last_reads.1 = (bf16[1024,1024]{1,0:T(8,128)(2,1)}, f32[8,256]{1,0:T(8,128)S(1)}) custom-call(s32[1]{0:T(128)S(6)} %copy.28.reach.refs_0_, bf16[1024,1024]{1,0:T(8,128)(2,1)S(1)} %copy-done.2, bf16[1024,1024]{1,0:T(8,128)(2,1)S(1)} %copy-done.3, f32[1024,8]{1,0:T(8,128)S(1)} %bitcast.9, ...), custom_call_target="tpu_custom_call", output_to_operand_aliasing={{0}: (8, {})} | custom-call | flops 100000000 | bytes 1048576 | tf_op jit(solution)/shard_map/last_reads/pallas_call | solution.py:426
  63.5 0.1 collective-permute-start.11
  63.6 0.0 copy-done
  63.6 1.6 %returns.4 = (bf16[1024,1024]{1,0:T(8,128)(2,1)}, bf16[1024,1024]{1,0:T(8,128)(2,1)}) custom-call(s32[1]{0:T(128)S(6)} %copy.28.reach.refs_0_, bf16[1024,1024]{1,0:T(8,128)(2,1)S(1)} %copy-done, bf16[1024,1024]{1,0:T(8,128)(2,1)S(1)} %copy-done.1, f32[1024,256]{1,0:T(8,128)S(1)} %get-tuple-element.93.refs_3_, f32[1024,256]{1,0:T(8,128)S(1)} %get-tuple-element.94.refs_4_, ...), custom_call_target="tpu_custom_call" | custom-call | flops 100000000 | bytes 1048576 | tf_op jit(solution)/shard_map/returns/pallas_call | solution.py:464
  65.2 0.0 collective-permute-done.11
  65.2 2.8 %collective-permute-start.14 = (f32[8,256]{1,0:T(8,128)S(1)}, f32[8,256]{1,0:T(8,128)S(1)}, u32[]{:S(2)}, u32[]{:S(2)}) collective-permute-start(f32[8,256]{1,0:T(8,128)S(1)} %add.30), channel_id=1, source_target_pairs={{0,6},{1,7},{2,4},{3,5},{4,2},{5,3},{6,0},{7,1},{8,14},{9,15},{10,... | collective-permute-start | bytes 24584 | tf_op jit(solution)/shard_map/ppermute | solution.py:308
  68.0 0.8 collective-permute-start.13
  68.9 0.5 collective-permute-start.12
  69.4 1.7 %returns.5 = (bf16[1024,1024]{1,0:T(8,128)(2,1)}, bf16[1024,1024]{1,0:T(8,128)(2,1)}) custom-call(s32[1]{0:T(128)S(6)} %copy.28.reach.refs_0_, bf16[1024,1024]{1,0:T(8,128)(2,1)S(1)} %copy-done, bf16[1024,1024]{1,0:T(8,128)(2,1)S(1)} %copy-done.1, f32[1024,256]{1,0:T(8,128)S(1)} %get-tuple-element.99.refs_3_, ...), custom_call_target="tpu_custom_call", output_to_operand_aliasing={{0}: (11, {}), {1}: (12, {})} | custom-call | flops 100000000 | bytes 1048576 | tf_op jit(solution)/shard_map/returns/pallas_call | solution.py:464
  71.1 0.0 collective-permute-done.14
  71.1 2.1 %collective-permute-done.13 = f32[8,256]{1,0:T(8,128)S(1)} collective-permute-done((f32[8,256]{1,0:T(8,128)S(1)}, f32[8,256]{1,0:T(8,128)S(1)}, u32[]{:S(2)}, u32[]{:S(2)}) %collective-permute-start.13) | collective-permute-done | bytes 8224 | tf_op jit(solution)/shard_map/ppermute | solution.py:308
  73.2 0.0 collective-permute-done.12
  73.2 1.5 %collective-permute-start.17 = (f32[8,256]{1,0:T(8,128)S(1)}, f32[8,256]{1,0:T(8,128)S(1)}, u32[]{:S(2)}, u32[]{:S(2)}) collective-permute-start(f32[8,256]{1,0:T(8,128)S(1)} %add_add_fusion.1), channel_id=1, source_target_pairs={{0,24},{8,16},{16,8},{24,0},{32,56},{40,48},{48,40},{56,32},{64,88... | collective-permute-start | bytes 24584 | tf_op jit(solution)/shard_map/ppermute | solution.py:308
  74.7 0.8 collective-permute-start.16
  75.5 1.9 %collective-permute-start.15 = (f32[8,256]{1,0:T(8,128)S(1)}, f32[8,256]{1,0:T(8,128)S(1)}, u32[]{:S(2)}, u32[]{:S(2)}) collective-permute-start(f32[8,256]{1,0:T(8,128)S(1)} %add_add_fusion.1), channel_id=1, source_target_pairs={{0,8},{8,0},{16,24},{24,16},{32,40},{40,32},{48,56},{56,48},{64,72... | collective-permute-start | bytes 24584 | tf_op jit(solution)/shard_map/ppermute | solution.py:308
  77.4 1.5 %returns.6 = (bf16[1024,1024]{1,0:T(8,128)(2,1)}, bf16[1024,1024]{1,0:T(8,128)(2,1)}) custom-call(s32[1]{0:T(128)S(6)} %copy.28.reach.refs_0_, bf16[1024,1024]{1,0:T(8,128)(2,1)S(1)} %copy-done, bf16[1024,1024]{1,0:T(8,128)(2,1)S(1)} %copy-done.1, f32[1024,256]{1,0:T(8,128)S(1)} %get-tuple-element.107.refs_3_, ...), custom_call_target="tpu_custom_call", output_to_operand_aliasing={{0}: (11, {}), {1}: (12, {})} | custom-call | flops 100000000 | bytes 1048576 | tf_op jit(solution)/shard_map/returns/pallas_call | solution.py:464
  78.9 0.0 collective-permute-done.17
  78.9 0.9 %collective-permute-done.16 = f32[8,256]{1,0:T(8,128)S(1)} collective-permute-done((f32[8,256]{1,0:T(8,128)S(1)}, f32[8,256]{1,0:T(8,128)S(1)}, u32[]{:S(2)}, u32[]{:S(2)}) %collective-permute-start.16) | collective-permute-done | bytes 8224 | tf_op jit(solution)/shard_map/ppermute | solution.py:308
  79.8 0.0 collective-permute-done.15
  79.9 3.1 %collective-permute-start.20 = (f32[8,256]{1,0:T(8,128)S(1)}, f32[8,256]{1,0:T(8,128)S(1)}, u32[]{:S(2)}, u32[]{:S(2)}) collective-permute-start(f32[8,256]{1,0:T(8,128)S(1)} %add_add_fusion), channel_id=1, source_target_pairs={{0,96},{8,104},{16,112},{24,120},{32,64},{40,72},{48,80},{56,88},{... | collective-permute-start | bytes 24584 | tf_op jit(solution)/shard_map/ppermute | solution.py:308
  83.0 0.5 collective-permute-start.19
  83.4 0.6 collective-permute-start.18
  84.0 1.5 %returns.7 = (bf16[1024,1024]{1,0:T(8,128)(2,1)}, bf16[1024,1024]{1,0:T(8,128)(2,1)}) custom-call(s32[1]{0:T(128)S(6)} %copy.28.reach.refs_0_, bf16[1024,1024]{1,0:T(8,128)(2,1)S(1)} %copy-done, bf16[1024,1024]{1,0:T(8,128)(2,1)S(1)} %copy-done.1, f32[1024,128]{1,0:T(8,128)S(1)} %get-tuple-element.115.refs_3_, ...), custom_call_target="tpu_custom_call", output_to_operand_aliasing={{0}: (13, {}), {1}: (14, {})} | custom-call | flops 100000000 | bytes 1048576 | tf_op jit(solution)/shard_map/returns/pallas_call | solution.py:464
  85.5 0.0 collective-permute-done.20
  85.5 2.6 %collective-permute-done.19 = f32[8,256]{1,0:T(8,128)S(1)} collective-permute-done((f32[8,256]{1,0:T(8,128)S(1)}, f32[8,256]{1,0:T(8,128)S(1)}, u32[]{:S(2)}, u32[]{:S(2)}) %collective-permute-start.19) | collective-permute-done | bytes 8224 | tf_op jit(solution)/shard_map/ppermute | solution.py:308
  88.1 0.0 collective-permute-done.18
  88.1 0.6 fusion.1
  (15 shorter events, 0.1 us)
Async XLA Ops:
  1.3 0.7 copy-start.4
  2.0 0.7 copy-start.6
  8.8 16.4 %collective-permute-start = (f32[2,2,2,128,128]{4,3,2,1,0:T(8,128)}, f32[2,2,2,128,128]{4,3,2,1,0:T(8,128)S(1)}, u32[]{:S(2)}, u32[]{:S(2)}) collective-permute-start(f32[2,2,2,128,128]{4,3,2,1,0:T(8,128)} %get-tuple-element.66), channel_id=1, source_target_pairs={{0,24},{8,16},{16,8},{24,0},{32,56},{40,48},{48,40},{56,32},{64,88... | collective-permute-start | bytes 1572872 | tf_op jit(solution)/shard_map/ppermute | solution.py:308
  13.1 13.4 %collective-permute-start.1 = (f32[8,128,128]{2,1,0:T(8,128)S(1)}, f32[8,128,128]{2,1,0:T(8,128)S(1)}, u32[]{:S(2)}, u32[]{:S(2)}) collective-permute-start(f32[8,128,128]{2,1,0:T(8,128)S(1)} %get-tuple-element.67.near_ref), channel_id=1, source_target_pairs={{0,8},{8,0},{16,24},{24,16},{32,40},{40,32},{48,56},{56,48},{64,72... | collective-permute-start | bytes 1572872 | tf_op jit(solution)/shard_map/ppermute | solution.py:308
  26.6 14.4 %collective-permute-start.5 = (f32[8,128,128]{2,1,0:T(8,128)S(1)}, f32[8,128,128]{2,1,0:T(8,128)S(1)}, u32[]{:S(2)}, u32[]{:S(2)}) collective-permute-start(f32[8,128,128]{2,1,0:T(8,128)S(1)} %get-tuple-element.75), channel_id=1, source_target_pairs={{0,24},{8,16},{16,8},{24,0},{32,56},{40,48},{48,40},{56,32},{64,88... | collective-permute-start | bytes 1572872 | tf_op jit(solution)/shard_map/ppermute | solution.py:308
  28.3 7.5 %collective-permute-start.2 = (f32[2,2,128,128]{3,2,1,0:T(8,128)S(1)}, f32[2,2,128,128]{3,2,1,0:T(8,128)S(1)}, u32[]{:S(2)}, u32[]{:S(2)}) collective-permute-start(f32[2,2,128,128]{3,2,1,0:T(8,128)S(1)} %get-tuple-element.71), channel_id=1, source_target_pairs={{0,8},{8,0},{16,24},{24,16},{32,40},{40,32},{48,56},{56,48},{64,72... | collective-permute-start | bytes 786440 | tf_op jit(solution)/shard_map/ppermute | solution.py:308
  33.2 13.9 %collective-permute-start.7 = (f32[8,128,128]{2,1,0:T(8,128)S(1)}, f32[8,128,128]{2,1,0:T(8,128)S(1)}, u32[]{:S(2)}, u32[]{:S(2)}) collective-permute-start(f32[8,128,128]{2,1,0:T(8,128)S(1)} %gate.1), channel_id=1, source_target_pairs={{0,8},{8,0},{16,24},{24,16},{32,40},{40,32},{48,56},{56,48},{64,72... | collective-permute-start | bytes 1572872 | tf_op jit(solution)/shard_map/ppermute | solution.py:308
  35.9 5.0 %collective-permute-start.4 = (f32[2,128,128]{2,1,0:T(8,128)S(1)}, f32[2,128,128]{2,1,0:T(8,128)S(1)}, u32[]{:S(2)}, u32[]{:S(2)}) collective-permute-start(f32[2,128,128]{2,1,0:T(8,128)S(1)} %get-tuple-element.74.after.rows_ref), channel_id=1, source_target_pairs={{0,32},{8,40},{16,48},{24,56},{32,0},{40,8},{48,16},{56,24},{64,96... | collective-permute-start | bytes 393224 | tf_op jit(solution)/shard_map/ppermute | solution.py:308
  37.5 9.5 %collective-permute-start.3 = (f32[2,128,128]{2,1,0:T(8,128)S(1)}, f32[2,128,128]{2,1,0:T(8,128)S(1)}, u32[]{:S(2)}, u32[]{:S(2)}) collective-permute-start(f32[2,128,128]{2,1,0:T(8,128)S(1)} %get-tuple-element.73), channel_id=1, source_target_pairs={{0,32},{8,40},{16,48},{24,56},{32,0},{40,8},{48,16},{56,24},{64,96... | collective-permute-start | bytes 393224 | tf_op jit(solution)/shard_map/ppermute | solution.py:308
  40.9 6.3 %collective-permute-start.6 = (f32[2,128,128]{2,1,0:T(8,128)S(1)}, f32[2,128,128]{2,1,0:T(8,128)S(1)}, u32[]{:S(2)}, u32[]{:S(2)}) collective-permute-start(f32[2,128,128]{2,1,0:T(8,128)S(1)} %cross.1.after), channel_id=1, source_target_pairs={{0,96},{8,104},{16,112},{24,120},{32,64},{40,72},{48,80},{56,88},{... | collective-permute-start | bytes 393224 | tf_op jit(solution)/shard_map/ppermute | solution.py:308
  44.0 4.7 %copy-start.2 = (bf16[1024,1024]{1,0:T(8,128)(2,1)S(1)}, bf16[1024,1024]{1,0:T(8,128)(2,1)}, u32[]{:S(2)}) copy-start(bf16[1024,1024]{1,0:T(8,128)(2,1)} %q_ref.15) | copy-start | bytes 6291460
  44.0 4.7 %copy-start.3 = (bf16[1024,1024]{1,0:T(8,128)(2,1)S(1)}, bf16[1024,1024]{1,0:T(8,128)(2,1)}, u32[]{:S(2)}) copy-start(bf16[1024,1024]{1,0:T(8,128)(2,1)} %g_ref.15) | copy-start | bytes 6291460
  47.2 10.5 %collective-permute-start.9 = (f32[2,2,128,128]{3,2,1,0:T(8,128)S(1)}, f32[2,2,128,128]{3,2,1,0:T(8,128)S(1)}, u32[]{:S(2)}, u32[]{:S(2)}) collective-permute-start(f32[2,2,128,128]{3,2,1,0:T(8,128)S(1)} %pack.1.y34_ref.rest_0_.refs_7_.refs_9_), channel_id=1, source_target_pairs={{0,24},{8,16},{16,8},{24,0},{32,56},{40,48},{48,40},{56,32},{64,88... | collective-permute-start | bytes 786440 | tf_op jit(solution)/shard_map/ppermute | solution.py:308
  48.7 9.0 %collective-permute-start.8 = (f32[2,2,128,128]{3,2,1,0:T(8,128)S(1)}, f32[2,2,128,128]{3,2,1,0:T(8,128)S(1)}, u32[]{:S(2)}, u32[]{:S(2)}) collective-permute-start(f32[2,2,128,128]{3,2,1,0:T(8,128)S(1)} %pack.1.y34_ref.rest_0_.refs_7_.refs_9_), channel_id=1, source_target_pairs={{0,8},{8,0},{16,24},{24,16},{32,40},{40,32},{48,56},{56,48},{64,72... | collective-permute-start | bytes 786440 | tf_op jit(solution)/shard_map/ppermute | solution.py:308
  48.7 9.0 %copy-start.5 = (s32[1024]{0:T(1024)S(1)}, s32[1024]{0:T(1024)}, u32[]{:S(2)}) copy-start(s32[1024]{0:T(1024)} %param.12) | copy-start | bytes 12292
  50.8 10.5 %collective-permute-start.10 = (f32[2,2,128,128]{3,2,1,0:T(8,128)S(1)}, f32[2,2,128,128]{3,2,1,0:T(8,128)S(1)}, u32[]{:S(2)}, u32[]{:S(2)}) collective-permute-start(f32[2,2,128,128]{3,2,1,0:T(8,128)S(1)} %get-tuple-element.87), channel_id=1, source_target_pairs={{0,16},{8,24},{16,0},{24,8},{32,48},{40,56},{48,32},{56,40},{64,80... | collective-permute-start | bytes 786440 | tf_op jit(solution)/shard_map/ppermute | solution.py:308
  61.2 2.4 %copy-start = (bf16[1024,1024]{1,0:T(8,128)(2,1)S(1)}, bf16[1024,1024]{1,0:T(8,128)(2,1)}, u32[]{:S(2)}) copy-start(bf16[1024,1024]{1,0:T(8,128)(2,1)} %refs_1_.7) | copy-start | bytes 6291460
  61.2 2.4 %copy-start.1 = (bf16[1024,1024]{1,0:T(8,128)(2,1)S(1)}, bf16[1024,1024]{1,0:T(8,128)(2,1)}, u32[]{:S(2)}) copy-start(bf16[1024,1024]{1,0:T(8,128)(2,1)} %refs_2_.7) | copy-start | bytes 6291460
  63.5 1.7 %collective-permute-start.11 = (f32[8,256]{1,0:T(8,128)S(1)}, f32[8,256]{1,0:T(8,128)S(1)}, u32[]{:S(2)}, u32[]{:S(2)}) collective-permute-start(f32[8,256]{1,0:T(8,128)S(1)} %get-tuple-element.91), channel_id=1, source_target_pairs={{0,1},{1,0},{2,3},{3,2},{4,5},{5,4},{6,7},{7,6},{8,9},{9,8},{10,11... | collective-permute-start | bytes 24584 | tf_op jit(solution)/shard_map/ppermute | solution.py:308
  65.2 5.9 %collective-permute-start.14 = (f32[8,256]{1,0:T(8,128)S(1)}, f32[8,256]{1,0:T(8,128)S(1)}, u32[]{:S(2)}, u32[]{:S(2)}) collective-permute-start(f32[8,256]{1,0:T(8,128)S(1)} %add.30), channel_id=1, source_target_pairs={{0,6},{1,7},{2,4},{3,5},{4,2},{5,3},{6,0},{7,1},{8,14},{9,15},{10,... | collective-permute-start | bytes 24584 | tf_op jit(solution)/shard_map/ppermute | solution.py:308
  68.0 5.2 %collective-permute-start.13 = (f32[8,256]{1,0:T(8,128)S(1)}, f32[8,256]{1,0:T(8,128)S(1)}, u32[]{:S(2)}, u32[]{:S(2)}) collective-permute-start(f32[8,256]{1,0:T(8,128)S(1)} %add.30), channel_id=1, source_target_pairs={{0,4},{1,5},{2,6},{3,7},{4,0},{5,1},{6,2},{7,3},{8,12},{9,13},{10,... | collective-permute-start | bytes 24584 | tf_op jit(solution)/shard_map/ppermute | solution.py:308
  68.9 4.3 %collective-permute-start.12 = (f32[8,256]{1,0:T(8,128)S(1)}, f32[8,256]{1,0:T(8,128)S(1)}, u32[]{:S(2)}, u32[]{:S(2)}) collective-permute-start(f32[8,256]{1,0:T(8,128)S(1)} %add.30), channel_id=1, source_target_pairs={{0,2},{1,3},{2,0},{3,1},{4,6},{5,7},{6,4},{7,5},{8,10},{9,11},{10,... | collective-permute-start | bytes 24584 | tf_op jit(solution)/shard_map/ppermute | solution.py:308
  73.2 5.7 %collective-permute-start.17 = (f32[8,256]{1,0:T(8,128)S(1)}, f32[8,256]{1,0:T(8,128)S(1)}, u32[]{:S(2)}, u32[]{:S(2)}) collective-permute-start(f32[8,256]{1,0:T(8,128)S(1)} %add_add_fusion.1), channel_id=1, source_target_pairs={{0,24},{8,16},{16,8},{24,0},{32,56},{40,48},{48,40},{56,32},{64,88... | collective-permute-start | bytes 24584 | tf_op jit(solution)/shard_map/ppermute | solution.py:308
  74.7 5.2 %collective-permute-start.16 = (f32[8,256]{1,0:T(8,128)S(1)}, f32[8,256]{1,0:T(8,128)S(1)}, u32[]{:S(2)}, u32[]{:S(2)}) collective-permute-start(f32[8,256]{1,0:T(8,128)S(1)} %add_add_fusion.1), channel_id=1, source_target_pairs={{0,16},{8,24},{16,0},{24,8},{32,48},{40,56},{48,32},{56,40},{64,80... | collective-permute-start | bytes 24584 | tf_op jit(solution)/shard_map/ppermute | solution.py:308
  75.5 4.3 %collective-permute-start.15 = (f32[8,256]{1,0:T(8,128)S(1)}, f32[8,256]{1,0:T(8,128)S(1)}, u32[]{:S(2)}, u32[]{:S(2)}) collective-permute-start(f32[8,256]{1,0:T(8,128)S(1)} %add_add_fusion.1), channel_id=1, source_target_pairs={{0,8},{8,0},{16,24},{24,16},{32,40},{40,32},{48,56},{56,48},{64,72... | collective-permute-start | bytes 24584 | tf_op jit(solution)/shard_map/ppermute | solution.py:308
  79.9 5.7 %collective-permute-start.20 = (f32[8,256]{1,0:T(8,128)S(1)}, f32[8,256]{1,0:T(8,128)S(1)}, u32[]{:S(2)}, u32[]{:S(2)}) collective-permute-start(f32[8,256]{1,0:T(8,128)S(1)} %add_add_fusion), channel_id=1, source_target_pairs={{0,96},{8,104},{16,112},{24,120},{32,64},{40,72},{48,80},{56,88},{... | collective-permute-start | bytes 24584 | tf_op jit(solution)/shard_map/ppermute | solution.py:308
  83.0 5.2 %collective-permute-start.19 = (f32[8,256]{1,0:T(8,128)S(1)}, f32[8,256]{1,0:T(8,128)S(1)}, u32[]{:S(2)}, u32[]{:S(2)}) collective-permute-start(f32[8,256]{1,0:T(8,128)S(1)} %add_add_fusion), channel_id=1, source_target_pairs={{0,64},{8,72},{16,80},{24,88},{32,96},{40,104},{48,112},{56,120},{... | collective-permute-start | bytes 24584 | tf_op jit(solution)/shard_map/ppermute | solution.py:308
  83.4 4.7 %collective-permute-start.18 = (f32[8,256]{1,0:T(8,128)S(1)}, f32[8,256]{1,0:T(8,128)S(1)}, u32[]{:S(2)}, u32[]{:S(2)}) collective-permute-start(f32[8,256]{1,0:T(8,128)S(1)} %add_add_fusion), channel_id=1, source_target_pairs={{0,32},{8,40},{16,48},{24,56},{32,0},{40,8},{48,16},{56,24},{64,96... | collective-permute-start | bytes 24584 | tf_op jit(solution)/shard_map/ppermute | solution.py:308
